TPU v7x, 512 devices: a whole 4x8x8 slice. The times are simulated.
512 devices in a mesh: grp: 8 (over z_hi, core), shard: 64 (over z_lo, y, x).
Axes of the slice: x: 4, y: 8, z: 8 (z_hi: 4, z_lo: 2; z = z_hi * 2 + z_lo), core: 2. Of those that a mesh axis runs over, the one named last changes fastest.
Arguments:
- gradients: float32 [8, 1024, 512], P('grp', 'shard'), may hold values from -6 to 6
- weight: float32 [1024, 512], P('shard'), may hold values from -0.1875 to 0.1875
- moment: float32 [1024, 512], P('shard'), may hold values from -4 to 4
- second: float32 [1024, 512], P('shard'), may hold values from 0.01 to 0.5
- left_gram: float32 [1024, 1024], P('shard'), may hold values from -3 to 60, as said below
- left_basis: float32 [1024, 1024], P('shard'), may hold values from -0.1 to 1.1, as said below
- right_gram: float32 [512, 512], P('shard'), may hold values from -3 to 60, as said below
- right_basis: float32 [512, 512], P('shard'), may hold values from -0.1 to 1.1, as said below
Outputs:
- weight_new: float32 [1024, 512], P('shard')
- moment_new: float32 [1024, 512], P('shard')
- second_new: float32 [1024, 512], P('shard')
- left_new: float32 [1024, 1024], P('shard')
- left_basis_new: float32 [1024, 1024], P('shard')
- right_new: float32 [512, 512], P('shard')
- right_basis_new: float32 [512, 512], P('shard')
Inputs may be any that keep to these rules, and one draw needn't show every extreme that they name: `left_gram`: symmetric positive definite. `right_gram`: symmetric positive definite. `left_basis`: square and of full rank. `right_basis`: square and of full rank.
All inputs are finite; a program needn't handle non-finite values.
Results may differ from a plain program's by a relative error of at most 0.0015.
The roundings to bfloat16 on the way count: a program that leaves them out, or rounds other values in their place, can miss the bound.
Values may be sent and summed in bfloat16 or wider, within the bound.
No kernel may reach another device: no remote copies, remote signals or barrier semaphores. Data moves between devices by JAX's collectives and lax.ppermute only.
A program may use at most 64 MiB of HBM per device.

v0:
```python
import jax
import jax.numpy as jnp
from jax import lax
from jax.sharding import PartitionSpec as P

NS_ITERS = 2


BETA_ONE = 0.9
BETA_TWO = 0.95
GRAM_DECAY = 0.95
ADAM_EPS = 1e-08
NORM_EPS = 1e-06
STEP_SIZE = 0.02
START_SCALE = 0.75
PRECISE = lax.Precision.HIGHEST


def inner_rows(former, latter):
    return lax.dot_general(
        former, latter, (((0,), (0,)), ((), ())), preferred_element_type=jnp.float32
    )


def outer_rows(former, latter):
    return lax.dot_general(
        former, latter, (((1,), (1,)), ((), ())), preferred_element_type=jnp.float32
    )


def start_rows(power_rows, column_sums):
    scaled = START_SCALE * power_rows / jnp.sqrt(column_sums + NORM_EPS)
    return lax.optimization_barrier(scaled.astype(jnp.bfloat16))


def left_sweep(current):
    segment = lax.all_gather(current, "shard", axis=0, tiled=True)
    square = outer_rows(current, segment).astype(jnp.bfloat16)
    running = jnp.dot(square, segment, preferred_element_type=jnp.float32)
    return 1.5 * current.astype(jnp.float32) - 0.5 * running


def right_sweep(current):
    segment = lax.all_gather(current, "shard", axis=0, tiled=True)
    square = outer_rows(current, segment).astype(jnp.bfloat16)
    running = jnp.dot(square, segment, preferred_element_type=jnp.float32)
    return 1.5 * current.astype(jnp.float32) - 0.5 * running


def local(gradients, weight, moment, second, left_gram, left_basis, right_gram, right_basis):
    local_rows = weight.shape[0]
    right_rows = right_gram.shape[0]
    row_first = lax.axis_index("shard") * local_rows
    right_first = lax.axis_index("shard") * right_rows
    gradient = lax.psum(gradients[0], "grp") / lax.axis_size("grp")
    moment_new = BETA_ONE * moment + (1.0 - BETA_ONE) * gradient
    grad_half = gradient.astype(jnp.bfloat16)
    moment_half = moment_new.astype(jnp.bfloat16)
    left_half = left_basis.astype(jnp.bfloat16)
    right_whole = lax.all_gather(right_basis.astype(jnp.bfloat16), "shard", axis=0, tiled=True)
    right_wide = lax.optimization_barrier(right_whole).astype(jnp.float32)
    basis_part = lax.all_gather(left_half, "shard", axis=0, tiled=True)
    grad_part = lax.all_gather(grad_half, "shard", axis=0, tiled=True)
    basis_columns = lax.dynamic_slice_in_dim(basis_part, row_first, local_rows, 1)
    turned = inner_rows(basis_columns, grad_part)
    gram_block = GRAM_DECAY * left_gram + (1.0 - GRAM_DECAY) * outer_rows(grad_half, grad_part)
    power_rows = jnp.dot(gram_block, basis_part.astype(jnp.float32), precision=PRECISE)
    grad_columns = lax.dynamic_slice_in_dim(grad_part, right_first, right_rows, 1)
    right_terms = inner_rows(grad_columns, grad_part)
    core_state, basis_columns = ((turned, gram_block, power_rows, right_terms), basis_columns)
    core_state, turned_moment = (
        core_state,
        inner_rows(basis_columns, lax.all_gather(moment_half, "shard", axis=0, tiled=True)),
    )
    turned_grad, left_new, left_power, right_terms = core_state
    right_new = GRAM_DECAY * right_gram + (1.0 - GRAM_DECAY) * right_terms
    rotated_grad = jnp.dot(
        turned_grad.astype(jnp.bfloat16), right_whole, preferred_element_type=jnp.float32
    )
    rotated_moment = jnp.dot(
        turned_moment.astype(jnp.bfloat16), right_whole, preferred_element_type=jnp.float32
    )
    second_new = BETA_TWO * second + (1.0 - BETA_TWO) * rotated_grad * rotated_grad
    direction = (rotated_moment / (jnp.sqrt(second_new) + ADAM_EPS)).astype(jnp.bfloat16)
    returned = outer_rows(direction, right_whole).astype(jnp.bfloat16)
    update = jnp.dot(
        left_half,
        lax.all_gather(returned, "shard", axis=0, tiled=True),
        preferred_element_type=jnp.float32,
    )
    weight_new = weight - STEP_SIZE * update
    right_power = jnp.dot(right_new, right_wide, precision=PRECISE)
    left_sums, right_sums = lax.psum(
        (jnp.sum(left_power * left_power, axis=0), jnp.sum(right_power * right_power, axis=0)),
        "shard",
    )
    right_current = start_rows(right_power, right_sums)
    right_result = right_power
    for sweep in range(NS_ITERS):
        right_result = right_sweep(right_current)
        right_current = lax.optimization_barrier(right_result.astype(jnp.bfloat16))
    left_current = start_rows(left_power, left_sums)
    left_result = left_power
    for sweep in range(NS_ITERS):
        left_result = left_sweep(left_current)
        left_current = lax.optimization_barrier(left_result.astype(jnp.bfloat16))
    return (weight_new, moment_new, second_new, left_new, left_result, right_new, right_result)


def solution(mesh):
    return jax.shard_map(
        local,
        mesh=mesh,
        in_specs=(
            P("grp", "shard", None),
            P("shard", None),
            P("shard", None),
            P("shard", None),
            P("shard", None),
            P("shard", None),
            P("shard", None),
            P("shard", None),
        ),
        out_specs=(
            P("shard", None),
            P("shard", None),
            P("shard", None),
            P("shard", None),
            P("shard", None),
            P("shard", None),
            P("shard", None),
        ),
        check_vma=False,
    )
```

profile of v0, /device:TPU:2, one launch (start us, length us, event | category | flops | bytes accessed | tf_op | source)
XLA Modules:
  0.0 1857.0 jit_solution(10023106520451230898)
XLA Ops:
  7.2 0.0 copy-start.8
  7.2 0.0 all-gather.11.cloned.1.call-start
  7.2 36.2 %psum.21 = f32[16,512]{1,0:T(8,128)S(1)} all-reduce(f32[16,512]{1,0:T(8,128)} %bitcast.32), channel_id=1, replica_groups=mesh['grp'=8,'shard'=64] {'grp'}, use_global_device_ids=true, to_apply=%region_0.0 | all-reduce | flops 8192 | bytes 65536 | tf_op jit(solution)/shard_map/psum | solution.py:55
  43.4 1.4 fusion.29
  44.8 0.0 all-gather.11.cloned.1.call-update
  44.8 0.0 all-gather.7.cloned.1.call-start
  44.9 1.5 convert_element_type.62
  46.3 0.0 all-gather.7.cloned.1.call-update
  46.4 0.0 all-gather.9.cloned.1.call-start
  46.4 0.7 all-gather.9.cloned.1.call-update
  47.1 0.0 all-gather.15.cloned.1.call-start
  47.1 0.7 convert_element_type.65
  47.9 154.5 %all_gather.29 = bf16[512,512]{1,0:T(8,128)(2,1)S(1)} all-gather(bf16[8,512]{1,0:T(8,128)(2,1)S(1)} %convert_element_type.65), channel_id=1, replica_groups=mesh['grp'=8,'shard'=64] {'shard'}, dimensions={0}, use_global_device_ids=true | all-gather | bytes 532480 | tf_op jit(solution)/shard_map/all_gather | solution.py:60
  202.3 138.1 %all-gather.11.cloned.1.call-done = bf16[1024,512]{1,0:T(8,128)(2,1)} async-done(((bf16[16,512]{1,0:T(8,128)(2,1)}), bf16[1024,512]{1,0:T(8,128)(2,1)}) %all-gather.11.cloned.1.call-update) | async-done | bytes 1048592 | tf_op jit(solution)/shard_map/all_gather | solution.py:63
  340.4 1.7 fusion.8
  342.1 0.3 multiply_reduce_fusion.1
  342.4 0.0 copy-done.8
  342.4 0.0 copy-done.5
  342.4 1.6 fusion.2
  344.0 0.0 copy-start
  344.1 0.0 copy-start.9
  344.1 298.7 %all-gather.7.cloned.1.call-done = bf16[1024,1024]{1,0:T(8,128)(2,1)} async-done(((bf16[16,1024]{1,0:T(8,128)(2,1)}), bf16[1024,1024]{1,0:T(8,128)(2,1)}) %all-gather.7.cloned.1.call-update) | async-done | bytes 2097168 | tf_op jit(solution)/shard_map/all_gather | solution.py:62
  642.8 2.5 multiply_reduce_fusion
  645.4 156.0 %all-reduce = (f32[1024]{0:T(1024)S(1)}, f32[512]{0:T(512)S(1)}) all-reduce(f32[1024]{0:T(1024)S(1)} %get-tuple-element.12, f32[512]{0:T(512)S(1)} %get-tuple-element.14), channel_id=1, replica_groups=mesh['grp'=8,'shard'=64] {'shard'}, use_global_device_ids=true, to_apply=%region_2.0 | all-reduce | flops 1536 | bytes 12288 | tf_op jit(solution)/shard_map/psum | solution.py:93
  801.3 0.6 divide_convert_fusion
  802.0 0.0 all-gather.15.cloned.1.call-update
  802.0 0.0 all-gather.13.cloned.1.call-start
  802.0 0.0 copy-start.2
  802.1 140.5 %all-gather.9.cloned.1.call-done = bf16[1024,512]{1,0:T(8,128)(2,1)} async-done(((bf16[16,512]{1,0:T(8,128)(2,1)}), bf16[1024,512]{1,0:T(8,128)(2,1)}) %all-gather.9.cloned.1.call-update) | async-done | bytes 1048592 | tf_op jit(solution)/shard_map/all_gather | solution.py:73
  942.6 1.7 convolution_convert_fusion.3
  944.3 0.0 copy-done
  944.3 0.0 copy-done.9
  944.3 1.5 fusion.18
  945.8 0.0 copy-start.6
  945.8 1.0 convolution_convert_fusion.4
  946.8 0.0 all-gather.13.cloned.1.call-update
  946.8 0.0 all-gather.17.cloned.1.call-start
  946.8 298.1 %all-gather.15.cloned.1.call-done = bf16[1024,1024]{1,0:T(8,128)(2,1)} async-done(((bf16[16,1024]{1,0:T(8,128)(2,1)}), bf16[1024,1024]{1,0:T(8,128)(2,1)}) %all-gather.15.cloned.1.call-update) | async-done | bytes 2097168 | tf_op jit(solution)/shard_map/all_gather | solution.py:37
  1244.9 3.8 fusion.3
  1248.7 0.0 all-gather.17.cloned.1.call-update
  1248.8 0.0 copy-start.1
  1248.8 154.3 %all_gather.34 = bf16[512,512]{1,0:T(8,128)(2,1)S(1)} all-gather(bf16[8,512]{1,0:T(8,128)(2,1)S(1)} %divide_convert_fusion.1), channel_id=1, replica_groups=mesh['grp'=8,'shard'=64] {'shard'}, dimensions={0}, use_global_device_ids=true | all-gather | bytes 532480 | tf_op jit(solution)/shard_map/all_gather | solution.py:44
  1403.1 0.4 fusion.11
  1403.5 157.4 %all_gather.35 = bf16[512,512]{1,0:T(8,128)(2,1)S(1)} all-gather(bf16[8,512]{1,0:T(8,128)(2,1)S(1)} %fusion.11), channel_id=1, replica_groups=mesh['grp'=8,'shard'=64] {'shard'}, dimensions={0}, use_global_device_ids=true | all-gather | bytes 532480 | tf_op jit(solution)/shard_map/all_gather | solution.py:44
  1560.9 1.0 fusion.9
  1561.9 2.1 fusion.5
  1564.0 282.3 %all-gather.17.cloned.1.call-done = bf16[1024,1024]{1,0:T(8,128)(2,1)} async-done(((bf16[16,1024]{1,0:T(8,128)(2,1)}), bf16[1024,1024]{1,0:T(8,128)(2,1)}) %all-gather.17.cloned.1.call-update) | async-done | bytes 2097168 | tf_op jit(solution)/shard_map/all_gather | solution.py:37
  1846.3 3.8 fusion
  (16 shorter events, 0.0 us)
Async XLA Ops:
  7.2 335.3 %copy-start.8 = (f32[16,1024]{1,0:T(8,128)S(1)}, f32[16,1024]{1,0:T(8,128)}, u32[]{:S(2)}) copy-start(f32[16,1024]{1,0:T(8,128)} %param.12) | copy-start | bytes 196612
  7.2 333.2 %all-gather.11.cloned.1.call-start = ((), (), s32[]{:S(2)}) async-start(), calls=%async_computation.2 | async-start | bytes 1064960 | tf_op jit(solution)/shard_map/all_gather | solution.py:63
  44.8 297.6 %copy-start.5 = (bf16[16,512]{1,0:T(8,128)(2,1)S(1)}, bf16[16,512]{1,0:T(8,128)(2,1)}, u32[]{:S(2)}) copy-start(bf16[16,512]{1,0:T(8,128)(2,1)} %get-tuple-element.11) | copy-start | bytes 49156
  44.8 598.0 %all-gather.7.cloned.1.call-start = ((), (), s32[]{:S(2)}) async-start(), calls=%async_computation | async-start | bytes 2129920 | tf_op jit(solution)/shard_map/all_gather | solution.py:62
  46.4 896.2 %all-gather.9.cloned.1.call-start = ((), (), s32[]{:S(2)}) async-start(), calls=%async_computation.1 | async-start | bytes 1064960 | tf_op jit(solution)/shard_map/all_gather | solution.py:73
  47.1 1197.8 %all-gather.15.cloned.1.call-start = ((), (), s32[]{:S(2)}) async-start(), calls=%async_computation.4 | async-start | bytes 2129920 | tf_op jit(solution)/shard_map/all_gather | solution.py:37
  342.1 602.2 %copy-start.7 = (f32[8,512]{1,0:T(8,128)}, f32[8,512]{1,0:T(8,128)S(1)}, u32[]{:S(2)}) copy-start(f32[8,512]{1,0:T(8,128)S(1)} %fusion.8) | copy-start | bytes 49156
  344.0 601.7 %copy-start.4 = (f32[16,1024]{1,0:T(8,128)}, f32[16,1024]{1,0:T(8,128)S(1)}, u32[]{:S(2)}) copy-start(f32[16,1024]{1,0:T(8,128)S(1)} %fusion.2) | copy-start | bytes 196612
  344.0 600.2 %copy-start = (bf16[1024,512]{1,0:T(8,128)(2,1)S(1)}, bf16[1024,512]{1,0:T(8,128)(2,1)}, u32[]{:S(2)}) copy-start(bf16[1024,512]{1,0:T(8,128)(2,1)} %all-gather.11.cloned.1.call-done) | copy-start | bytes 3145732
  344.1 600.2 %copy-start.9 = (f32[16,512]{1,0:T(8,128)S(1)}, f32[16,512]{1,0:T(8,128)}, u32[]{:S(2)}) copy-start(f32[16,512]{1,0:T(8,128)} %param.11) | copy-start | bytes 98308
  802.0 759.9 %all-gather.13.cloned.1.call-start = ((), (), s32[]{:S(2)}) async-start(), calls=%async_computation.3 | async-start | bytes 1064960 | tf_op jit(solution)/shard_map/all_gather | solution.py:88
  802.0 442.9 %copy-start.2 = (bf16[16,1024]{1,0:T(8,128)(2,1)S(1)}, bf16[16,1024]{1,0:T(8,128)(2,1)}, u32[]{:S(2)}) copy-start(bf16[16,1024]{1,0:T(8,128)(2,1)} %divide_convert_fusion) | copy-start | bytes 98308
  945.8 303.0 %copy-start.6 = (f32[16,512]{1,0:T(8,128)}, f32[16,512]{1,0:T(8,128)S(1)}, u32[]{:S(2)}) copy-start(f32[16,512]{1,0:T(8,128)S(1)} %fusion.18) | copy-start | bytes 98308
  946.8 899.6 %all-gather.17.cloned.1.call-start = ((), (), s32[]{:S(2)}) async-start(), calls=%async_computation.5 | async-start | bytes 2129920 | tf_op jit(solution)/shard_map/all_gather | solution.py:37
  1248.7 313.2 %copy-start.3 = (bf16[16,1024]{1,0:T(8,128)(2,1)S(1)}, bf16[16,1024]{1,0:T(8,128)(2,1)}, u32[]{:S(2)}) copy-start(bf16[16,1024]{1,0:T(8,128)(2,1)} %convert_element_type.62) | copy-start | bytes 98308
  1248.7 313.2 %copy-start.10 = (f32[16,512]{1,0:T(8,128)S(1)}, f32[16,512]{1,0:T(8,128)}, u32[]{:S(2)}) copy-start(f32[16,512]{1,0:T(8,128)} %param.9) | copy-start | bytes 98308
  1248.8 597.6 %copy-start.1 = (bf16[16,1024]{1,0:T(8,128)(2,1)S(1)}, bf16[16,1024]{1,0:T(8,128)(2,1)}, u32[]{:S(2)}) copy-start(bf16[16,1024]{1,0:T(8,128)(2,1)} %fusion.3) | copy-start | bytes 98308
Sparse Core Ops, SparseCore 0:
  44.9 295.3 all-gather.10
  343.0 299.7 all-gather.6
  645.5 297.0 all-gather.8
  945.1 299.8 all-gather.14
  1246.9 297.0 all-gather.12
  1546.5 299.7 all-gather.16
where the time goes:
time: 1860 us
  waiting for transfers between devices  1160 us (62%)
  blocking collectives  658 us (35%)
  matrix products  21.4 us (1%)
    all_gather x2, waiting for transfers between devices, left_sweep(): segment = lax.all_gather(current, 'shard', axis=0, tiled=True)  580 us
    all_gather x2, blocking collectives, right_sweep(): segment = lax.all_gather(current, 'shard', axis=0, tiled=True)  312 us
    all_gather x1, waiting for transfers between devices, local(): basis_part = lax.all_gather(left_half, 'shard', axis=0, tiled=True)  299 us
    psum x1, blocking collectives, local(): lax.psum((jnp.sum(left_power * left_power, axis=0), jnp.sum(right_power *...  156 us
    all_gather x1, blocking collectives, local(): lax.all_gather(right_basis.astype(jnp.bfloat16), 'shard', axis=0, tiled=T...  154 us
    all_gather x1, waiting for transfers between devices, local(): lax.all_gather(moment_half, 'shard', axis=0, tiled=True)  141 us
    all_gather x1, waiting for transfers between devices, local(): grad_part = lax.all_gather(grad_half, 'shard', axis=0, tiled=True)  138 us
  transfers between devices with their start and end apart: 6, of which 5 were waited for; matrix products, arithmetic and copies ran while one was open for 1% of the time, Pallas kernels for 0%

commit v1 on v0

v1 whole, which is shorter than its diff:
```python
import jax
import jax.numpy as jnp
from jax import lax
from jax.sharding import Mesh, PartitionSpec as P

NS_ITERS = 2

BETA_ONE = 0.9
BETA_TWO = 0.95
GRAM_DECAY = 0.95
ADAM_EPS = 1e-08
NORM_EPS = 1e-06
STEP_SIZE = 0.02
START_SCALE = 0.75

AXES = ("zhi", "core", "zlo", "y", "x")
CUT = (4, 2, 2, 8, 4)
GRP = ("zhi", "core")
SHARD = ("zlo", "y", "x")
bf16 = jnp.bfloat16
f32 = jnp.float32


def mm(a, b, ca, cb):
    return lax.dot_general(a, b, (((ca,), (cb,)), ((), ())), preferred_element_type=f32)


def gather(value, axes, size):
    copies = jnp.broadcast_to(value[None], (size,) + value.shape)
    return lax.all_to_all(copies, axes, 0, 0)


def pair(value):
    high = lax.reduce_precision(value, 8, 7)
    return high.astype(bf16), (value - high).astype(bf16)


def newton_schulz(high, low, basis, first, count):
    power = mm(high, basis, 1, 0) + mm(low, basis, 1, 0)
    sums = jnp.sum(power * power, axis=0)
    current = lax.optimization_barrier((START_SCALE * power / jnp.sqrt(sums + NORM_EPS)).astype(bf16))
    for _ in range(NS_ITERS - 1):
        square = mm(current, current, 1, 1).astype(bf16)
        running = 1.5 * current.astype(f32) - 0.5 * mm(square, current, 1, 0)
        current = lax.optimization_barrier(running.astype(bf16))
    rows = lax.dynamic_slice_in_dim(current, first, count, 0)
    square = mm(rows, current, 1, 1).astype(bf16)
    return 1.5 * rows.astype(f32) - 0.5 * mm(square, current, 1, 0)


def local(gradients, weight, moment, second, left_gram, left_basis, right_gram, right_basis):
    n_grp = lax.axis_size(GRP)
    n_zlo, n_y, n_x = (lax.axis_size(a) for a in SHARD)
    rows, width = weight.shape
    right_rows = right_gram.shape[0]
    n_shard = n_zlo * n_y * n_x
    deep = n_shard * rows
    core = lax.axis_index("core")
    shard = lax.axis_index(SHARD)

    gradient = jnp.sum(gather(gradients[0], GRP, n_grp), axis=0) / n_grp
    moment_new = BETA_ONE * moment + (1.0 - BETA_ONE) * gradient
    grad_half = gradient.astype(bf16)
    moment_half = moment_new.astype(bf16)
    left_half = left_basis.astype(bf16)
    right_half = right_basis.astype(bf16)

    def mine(value):
        half = value.shape[1] // 2
        return jnp.where(core == 0, value[:, :half], value[:, half:])

    left_high, left_low = pair(left_gram)
    right_high, right_low = pair(right_gram)
    second_high, second_low = pair(second)
    right_pack = jnp.concatenate(
        [
            jnp.concatenate([mine(right_half), mine(right_high)], axis=0),
            jnp.concatenate([mine(right_low), mine(right_low)], axis=0),
        ],
        axis=1,
    )
    payload = jnp.stack(
        [
            mine(left_half),
            mine(left_high),
            mine(left_low),
            jnp.concatenate([mine(grad_half), mine(moment_half)], axis=1),
            jnp.concatenate([mine(second_high), mine(second_low)], axis=1),
            right_pack,
        ]
    )
    payload = gather(payload, "y", n_y)
    payload = gather(payload, ("zlo", "x"), n_zlo * n_x)
    other = lax.ppermute(payload, "core", [(0, 1), (1, 0)])
    def order(value):
        value = value.reshape(n_zlo, n_x, n_y, 6, rows, width)
        return value.transpose(3, 0, 2, 1, 4, 5)

    payload, other = order(payload), order(other)
    lower = jnp.where(core == 0, payload, other)
    upper = jnp.where(core == 0, other, payload)

    def whole(kind, which=slice(None), rows_=slice(None)):
        parts = [v[kind][..., rows_, :] for v in (lower, upper)]
        parts = [v.reshape(-1, v.shape[-1])[:, which] for v in parts]
        return jnp.concatenate(parts, axis=1)

    quarter = width // 2
    first_q, second_q = slice(0, quarter), slice(quarter, width)
    basis = whole(0)
    gram_high, gram_low = whole(1), whole(2)
    grad, mom = whole(3, first_q), whole(3, second_q)
    second_all = whole(4, first_q).astype(f32) + whole(4, second_q).astype(f32)
    right = whole(5, first_q, slice(0, right_rows))
    rgram_high = whole(5, first_q, slice(right_rows, rows))
    rgram_low = whole(5, second_q, slice(0, right_rows))

    row_first = shard * rows
    right_first = shard * right_rows

    gram = GRAM_DECAY * (gram_high.astype(f32) + gram_low.astype(f32)) + (1.0 - GRAM_DECAY) * mm(grad, grad, 1, 1)
    left_new = GRAM_DECAY * left_gram + (1.0 - GRAM_DECAY) * mm(grad_half, grad, 1, 1)
    left_result = newton_schulz(*pair(gram), basis, row_first, rows)
    rgram = GRAM_DECAY * (rgram_high.astype(f32) + rgram_low.astype(f32)) + (1.0 - GRAM_DECAY) * mm(grad, grad, 0, 0)
    grad_columns = lax.dynamic_slice_in_dim(grad, right_first, right_rows, 1)
    right_new = GRAM_DECAY * right_gram + (1.0 - GRAM_DECAY) * mm(grad_columns, grad, 0, 0)
    right_result = newton_schulz(*pair(rgram), right, right_first, right_rows)
    turned_grad = mm(basis, grad, 0, 0).astype(bf16)
    turned_moment = mm(basis, mom, 0, 0).astype(bf16)
    rotated_grad = mm(turned_grad, right, 1, 0)
    rotated_moment = mm(turned_moment, right, 1, 0)
    second_full = BETA_TWO * second_all + (1.0 - BETA_TWO) * rotated_grad * rotated_grad
    own_rotated = lax.dynamic_slice_in_dim(rotated_grad, row_first, rows, 0)
    second_new = BETA_TWO * second + (1.0 - BETA_TWO) * own_rotated * own_rotated
    direction = (rotated_moment / (jnp.sqrt(second_full) + ADAM_EPS)).astype(bf16)
    returned = mm(direction, right, 1, 1).astype(bf16)
    weight_new = weight - STEP_SIZE * mm(left_half, returned, 1, 0)
    return (weight_new, moment_new, second_new, left_new, left_result, right_new, right_result)


def solution(mesh):
    cut = Mesh(mesh.devices.reshape(CUT), AXES)
    rowwise = P(SHARD, None)
    return jax.shard_map(
        local,
        mesh=cut,
        in_specs=(P(GRP, SHARD, None),) + (rowwise,) * 7,
        out_specs=(rowwise,) * 7,
        check_vma=False,
    )
```

time: 1860 us -> 214 us (0.12)
  the two profiles are of different devices: /device:TPU:2 before, /device:TPU:1 now
where the time goes in v1:
time: 214 us; the launch traced here: 213 us
  blocking collectives  101 us (47%)
  matrix products  39.3 us (18%)
  local copies, waits for them, and re-layouts  20.4 us (10%)
  waiting for transfers between devices  18.3 us (9%)
  starting transfers between devices  17.8 us (8%)
  other arithmetic  14.9 us (7%)
    all_to_all x2, blocking collectives, gather(): return lax.all_to_all(copies, axes, 0, 0)  101 us
    dot_general x15, matrix products, mm(): lax.dot_general(a, b, (((ca,), (cb,)), ((), ())), preferred_element_type=...  39.3 us
    slice x18, local copies, waits for them, and re-layouts, whole(): parts = [v[kind][..., rows_, :] for v in (lower, upper)]  13 us
    all_to_all x1, starting transfers between devices, gather(): return lax.all_to_all(copies, axes, 0, 0)  11.8 us
    ppermute x1, waiting for transfers between devices, local(): other = lax.ppermute(payload, 'core', [(0, 1), (1, 0)])  10.1 us
    all_to_all x1, waiting for transfers between devices, gather(): return lax.all_to_all(copies, axes, 0, 0)  8.2 us
    ppermute x1, starting transfers between devices, local(): other = lax.ppermute(payload, 'core', [(0, 1), (1, 0)])  5.96 us
    select_n x1, other arithmetic, local(): lower = jnp.where(core == 0, payload, other)  5.26 us
  transfers between devices with their start and end apart: 2, of which 2 were waited for; matrix products, arithmetic and copies ran while one was open for 2% of the time, Pallas kernels for 0%

profile of v1, /device:TPU:1, one launch (start us, length us, event | category | flops | bytes accessed | tf_op | source)
XLA Modules:
  0.0 213.1 jit_solution(16783154568718157394)
XLA Ops:
  0.6 1.5 broadcast_in_dim.9
  2.1 11.8 %all-to-all-start = ((f32[8,16,512]{2,1,0:T(8,128)}), f32[8,16,512]{2,1,0:T(8,128)S(1)}, u32[]{:S(2)}, u32[]{:S(2)}) async-start(f32[8,16,512]{2,1,0:T(8,128)} %broadcast_in_dim.9), calls=%async_computation | async-start | bytes 524288 | tf_op jit(solution)/shard_map/all_to_all | solution.py:30
  13.9 0.8 convert_element_type.108
  14.8 0.8 fusion.36
  15.6 0.7 reduce-precision_convert_fusion.8
  16.4 0.7 convert_element_type.115
  17.1 0.8 reduce-precision_convert_fusion.7
  17.9 8.2 %all-to-all-done = f32[8,16,512]{2,1,0:T(8,128)S(1)} async-done(((f32[8,16,512]{2,1,0:T(8,128)}), f32[8,16,512]{2,1,0:T(8,128)S(1)}, u32[]{:S(2)}, u32[]{:S(2)}) %all-to-all-start) | async-done | bytes 262176 | tf_op jit(solution)/shard_map/all_to_all | solution.py:30
  26.2 1.4 fusion.61
  27.7 28.4 %all_to_all.15 = bf16[8,6,16,512]{3,2,1,0:T(8,128)(2,1)S(1)} all-to-all(bf16[8,6,16,512]{3,2,1,0:T(8,128)(2,1)S(1)} %broadcast_in_dim.10), channel_id=1, replica_groups=mesh['zhi'=4,'core'=2,'zlo'=2,'y'=8,'x'=4] {'y'}, dimensions={0} | all-to-all | bytes 1572864 | tf_op jit(solution)/shard_map/all_to_all | solution.py:30
  56.1 0.8 broadcast_in_dim.11
  56.9 73.0 %all_to_all.16 = bf16[8,8,6,16,512]{4,3,2,1,0:T(8,128)(2,1)} all-to-all(bf16[8,8,6,16,512]{4,3,2,1,0:T(8,128)(2,1)S(1)} %broadcast_in_dim.11), channel_id=1, replica_groups=mesh['zhi'=4,'core'=2,'zlo'=2,'y'=8,'x'=4] {'zlo','x'}, dimensions={0} | all-to-all | bytes 12582912 | tf_op jit(solution)/shard_map/all_to_all | solution.py:30
  129.9 6.0 %collective-permute-start = (bf16[8,8,6,16,512]{4,3,2,1,0:T(8,128)(2,1)}, bf16[8,8,6,16,512]{4,3,2,1,0:T(8,128)(2,1)}, u32[]{:S(2)}, u32[]{:S(2)}) collective-permute-start(bf16[8,8,6,16,512]{4,3,2,1,0:T(8,128)(2,1)} %all_to_all.16), channel_id=1, source_target_pairs={{0,64},{64,0},{1,65},{65,1},{2,66},{66,2},{3,67},{67,3},{4,68},{68... | collective-permute-start | bytes 18874376 | tf_op jit(solution)/shard_map/ppermute | solution.py:94
  135.9 10.1 %collective-permute-done = bf16[8,8,6,16,512]{4,3,2,1,0:T(8,128)(2,1)} collective-permute-done((bf16[8,8,6,16,512]{4,3,2,1,0:T(8,128)(2,1)}, bf16[8,8,6,16,512]{4,3,2,1,0:T(8,128)(2,1)}, u32[]{:S(2)}, u32[]{:S(2)}) %collective-permute-start) | collective-permute-done | bytes 6291488 | tf_op jit(solution)/shard_map/ppermute | solution.py:94
  146.0 5.3 %broadcast_select_fusion.1 = (bf16[8,8,6,16,512]{4,3,2,1,0:T(8,128)(2,1)S(1)}, bf16[8,8,6,16,512]{4,3,2,1,0:T(8,128)(2,1)S(1)}) fusion(bf16[8,8,6,16,512]{4,3,2,1,0:T(8,128)(2,1)} %all_to_all.16, bf16[8,8,6,16,512]{4,3,2,1,0:T(8,128)(2,1)} %collective-permute-done, pred[]{:T(512)S(6)} %eq.2), kind=kLoop, calls=%fused_computation.1 | loop fusion | flops 6291456 | bytes 25165824 | tf_op jit(solution)/shard_map/jit(_where)/select_n | solution.py:100
  151.3 2.0 fusion.62
  153.3 0.1 fusion.64
  153.5 2.3 %fusion.63 = (bf16[1,2,8,4,16,512]{5,4,0,2,3,1:T(8,128)(2,1)}, bf16[1,2,8,4,16,512]{5,4,0,2,3,1:T(8,128)(2,1)}, bf16[1,2,8,4,16,512]{5,4,0,2,3,1:T(8,128)(2,1)},...) fusion(bf16[6,2,8,4,16,512]{5,4,0,2,3,1:T(8,128)(2,1)S(1)} %bit, ...), kind=kLoop, calls=%fused_computation.108 | loop fusion | bytes 12582912 | tf_op jit(solution)/shard_map/slice | solution.py:104
  156.1 0.9 fusion.68
  157.1 0.9 fusion.69
  158.1 0.7 copy-done.12
  158.8 1.0 fusion.17
  159.8 0.8 fusion.13
  160.6 0.4 fusion.33
  161.1 0.5 multiply_reduce_fusion.1
  161.5 0.9 divide_convert_fusion.1
  162.5 3.6 %fusion.14 = bf16[512,512]{1,0:T(8,128)(2,1)} fusion(bf16[512,512]{1,0:T(8,128)(2,1)} %divide_convert_fusion.1), kind=kOutput, calls=%fused_computation.31 | convolution fusion | flops 538443776 | bytes 1048576 | tf_op jit(solution)/shard_map/dot_general | solution.py:25
  166.0 1.1 fusion.21
  167.2 2.2 %fusion.22 = f32[8,512]{1,0:T(8,128)} fusion(bf16[512,512]{1,0:T(8,128)(2,1)} %fusion.14, s32[]{:T(128)S(6)} %select_n.107), kind=kOutput, calls=%fused_computation.48 | convolution fusion | flops 8409088 | bytes 1082368 | tf_op jit(solution)/shard_map/dot_general | solution.py:25
  169.4 2.6 %copy.47 = bf16[1,2,8,4,16,512]{5,4,3,2,1,0:T(8,128)(2,1)} copy(bf16[1,2,8,4,16,512]{5,4,0,2,3,1:T(8,128)(2,1)} %get-tuple-element.12) | data formatting | bytes 2097152 | tf_op jit(solution)/shard_map/slice | solution.py:104
  171.9 1.1 copy.48
  173.0 1.1 copy.49
  174.1 1.2 copy.50
  175.3 1.1 copy.40
  176.3 1.1 copy.39
  177.4 4.8 %fusion.15 = f32[1024,512]{1,0:T(8,128)} fusion(bf16[1024,512]{1,0:T(8,128)(2,1)} %bitcast.76, bf16[1024,512]{1,0:T(8,128)(2,1)} %bitcast.80, bf16[512,256]{1,0:T(8,128)(2,1)} %copy-done.5, bf16[512,256]{1,0:T(8,128)(2,1)S(1)} %get-tuple-element.36, bf16[1024,256]{1,0:T(8,128)(2,1)S(1)} %get-tuple-element.34, bf16[1024,256]{1,0:T(8,128)(2,1)S(1)} %get-tuple-element.32), kind=kOutput, calls=%fused_computation.36 | convolution fusion | flops 1618477056 | bytes 5767168 | tf_op jit(solution)/shard_map/dot_general | solution.py:25
  182.1 3.5 %multiply_add_fusion = f32[1024,1024]{1,0:T(8,128)S(1)} fusion(bf16[1024,512]{1,0:T(8,128)(2,1)} %bitcast.85, bf16[1024,512]{1,0:T(8,128)(2,1)} %bitcast.84, bf16[1024,512]{1,0:T(8,128)(2,1)} %bitcast.87, bf16[1024,512]{1,0:T(8,128)(2,1)} %bitcast.86, bf16[1024,256]{1,0:T(8,128)(2,1)S(1)} %get-tuple-element.34, bf16[1024,256]{1,0:T(8,128)(2,1)S(1)} %get-tuple-element.32), kind=kOutput, calls=%fused_computation.8 | convolution fusion | flops 1088421888 | bytes 9437184 | tf_op jit(solution)/shard_map/dot_general | solution.py:25
  185.7 2.3 %fusion.5 = f32[1024,1024]{1,0:T(8,128)S(1)} fusion(f32[1024,1024]{1,0:T(8,128)S(1)} %multiply_add_fusion, bf16[1024,512]{1,0:T(8,128)(2,1)S(1)} %bitcast.78, bf16[1024,512]{1,0:T(8,128)(2,1)S(1)} %bitcast.82), kind=kOutput, calls=%fused_computation.14 | convolution fusion | flops 2154823680 | bytes 10485760 | tf_op jit(solution)/shard_map/dot_general | solution.py:25
  188.0 2.3 %multiply_reduce_fusion = (f32[1024]{0:T(1024)S(1)}, f32[1024,1024]{1,0:T(8,128)S(1)}) fusion(f32[1024,1024]{1,0:T(8,128)S(1)} %fusion.5, bf16[1024,512]{1,0:T(8,128)(2,1)S(1)} %bitcast.79, bf16[1024,512]{1,0:T(8,128)(2,1)S(1)} %bitcast.83, f32[1024,1024]{1,0:T(8,128)S(1)} %multiply_add_fusion), kind=kOutput, calls=%fused_computation.7 | convolution fusion | flops 2156919808 | bytes 14684160 | tf_op jit(solution)/shard_map/dot_general | solution.py:25
  190.4 1.9 divide_convert_fusion
  192.4 8.1 %subtract_convert_fusion = bf16[1024,1024]{1,0:T(8,128)(2,1)S(1)} fusion(bf16[1024,1024]{1,0:T(8,128)(2,1)} %divide_convert_fusion), kind=kOutput, calls=%fused_computation.5 | convolution fusion | flops 4301258752 | bytes 4194304 | tf_op jit(solution)/shard_map/dot_general | solution.py:25
  200.5 1.1 fusion.66
  201.6 0.4 copy-done
  202.1 1.0 fusion.67
  203.1 1.6 fusion.16
  204.7 1.4 fusion.38
  206.1 5.6 %fusion.9 = bf16[1024,512]{1,0:T(8,128)(2,1)S(1)} fusion(f32[1024,512]{1,0:T(8,128)} %fusion.15, bf16[1024,256]{1,0:T(8,128)(2,1)} %get-tuple-element.33, bf16[1024,256]{1,0:T(8,128)(2,1)S(1)} %copy-done.9, bf16[1024,256]{1,0:T(8,128)(2,1)} %get-tuple-element.30, bf16[1024,256]{1,0:T(8,128)(2,1)} %get-tuple-element.28, ...), kind=kOutput, calls=%fused_computation.18 | convolution fusion | flops 1626865664 | bytes 8912896 | tf_op jit(solution)/shard_map/dot_general | solution.py:25
  211.7 1.5 fusion.20
  (53 shorter events, 0.9 us)
Async XLA Ops:
  2.1 24.0 %all-to-all-start = ((f32[8,16,512]{2,1,0:T(8,128)}), f32[8,16,512]{2,1,0:T(8,128)S(1)}, u32[]{:S(2)}, u32[]{:S(2)}) async-start(f32[8,16,512]{2,1,0:T(8,128)} %broadcast_in_dim.9), calls=%async_computation | async-start | bytes 524288 | tf_op jit(solution)/shard_map/all_to_all | solution.py:30
  129.9 16.1 %collective-permute-start = (bf16[8,8,6,16,512]{4,3,2,1,0:T(8,128)(2,1)}, bf16[8,8,6,16,512]{4,3,2,1,0:T(8,128)(2,1)}, u32[]{:S(2)}, u32[]{:S(2)}) collective-permute-start(bf16[8,8,6,16,512]{4,3,2,1,0:T(8,128)(2,1)} %all_to_all.16), channel_id=1, source_target_pairs={{0,64},{64,0},{1,65},{65,1},{2,66},{66,2},{3,67},{67,3},{4,68},{68... | collective-permute-start | bytes 18874376 | tf_op jit(solution)/shard_map/ppermute | solution.py:94
  156.0 5.0 %copy-start.5 = (bf16[512,256]{1,0:T(8,128)(2,1)}, bf16[512,256]{1,0:T(8,128)(2,1)S(1)}, u32[]{:S(2)}) copy-start(bf16[512,256]{1,0:T(8,128)(2,1)S(1)} %get-tuple-element.38) | copy-start | bytes 786436
  157.9 0.8 copy-start.12
  162.5 3.6 %copy-start.11 = (f32[8,512]{1,0:T(8,128)S(1)}, f32[8,512]{1,0:T(8,128)}, u32[]{:S(2)}) copy-start(f32[8,512]{1,0:T(8,128)} %param.14) | copy-start | bytes 49156
  169.4 2.6 %copy-start.4 = (bf16[1,2,8,4,16,512]{5,4,0,2,3,1:T(8,128)(2,1)S(1)}, bf16[1,2,8,4,16,512]{5,4,0,2,3,1:T(8,128)(2,1)}, u32[]{:S(2)}) copy-start(bf16[1,2,8,4,16,512]{5,4,0,2,3,1:T(8,128)(2,1)} %get-tuple-element.18) | copy-start | bytes 3145732
  169.4 3.6 %copy-start.1 = (bf16[1,2,8,4,16,512]{5,4,0,2,3,1:T(8,128)(2,1)S(1)}, bf16[1,2,8,4,16,512]{5,4,0,2,3,1:T(8,128)(2,1)}, u32[]{:S(2)}) copy-start(bf16[1,2,8,4,16,512]{5,4,0,2,3,1:T(8,128)(2,1)} %get-tuple-element.11) | copy-start | bytes 3145732
  171.9 2.1 %copy-start.3 = (bf16[1,2,8,4,16,512]{5,4,0,2,3,1:T(8,128)(2,1)S(1)}, bf16[1,2,8,4,16,512]{5,4,0,2,3,1:T(8,128)(2,1)}, u32[]{:S(2)}) copy-start(bf16[1,2,8,4,16,512]{5,4,0,2,3,1:T(8,128)(2,1)} %get-tuple-element.17) | copy-start | bytes 3145732
  173.0 2.2 %copy-start.2 = (bf16[1,2,8,4,16,512]{5,4,0,2,3,1:T(8,128)(2,1)S(1)}, bf16[1,2,8,4,16,512]{5,4,0,2,3,1:T(8,128)(2,1)}, u32[]{:S(2)}) copy-start(bf16[1,2,8,4,16,512]{5,4,0,2,3,1:T(8,128)(2,1)} %get-tuple-element.22) | copy-start | bytes 3145732
  182.1 3.6 %copy-start.7 = (bf16[1,2,8,4,16,512]{5,4,3,2,1,0:T(8,128)(2,1)S(1)}, bf16[1,2,8,4,16,512]{5,4,3,2,1,0:T(8,128)(2,1)}, u32[]{:S(2)}) copy-start(bf16[1,2,8,4,16,512]{5,4,3,2,1,0:T(8,128)(2,1)} %copy.40) | copy-start | bytes 3145732
  182.1 3.6 %copy-start.8 = (bf16[1,2,8,4,16,512]{5,4,3,2,1,0:T(8,128)(2,1)S(1)}, bf16[1,2,8,4,16,512]{5,4,3,2,1,0:T(8,128)(2,1)}, u32[]{:S(2)}) copy-start(bf16[1,2,8,4,16,512]{5,4,3,2,1,0:T(8,128)(2,1)} %copy.39) | copy-start | bytes 3145732
  200.4 1.5 copy-start
  203.1 1.6 copy-start.10
  203.1 3.0 %copy-start.6 = (bf16[512,256]{1,0:T(8,128)(2,1)S(1)}, bf16[512,256]{1,0:T(8,128)(2,1)}, u32[]{:S(2)}) copy-start(bf16[512,256]{1,0:T(8,128)(2,1)} %copy-done.5) | copy-start | bytes 786436
  203.1 3.0 %copy-start.9 = (bf16[1024,256]{1,0:T(8,128)(2,1)S(1)}, bf16[1024,256]{1,0:T(8,128)(2,1)}, u32[]{:S(2)}) copy-start(bf16[1024,256]{1,0:T(8,128)(2,1)} %get-tuple-element.31) | copy-start | bytes 1572868
  206.1 5.6 %copy-start.13 = (f32[16,512]{1,0:T(8,128)S(1)}, f32[16,512]{1,0:T(8,128)}, u32[]{:S(2)}) copy-start(f32[16,512]{1,0:T(8,128)} %param.9) | copy-start | bytes 98308

commit v2 on v1

v2 whole, which is shorter than its diff:
```python
import jax
import jax.numpy as jnp
from jax import lax
from jax.experimental import pallas as pl
from jax.experimental.pallas import tpu as pltpu
from jax.sharding import Mesh, PartitionSpec as P

NS_ITERS = 2

BETA_ONE = 0.9
BETA_TWO = 0.95
GRAM_DECAY = 0.95
ADAM_EPS = 1e-08
NORM_EPS = 1e-06
STEP_SIZE = 0.02
START_SCALE = 0.75

AXES = ("zhi", "core", "zlo", "y", "x")
CUT = (4, 2, 2, 8, 4)
GRP = ("zhi", "core")
SHARD = ("zlo", "y", "x")
NZ, NY, NX = CUT[2:]
bf16 = jnp.bfloat16
f32 = jnp.float32

BLOCK = 128
BLOCKS = 8
SENT = BLOCKS // 2 + 1


def mm(a, b, ca, cb):
    return lax.dot_general(a, b, (((ca,), (cb,)), ((), ())), preferred_element_type=f32)


def gather(value, axes, size):
    copies = jnp.broadcast_to(value[None], (size,) + value.shape)
    return lax.all_to_all(copies, axes, 0, 0)


def pair(value):
    high = lax.reduce_precision(value, 8, 7)
    return high.astype(bf16), (value - high).astype(bf16)


def split(value):
    high = value.astype(bf16)
    return high, (value - high.astype(f32)).astype(bf16)


def refresh(power_tile, n_tiles, tile, first, count, power, start, current, out_ref):
    sums = None
    for t in range(n_tiles):
        p = power_tile(t)
        power[pl.ds(t * tile, tile), :] = p
        s = jnp.sum(p * p, axis=0, keepdims=True)
        sums = s if sums is None else sums + s
    scale = START_SCALE / jnp.sqrt(sums + NORM_EPS)
    for t in range(n_tiles):
        at = pl.ds(t * tile, tile)
        start[at, :] = (power[at, :] * scale).astype(bf16)
    x = start[...]
    for t in range(n_tiles):
        at = pl.ds(t * tile, tile)
        mine = start[at, :]
        square = mm(mine, x, 1, 1).astype(bf16)
        current[at, :] = (1.5 * mine.astype(f32) - 0.5 * mm(square, x, 1, 0)).astype(bf16)
    x = current[...]
    rows = current[pl.ds(pl.multiple_of(first, count), count), :]
    square = mm(rows, x, 1, 1).astype(bf16)
    out_ref[...] = 1.5 * rows.astype(f32) - 0.5 * mm(square, x, 1, 0)


def left_kernel(first_ref, mine_ref, other_ref, grad_ref, basis_ref, out_ref, gram, power, start, current):
    rows = mine_ref.shape[3]
    for r in range(BLOCKS):
        zlo, y2 = r // (BLOCKS // NZ), r % (BLOCKS // NZ)
        for j in range(SENT):
            c = (r + j) % BLOCKS
            pieces = []
            for y in (2 * y2, 2 * y2 + 1):
                for x in range(NX):
                    a = mine_ref[zlo, x, y, :, j * BLOCK : (j + 1) * BLOCK].astype(f32)
                    b = other_ref[zlo, x, y, :, j * BLOCK : (j + 1) * BLOCK].astype(f32)
                    pieces.append(a + b)
            block = GRAM_DECAY * jnp.concatenate(pieces, axis=0)
            gram[r * BLOCK : (r + 1) * BLOCK, c * BLOCK : (c + 1) * BLOCK] = block
            if 0 < j < BLOCKS // 2:
                gram[c * BLOCK : (c + 1) * BLOCK, r * BLOCK : (r + 1) * BLOCK] = block.T
    grad = grad_ref[...]
    basis = basis_ref[...]
    tile = 256

    def power_tile(t):
        at = pl.ds(t * tile, tile)
        whole = gram[at, :] + (1.0 - GRAM_DECAY) * mm(grad_ref[at, :], grad, 1, 1)
        high, low = split(whole)
        return mm(high, basis, 1, 0) + mm(low, basis, 1, 0)

    refresh(power_tile, gram.shape[0] // tile, tile, first_ref[0], rows, power, start, current, out_ref)


def left_call(first, mine, other, grad, basis, rows):
    deep = basis.shape[0]
    vmem = pl.BlockSpec(memory_space=pltpu.VMEM)
    return pl.pallas_call(
        left_kernel,
        out_shape=jax.ShapeDtypeStruct((rows, deep), f32),
        in_specs=[pl.BlockSpec(memory_space=pltpu.SMEM)] + [vmem] * 4,
        out_specs=vmem,
        scratch_shapes=[
            pltpu.VMEM((deep, deep), f32),
            pltpu.VMEM((deep, deep), f32),
            pltpu.VMEM((deep, deep), bf16),
            pltpu.VMEM((deep, deep), bf16),
        ],
        compiler_params=pltpu.CompilerParams(vmem_limit_bytes=40 << 20),
        name="left_refresh",
    )(first, mine, other, grad, basis)


def right_kernel(first_ref, gram_ref, grad_ref, basis_ref, out_ref, power, start, current):
    rows = out_ref.shape[0]
    basis = basis_ref[...]
    grad = grad_ref[...]
    tile = 256

    def power_tile(t):
        at = pl.ds(t * tile, tile)
        whole = GRAM_DECAY * gram_ref[at, :] + (1.0 - GRAM_DECAY) * mm(grad_ref[:, t * tile : (t + 1) * tile], grad, 0, 0)
        high, low = split(whole)
        return mm(high, basis, 1, 0) + mm(low, basis, 1, 0)

    refresh(power_tile, gram_ref.shape[0] // tile, tile, first_ref[0], rows, power, start, current, out_ref)


def right_call(first, gram, grad, basis, rows):
    width = basis.shape[0]
    vmem = pl.BlockSpec(memory_space=pltpu.VMEM)
    return pl.pallas_call(
        right_kernel,
        out_shape=jax.ShapeDtypeStruct((rows, width), f32),
        in_specs=[pl.BlockSpec(memory_space=pltpu.SMEM)] + [vmem] * 3,
        out_specs=vmem,
        scratch_shapes=[
            pltpu.VMEM((width, width), f32),
            pltpu.VMEM((width, width), bf16),
            pltpu.VMEM((width, width), bf16),
        ],
        compiler_params=pltpu.CompilerParams(vmem_limit_bytes=16 << 20),
        name="right_refresh",
    )(first, gram, grad, basis)


def local(gradients, weight, moment, second, left_gram, left_basis, right_gram, right_basis):
    n_grp = CUT[0] * CUT[1]
    rows, width = weight.shape
    right_rows = right_gram.shape[0]
    n_shard = NZ * NY * NX
    deep = n_shard * rows
    core = lax.axis_index("core")
    group = lax.axis_index(GRP)
    shard = lax.axis_index(SHARD)
    row_first = shard * rows
    right_first = shard * right_rows
    first = core == 0

    gradient = jnp.sum(gather(gradients[0], GRP, n_grp), axis=0) / n_grp
    moment_new = BETA_ONE * moment + (1.0 - BETA_ONE) * gradient
    grad_half = gradient.astype(bf16)
    moment_half = moment_new.astype(bf16)
    left_half = left_basis.astype(bf16)
    right_half = right_basis.astype(bf16)

    def fold(value, parts):
        return jnp.concatenate(jnp.split(value, parts, axis=1), axis=0)

    share = rows // n_grp
    own_second = jnp.concatenate([fold(v, 4) for v in pair(lax.dynamic_slice_in_dim(second, group * share, share, 0))], axis=0)
    start = (shard // (n_shard // BLOCKS)) * BLOCK
    round_gram = jnp.concatenate([left_gram, left_gram[:, : (SENT - 1) * BLOCK]], axis=1)
    sent_gram = lax.dynamic_slice_in_dim(round_gram, start, SENT * BLOCK, 1)
    half = deep // 2
    payload = jnp.concatenate(
        [
            jnp.where(first, left_half[:, :half], left_half[:, half:]),
            jnp.where(first, grad_half, moment_half),
            fold(jnp.where(first, right_half[:, : width // 2], right_half[:, width // 2 :]), 2),
            fold(jnp.where(first, *pair(right_gram)), 2),
            own_second,
            jnp.where(first, *pair(sent_gram)),
        ],
        axis=1,
    )
    cut = payload.shape[1] - SENT * BLOCK
    payload = gather(payload, "y", NY)
    early = gather(payload[..., :cut], ("zlo", "x"), NZ * NX)
    swap = [(0, 1), (1, 0)]
    shared = early[..., : cut - 128]
    shared_other = lax.ppermute(shared, "core", swap)
    late = gather(payload[..., cut:], ("zlo", "x"), NZ * NX)
    late_other = lax.ppermute(late, "core", swap)

    def order(value):
        value = value.reshape((NZ, NX) + value.shape[1:])
        return value.transpose(0, 2, 1, 3, 4)

    def unfold(value, parts):
        value = jnp.concatenate(jnp.split(value, parts, axis=-2), axis=-1)
        return value.reshape(-1, value.shape[-1])

    def lanes(at, n):
        return order(shared[..., at : at + n]), order(shared_other[..., at : at + n])

    basis = jnp.concatenate([v.reshape(deep, half) for v in lanes(0, half)], axis=1)
    a, b = (v.reshape(deep, width) for v in lanes(half, width))
    grad, mom = jnp.where(first, a, b), jnp.where(first, b, a)
    a, b = (unfold(v, 2) for v in lanes(half + width, width // 4))
    right = jnp.where(first, jnp.concatenate([a, b], axis=1), jnp.concatenate([b, a], axis=1))
    a, b = (unfold(v, 2) for v in lanes(half + width + width // 4, width // 2))
    rgram = a.astype(f32) + b.astype(f32)
    second_parts = early[..., cut - 128 :]
    n_part = rows // 2
    second_rows = unfold(second_parts[..., :n_part, :], 4).astype(f32) + unfold(second_parts[..., n_part:, :], 4).astype(f32)

    mine_rows = n_shard * share
    q = lax.broadcasted_iota(jnp.int32, (deep, mine_rows), 1)
    column = (lax.broadcasted_iota(jnp.int32, (deep, mine_rows), 0) + core * half) % deep
    zx, y, r = q // (NY * share), (q // share) % NY, q % share
    wanted = ((zx // NX * NY + y) * NX + zx % NX) * rows + group * share + r
    pick = (column == wanted).astype(bf16)
    q = lax.broadcasted_iota(jnp.int32, (deep, rows), 1)
    column = (lax.broadcasted_iota(jnp.int32, (deep, rows), 0) + core * half) % deep
    pick_own = (column == row_first + q).astype(bf16)
    left_columns = mm(basis, jnp.concatenate([pick, pick_own], axis=1), 1, 0).astype(bf16)
    turned_grad = mm(left_columns, grad, 0, 0).astype(bf16)
    turned_moment = mm(left_columns[:, :mine_rows], mom, 0, 0).astype(bf16)
    rotated_grad = mm(turned_grad, right, 1, 0)
    rotated_moment = mm(turned_moment, right, 1, 0)
    part_grad, own_grad = rotated_grad[:mine_rows], rotated_grad[mine_rows:]
    second_part = BETA_TWO * second_rows + (1.0 - BETA_TWO) * part_grad * part_grad
    second_new = BETA_TWO * second + (1.0 - BETA_TWO) * own_grad * own_grad
    direction = (rotated_moment / (jnp.sqrt(second_part) + ADAM_EPS)).astype(bf16)
    returned = mm(direction, right, 1, 1).astype(bf16)
    left_rows = jnp.where(first, left_half, jnp.concatenate([left_half[:, half:], left_half[:, :half]], axis=1))
    left_rows = mm(left_rows, pick, 1, 0).astype(bf16)
    update = jnp.sum(gather(mm(left_rows, returned, 1, 0), GRP, n_grp), axis=0)
    weight_new = weight - STEP_SIZE * update

    left_new = GRAM_DECAY * left_gram + (1.0 - GRAM_DECAY) * mm(grad_half, grad, 1, 1)
    grad_columns = lax.dynamic_slice_in_dim(grad, right_first, right_rows, 1)
    right_new = GRAM_DECAY * right_gram + (1.0 - GRAM_DECAY) * mm(grad_columns, grad, 0, 0)
    right_result = right_call((right_first // rows * rows)[None], rgram, grad, right, rows)
    right_result = lax.dynamic_slice_in_dim(right_result, right_first % rows, right_rows, 0)

    five = lambda v: v.reshape((NZ, NX) + v.shape[1:])
    left_result = left_call(row_first[None], five(late), five(late_other), grad, basis, rows)
    swapped = jnp.concatenate([left_result[:, half:], left_result[:, :half]], axis=1)
    left_result = jnp.where(first, left_result, swapped)
    return (weight_new, moment_new, second_new, left_new, left_result, right_new, right_result)


def solution(mesh):
    cut = Mesh(mesh.devices.reshape(CUT), AXES)
    rowwise = P(SHARD, None)
    return jax.shard_map(
        local,
        mesh=cut,
        in_specs=(P(GRP, SHARD, None),) + (rowwise,) * 7,
        out_specs=(rowwise,) * 7,
        check_vma=False,
    )
```

time: 214 us -> 171 us (0.80)
  blocking collectives: 101 us -> 23.4 us
  waiting for transfers between devices: 18.3 us -> 59.1 us
  matrix products: 39.3 us -> 7.74 us
  Pallas kernels: 0 us -> 15.6 us
  starting transfers between devices: 17.8 us -> 28.7 us
  other arithmetic: 14.9 us -> 12.3 us
    all_to_all x2 -> x1, blocking collectives: 101 us -> 23.4 us  [gather(): return lax.all_to_all(copies, axes, 0, 0)]
    all_to_all x1 -> x4, waiting for transfers between devices: 8.2 us -> 59.1 us  [gather(): return lax.all_to_all(copies, axes, 0, 0)]
    dot_general x15 -> x7, matrix products: 39.3 us -> 7.74 us  [mm(): lax.dot_general(a, b, (((ca,), (cb,)), ((), ())), preferred_element_type=...]
    pallas_call x0 -> x2, Pallas kernels: none -> 15.6 us  [the longest x1 12.8 us: left_call(): pl.pallas_call(left_kernel, out_shape=jax.ShapeDtypeStruct((rows, deep),...]
    all_to_all x1 -> x4, starting transfers between devices: 11.8 us -> 23 us  [gather(): return lax.all_to_all(copies, axes, 0, 0)]
    slice x26 -> x12, local copies, waits for them, and re-layouts: 17 us -> 6.58 us  [the longest x1 3.73 us: local(): shared = early[..., :cut - 128]]
    ppermute x1 -> x2, waiting for transfers between devices: 10.1 us -> 0.01 us  [the longest x1 0.01 us: local(): shared_other = lax.ppermute(shared, 'core', swap)]
    convert_element_type x3 -> x0, other arithmetic: 4.27 us -> none  [the longest x2 2.89 us: newton_schulz(): (START_SCALE * power / jnp.sqrt(sums + NORM_EPS)).astype(bf16)]
  transfers between devices with their start and end apart: 2 -> 6, of which waited for: 2 -> 4; matrix products, arithmetic and copies ran while one was open for 2% -> 13% of each run, Pallas kernels for 0% -> 2%
where the time goes in v2:
time: 171 us; the launch traced here: 169 us
  waiting for transfers between devices  59.1 us (35%)
  starting transfers between devices  28.7 us (17%)
  blocking collectives  23.4 us (14%)
  local copies, waits for them, and re-layouts  21.4 us (13%)
  Pallas kernels  15.6 us (9%)
  other arithmetic  12.3 us (7%)
  matrix products  7.74 us (5%)
    all_to_all x4, waiting for transfers between devices, gather(): return lax.all_to_all(copies, axes, 0, 0)  59.1 us
    all_to_all x1, blocking collectives, gather(): return lax.all_to_all(copies, axes, 0, 0)  23.4 us
    all_to_all x4, starting transfers between devices, gather(): return lax.all_to_all(copies, axes, 0, 0)  23 us
    pallas_call x1, Pallas kernels, left_call(): pl.pallas_call(left_kernel, out_shape=jax.ShapeDtypeStruct((rows, deep),...  12.8 us
    dot_general x7, matrix products, mm(): lax.dot_general(a, b, (((ca,), (cb,)), ((), ())), preferred_element_type=...  7.74 us
    broadcast_in_dim x5, local copies, waits for them, and re-layouts, gather(): copies = jnp.broadcast_to(value[None], (size,) + value.shape)  5.59 us
    slice x1, local copies, waits for them, and re-layouts, local(): shared = early[..., :cut - 128]  3.73 us
    unnamed x23, local copies, waits for them, and re-layouts  3.56 us
  transfers between devices with their start and end apart: 6, of which 4 were waited for; matrix products, arithmetic and copies ran while one was open for 13% of the time, Pallas kernels for 2%

profile of v2, /device:TPU:1, one launch (start us, length us, event | category | flops | bytes accessed | tf_op | source)
XLA Modules:
  0.0 169.4 jit_solution(16440564579464244268)
XLA Ops:
  0.6 1.5 broadcast_in_dim.17
  2.1 11.8 %all-to-all-start = ((f32[8,16,512]{2,1,0:T(8,128)}), f32[8,16,512]{2,1,0:T(8,128)S(1)}, u32[]{:S(2)}, u32[]{:S(2)}) async-start(f32[8,16,512]{2,1,0:T(8,128)} %broadcast_in_dim.17), calls=%async_computation | async-start | bytes 524288 | tf_op jit(solution)/shard_map/all_to_all | solution.py:37
  13.9 0.7 convert_element_type.70
  14.7 0.7 fusion.36
  15.4 0.7 fusion.37
  16.1 0.8 convert_element_type.66
  17.0 0.8 slice.86
  17.8 8.3 %all-to-all-done = f32[8,16,512]{2,1,0:T(8,128)S(1)} async-done(((f32[8,16,512]{2,1,0:T(8,128)}), f32[8,16,512]{2,1,0:T(8,128)S(1)}, u32[]{:S(2)}, u32[]{:S(2)}) %all-to-all-start) | async-done | bytes 262176 | tf_op jit(solution)/shard_map/all_to_all | solution.py:37
  26.1 1.4 select_dynamic-update-slice_fusion
  27.5 0.8 fusion.34
  28.4 23.4 %all_to_all.25 = bf16[8,16,2176]{2,1,0:T(8,128)(2,1)S(1)} all-to-all(bf16[8,16,2176]{2,1,0:T(8,128)(2,1)S(1)} %broadcast_in_dim.18), channel_id=1, replica_groups=mesh['zhi'=4,'core'=2,'zlo'=2,'y'=8,'x'=4] {'y'}, dimensions={0} | all-to-all | bytes 1114112 | tf_op jit(solution)/shard_map/all_to_all | solution.py:37
  51.8 0.8 copy-done.2
  52.6 2.0 %broadcast_in_dim.19 = bf16[8,8,16,1536]{3,2,1,0:T(8,128)(2,1)} broadcast(bf16[8,16,1536]{2,1,0:T(8,128)(2,1)S(1)} %slice.107), dimensions={1,2,3} | broadcast | bytes 3538944 | tf_op jit(solution)/shard_map/broadcast_in_dim | solution.py:36
  54.6 4.2 %all-to-all-start.2 = ((bf16[8,8,16,1536]{3,2,1,0:T(8,128)(2,1)}), bf16[8,8,16,1536]{3,2,1,0:T(8,128)(2,1)S(1)}, u32[]{:S(2)}, u32[]{:S(2)}) async-start(bf16[8,8,16,1536]{3,2,1,0:T(8,128)(2,1)} %broadcast_in_dim.19), calls=%async_computation.2 | async-start | bytes 6291456 | tf_op jit(solution)/shard_map/all_to_all | solution.py:37
  58.8 37.4 %all-to-all-done.2 = bf16[8,8,16,1536]{3,2,1,0:T(8,128)(2,1)S(1)} async-done(((bf16[8,8,16,1536]{3,2,1,0:T(8,128)(2,1)}), bf16[8,8,16,1536]{3,2,1,0:T(8,128)(2,1)S(1)}, u32[]{:S(2)}, u32[]{:S(2)}) %all-to-all-start.2) | async-done | bytes 3145760 | tf_op jit(solution)/shard_map/all_to_all | solution.py:37
  96.2 1.3 broadcast_in_dim.43
  97.5 0.7 copy-done
  98.2 3.7 %all-to-all-start.4 = ((bf16[8,8,16,640]{3,2,1,0:T(8,128)(2,1)}), bf16[8,8,16,640]{3,2,1,0:T(8,128)(2,1)S(1)}, u32[]{:S(2)}, u32[]{:S(2)}) async-start(bf16[8,8,16,640]{3,2,1,0:T(8,128)(2,1)} %broadcast_in_dim.43), calls=%async_computation.4 | async-start | bytes 2621440 | tf_op jit(solution)/shard_map/all_to_all | solution.py:37
  101.9 3.7 %slice.109 = bf16[8,8,16,1408]{3,2,1,0:T(8,128)(2,1)} slice(bf16[8,8,16,1536]{3,2,1,0:T(8,128)(2,1)} %copy-done), slice={[0:8], [0:8], [0:16], [0:1408]} | slice | bytes 5767168 | tf_op jit(solution)/shard_map/slice | solution.py:198
  105.6 2.8 %collective-permute-start = (bf16[8,8,16,1408]{3,2,1,0:T(8,128)(2,1)}, bf16[8,8,16,1408]{3,2,1,0:T(8,128)(2,1)}, u32[]{:S(2)}, u32[]{:S(2)}) collective-permute-start(bf16[8,8,16,1408]{3,2,1,0:T(8,128)(2,1)} %slice.109), channel_id=1, source_target_pairs={{0,64},{64,0},{1,65},{65,1},{2,66},{66,2},{3,67},{67,3},{4,68},{68... | collective-permute-start | bytes 8650760 | tf_op jit(solution)/shard_map/ppermute | solution.py:199
  108.6 0.9 fusion.15
  109.7 0.5 copy-done.4
  110.1 1.4 select_compare_fusion.2
  111.6 8.1 %all-to-all-done.4 = bf16[8,8,16,640]{3,2,1,0:T(8,128)(2,1)S(1)} async-done(((bf16[8,8,16,640]{3,2,1,0:T(8,128)(2,1)}), bf16[8,8,16,640]{3,2,1,0:T(8,128)(2,1)S(1)}, u32[]{:S(2)}, u32[]{:S(2)}) %all-to-all-start.4) | async-done | bytes 1310752 | tf_op jit(solution)/shard_map/all_to_all | solution.py:37
  119.7 2.9 %collective-permute-start.1 = (bf16[8,8,16,640]{3,2,1,0:T(8,128)(2,1)S(1)}, bf16[8,8,16,640]{3,2,1,0:T(8,128)(2,1)}, u32[]{:S(2)}, u32[]{:S(2)}) collective-permute-start(bf16[8,8,16,640]{3,2,1,0:T(8,128)(2,1)S(1)} %all-to-all-done.4), channel_id=1, source_target_pairs={{0,64},{64,0},{1,65},{65,1},{2,66},{66,2},{3,67},{67,3},{4,68},{68... | collective-permute-start | bytes 3932168 | tf_op jit(solution)/shard_map/ppermute | solution.py:201
  122.7 1.8 %fusion.43 = (bf16[8,8,2,128]{3,2,1,0:T(2,128)(2,1)S(1)}, bf16[8,8,2,128]{3,2,1,0:T(2,128)(2,1)S(1)}, bf16[8,8,2,128]{3,2,1,0:T(2,128)(2,1)S(1)}, bf16[8,8,2,128...) fusion(bf16[8,8,16,1536]{3,2,1,0:T(8,128)(2,1)} %copy-done), kind=kLoop, calls=%fused_computation.110 | loop fusion | bytes 524288 | tf_op jit(solution)/shard_map/split | solution.py:208
  124.9 0.7 copy.25
  125.6 0.9 mul.135
  126.5 1.1 slice.122
  127.9 1.6 copy-done.1
  129.4 1.8 %broadcast_select_fusion = (bf16[8,8,16,512]{3,2,1,0:T(8,128)(2,1)S(1)}, bf16[8,8,16,512]{3,2,1,0:T(8,128)(2,1)S(1)}, bf16[8,8,16,512]{3,2,1,0:T(8,128)(2,1)S(1)}, bf16[8,8,16,512]{3,2,1,0:T(8,128)(2,1)S(1)}) fusion(pred[]{:T(512)S(6)} %eq.18, bf16[8,8,16,1536]{3,2,1,0:T(8,128)(2,1)S(1)} %copy-done.1, bf16[8,8,16,1408]{3,2,1,0:T(8,128)(2,1)} %collective-permute-done), kind=kLoop, calls=%fused_computation.22 | loop fusion | flops 1048576 | bytes 8388609 | tf_op jit(solution)/shard_map/jit(_where)/select_n | solution.py:216
  131.4 1.0 slice.115
  132.9 12.8 %left_refresh.1 = f32[16,1024]{1,0:T(8,128)S(1)} custom-call(s32[1]{0:T(128)} %bitcast.21.first_ref, bf16[2,4,8,16,640]{4,3,2,1,0:T(8,128)(2,1)S(1)} %bitcast.52, bf16[2,4,8,16,640]{4,3,2,1,0:T(8,128)(2,1)} %bitcast.23.other_ref, bf16[1024,512]{1,0:T(8,128)(2,1)S(1)} %bitcast.47, bf16[1024,1024]{1,0:T(8,128)(2,1)S(1)} %pad_maximum_fusion.basis_ref), custom_call_target="tpu_custom_call" | custom-call | tf_op jit(solution)/shard_map/left_refresh/pallas_call | solution.py:105
  145.8 1.8 %convolution_convert_fusion = bf16[1024,144]{0,1:T(8,128)(2,1)} fusion(pred[1024,16]{1,0:T(32,128)(4,1)S(1)} %copy-done.7, pred[1024,128]{1,0:T(32,128)(4,1)S(1)} %copy-done.5, bf16[1024,512]{1,0:T(8,128)(2,1)S(1)} %bitcast.63, bf16[1024,512]{1,0:T(8,128)(2,1)S(1)} %bitcast.61), kind=kOutput, calls=%fused_computation.5 | convolution fusion | flops 306479104 | bytes 2539520 | tf_op jit(solution)/shard_map/dot_general | solution.py:32
  147.5 1.0 copy.24
  148.7 1.5 fusion.1
  150.2 1.8 %fusion = bf16[128,512]{1,0:T(8,128)(2,1)S(1)} fusion(bf16[512,512]{1,0:T(8,128)(2,1)S(1)} %maximum_select_fusion.basis_ref, bf16[1024,512]{1,0:T(8,128)(2,1)} %bitcast.65, f32[128,512]{1,0:T(8,128)} %mul.135, f32[144,512]{1,0:T(8,128)S(1)} %fusion.1, bf16[1024,144]{0,1:T(8,128)(2,1)} %convolution_convert_fusion), kind=kOutput, calls=%fused_computation.8 | convolution fusion | flops 201785344 | bytes 2490368 | tf_op jit(solution)/shard_map/dot_general | solution.py:32
  152.1 0.4 fusion.2
  152.5 0.7 broadcast_in_dim.20
  153.2 3.4 %all-to-all-start.3 = ((f32[8,16,512]{2,1,0:T(8,128)}), f32[8,16,512]{2,1,0:T(8,128)S(1)}, u32[]{:S(2)}, u32[]{:S(2)}) async-start(f32[8,16,512]{2,1,0:T(8,128)} %broadcast_in_dim.20), calls=%async_computation.3 | async-start | bytes 524288 | tf_op jit(solution)/shard_map/all_to_all | solution.py:37
  156.6 1.1 fusion.4
  157.7 2.8 %right_refresh.1 = f32[16,512]{1,0:T(8,128)S(1)} custom-call(s32[1]{0:T(128)} %bitcast.24.first_ref, f32[512,512]{1,0:T(8,128)S(1)} %bitcast.53, bf16[1024,512]{1,0:T(8,128)(2,1)S(1)} %bitcast.50, bf16[512,512]{1,0:T(8,128)(2,1)S(1)} %maximum_select_fusion.basis_ref), custom_call_target="tpu_custom_call" | custom-call | tf_op jit(solution)/shard_map/right_refresh/pallas_call | solution.py:139
  160.5 0.6 constant_dynamic-slice_fusion
  161.1 0.6 maximum_select_fusion.1
  161.7 0.6 fusion.29
  162.4 1.0 fusion.3
  163.4 5.4 %all-to-all-done.3 = f32[8,16,512]{2,1,0:T(8,128)S(1)} async-done(((f32[8,16,512]{2,1,0:T(8,128)}), f32[8,16,512]{2,1,0:T(8,128)S(1)}, u32[]{:S(2)}, u32[]{:S(2)}) %all-to-all-start.3) | async-done | bytes 262176 | tf_op jit(solution)/shard_map/all_to_all | solution.py:37
  168.8 0.6 multiply_subtract_fusion
  (64 shorter events, 2.0 us)
Async XLA Ops:
  2.1 24.0 %all-to-all-start = ((f32[8,16,512]{2,1,0:T(8,128)}), f32[8,16,512]{2,1,0:T(8,128)S(1)}, u32[]{:S(2)}, u32[]{:S(2)}) async-start(f32[8,16,512]{2,1,0:T(8,128)} %broadcast_in_dim.17), calls=%async_computation | async-start | bytes 524288 | tf_op jit(solution)/shard_map/all_to_all | solution.py:37
  51.8 0.8 copy-start.2
  54.6 41.5 %slice-start.2 = ((bf16[8,16,2176]{2,1,0:T(8,128)(2,1)}), bf16[8,16,640]{2,1,0:T(8,128)(2,1)S(1)}, s32[]{:S(2)}) async-start(bf16[8,16,2176]{2,1,0:T(8,128)(2,1)} %copy-done.2), calls=%async_computation.7 | async-start | bytes 327680 | tf_op jit(solution)/shard_map/slice | solution.py:200
  54.6 41.5 %all-to-all-start.2 = ((bf16[8,8,16,1536]{3,2,1,0:T(8,128)(2,1)}), bf16[8,8,16,1536]{3,2,1,0:T(8,128)(2,1)S(1)}, u32[]{:S(2)}, u32[]{:S(2)}) async-start(bf16[8,8,16,1536]{3,2,1,0:T(8,128)(2,1)} %broadcast_in_dim.19), calls=%async_computation.2 | async-start | bytes 6291456 | tf_op jit(solution)/shard_map/all_to_all | solution.py:37
  96.2 2.0 %copy-start = (bf16[8,8,16,1536]{3,2,1,0:T(8,128)(2,1)}, bf16[8,8,16,1536]{3,2,1,0:T(8,128)(2,1)S(1)}, u32[]{:S(2)}) copy-start(bf16[8,8,16,1536]{3,2,1,0:T(8,128)(2,1)S(1)} %all-to-all-done.2) | copy-start | bytes 9437188
  98.2 21.5 %all-to-all-start.4 = ((bf16[8,8,16,640]{3,2,1,0:T(8,128)(2,1)}), bf16[8,8,16,640]{3,2,1,0:T(8,128)(2,1)S(1)}, u32[]{:S(2)}, u32[]{:S(2)}) async-start(bf16[8,8,16,640]{3,2,1,0:T(8,128)(2,1)} %broadcast_in_dim.43), calls=%async_computation.4 | async-start | bytes 2621440 | tf_op jit(solution)/shard_map/all_to_all | solution.py:37
  101.9 20.7 %slice-start.1 = ((bf16[8,8,16,1536]{3,2,1,0:T(8,128)(2,1)}), bf16[8,8,16,128]{3,2,1,0:T(8,128)(2,1)S(1)}, s32[]{:S(2)}) async-start(bf16[8,8,16,1536]{3,2,1,0:T(8,128)(2,1)} %copy-done), calls=%async_computation.6 | async-start | bytes 524288 | tf_op jit(solution)/shard_map/slice | solution.py:212
  105.6 18.8 %slice-start = ((bf16[8,8,16,1536]{3,2,1,0:T(8,128)(2,1)}), bf16[8,8,16,256]{3,2,1,0:T(8,128)(2,1)S(1)}, s32[]{:S(2)}) async-start(bf16[8,8,16,1536]{3,2,1,0:T(8,128)(2,1)} %copy-done), calls=%async_computation.5 | async-start | bytes 1048576 | tf_op jit(solution)/shard_map/slice | solution.py:212
  105.6 20.8 %collective-permute-start = (bf16[8,8,16,1408]{3,2,1,0:T(8,128)(2,1)}, bf16[8,8,16,1408]{3,2,1,0:T(8,128)(2,1)}, u32[]{:S(2)}, u32[]{:S(2)}) collective-permute-start(bf16[8,8,16,1408]{3,2,1,0:T(8,128)(2,1)} %slice.109), channel_id=1, source_target_pairs={{0,64},{64,0},{1,65},{65,1},{2,66},{66,2},{3,67},{67,3},{4,68},{68... | collective-permute-start | bytes 8650760 | tf_op jit(solution)/shard_map/ppermute | solution.py:199
  109.5 0.6 copy-start.4
  119.7 13.2 %collective-permute-start.1 = (bf16[8,8,16,640]{3,2,1,0:T(8,128)(2,1)S(1)}, bf16[8,8,16,640]{3,2,1,0:T(8,128)(2,1)}, u32[]{:S(2)}, u32[]{:S(2)}) collective-permute-start(bf16[8,8,16,640]{3,2,1,0:T(8,128)(2,1)S(1)} %all-to-all-done.4), channel_id=1, source_target_pairs={{0,64},{64,0},{1,65},{65,1},{2,66},{66,2},{3,67},{67,3},{4,68},{68... | collective-permute-start | bytes 3932168 | tf_op jit(solution)/shard_map/ppermute | solution.py:201
  127.6 1.9 %copy-start.1 = (bf16[8,8,16,1536]{3,2,1,0:T(8,128)(2,1)S(1)}, bf16[8,8,16,1536]{3,2,1,0:T(8,128)(2,1)}, u32[]{:S(2)}) copy-start(bf16[8,8,16,1536]{3,2,1,0:T(8,128)(2,1)} %copy-done) | copy-start | bytes 9437188
  132.9 12.8 %copy-start.5 = (pred[1024,128]{1,0:T(32,128)(4,1)S(1)}, pred[1024,128]{1,0:T(32,128)(4,1)}, u32[]{:S(2)}) copy-start(pred[1024,128]{1,0:T(32,128)(4,1)} %copy-done.4) | copy-start | bytes 393220
  132.9 12.8 %copy-start.7 = (pred[1024,16]{1,0:T(32,128)(4,1)S(1)}, pred[1024,16]{1,0:T(32,128)(4,1)}, u32[]{:S(2)}) copy-start(pred[1024,16]{1,0:T(32,128)(4,1)} %select_compare_fusion.2) | copy-start | bytes 49156
  145.7 2.8 %copy-start.3 = (bf16[2,8,4,8,256]{4,3,2,1,0:T(8,128)(2,1)S(1)}, bf16[2,8,4,8,256]{4,3,2,1,0:T(8,128)(2,1)}, u32[]{:S(2)}) copy-start(bf16[2,8,4,8,256]{4,3,2,1,0:T(8,128)(2,1)} %copy.25) | copy-start | bytes 786436
  148.7 7.9 %copy-start.8 = (f32[8,512]{1,0:T(8,128)S(1)}, f32[8,512]{1,0:T(8,128)}, u32[]{:S(2)}) copy-start(f32[8,512]{1,0:T(8,128)} %param.14) | copy-start | bytes 49156
  152.0 9.7 %copy-start.9 = (f32[16,512]{1,0:T(8,128)S(1)}, f32[16,512]{1,0:T(8,128)}, u32[]{:S(2)}) copy-start(f32[16,512]{1,0:T(8,128)} %param.11) | copy-start | bytes 98308
  152.1 10.3 %copy-start.6 = (f32[16,1024]{1,0:T(8,128)S(1)}, f32[16,1024]{1,0:T(8,128)}, u32[]{:S(2)}) copy-start(f32[16,1024]{1,0:T(8,128)} %param.12) | copy-start | bytes 196612
  153.2 15.5 %all-to-all-start.3 = ((f32[8,16,512]{2,1,0:T(8,128)}), f32[8,16,512]{2,1,0:T(8,128)S(1)}, u32[]{:S(2)}, u32[]{:S(2)}) async-start(f32[8,16,512]{2,1,0:T(8,128)} %broadcast_in_dim.20), calls=%async_computation.3 | async-start | bytes 524288 | tf_op jit(solution)/shard_map/all_to_all | solution.py:37
  156.6 12.2 %copy-start.10 = (f32[16,512]{1,0:T(8,128)S(1)}, f32[16,512]{1,0:T(8,128)}, u32[]{:S(2)}) copy-start(f32[16,512]{1,0:T(8,128)} %param.9) | copy-start | bytes 98308

commit v3 on v2

v3 whole, which is shorter than its diff:
```python
import jax
import jax.numpy as jnp
from jax import lax
from jax.experimental import pallas as pl
from jax.experimental.pallas import tpu as pltpu
from jax.sharding import Mesh, PartitionSpec as P

NS_ITERS = 2

BETA_ONE = 0.9
BETA_TWO = 0.95
GRAM_DECAY = 0.95
ADAM_EPS = 1e-08
NORM_EPS = 1e-06
STEP_SIZE = 0.02
START_SCALE = 0.75

AXES = ("zhi", "core", "zlo", "yhi", "ylo", "x")
CUT = (4, 2, 2, 4, 2, 4)
GRP = ("zhi", "core")
SHARD = ("zlo", "yhi", "ylo", "x")
NEAR = ("zlo", "ylo", "x")
NZ, NF, NY, NX = CUT[2:]
bf16 = jnp.bfloat16
f32 = jnp.float32

BLOCK = 128
BLOCKS = 8
SENT = BLOCKS // 2 + 1


def mm(a, b, ca, cb):
    return lax.dot_general(a, b, (((ca,), (cb,)), ((), ())), preferred_element_type=f32)


def gather(value, axes, size):
    copies = jnp.broadcast_to(value[None], (size,) + value.shape)
    return lax.all_to_all(copies, axes, 0, 0)


def pair(value):
    high = lax.reduce_precision(value, 8, 7)
    return high.astype(bf16), (value - high).astype(bf16)


def split(value):
    high = value.astype(bf16)
    return high, (value - high.astype(f32)).astype(bf16)


def refresh(power_tile, n_tiles, tile, first, count, power, start, current, out_ref):
    sums = None
    for t in range(n_tiles):
        p = power_tile(t)
        power[pl.ds(t * tile, tile), :] = p
        s = jnp.sum(p * p, axis=0, keepdims=True)
        sums = s if sums is None else sums + s
    scale = START_SCALE / jnp.sqrt(sums + NORM_EPS)
    for t in range(n_tiles):
        at = pl.ds(t * tile, tile)
        start[at, :] = (power[at, :] * scale).astype(bf16)
    x = start[...]
    for t in range(n_tiles):
        at = pl.ds(t * tile, tile)
        mine = start[at, :]
        square = mm(mine, x, 1, 1).astype(bf16)
        current[at, :] = (1.5 * mine.astype(f32) - 0.5 * mm(square, x, 1, 0)).astype(bf16)
    x = current[...]
    rows = current[pl.ds(pl.multiple_of(first, count), count), :]
    square = mm(rows, x, 1, 1).astype(bf16)
    out_ref[...] = 1.5 * rows.astype(f32) - 0.5 * mm(square, x, 1, 0)


def left_kernel(first_ref, mine_ref, other_ref, grad_ref, basis_ref, out_ref, gram, power, start, current):
    rows = mine_ref.shape[-2]
    for r in range(BLOCKS):
        zlo, far = r // NF, r % NF
        for j in range(SENT):
            c = (r + j) % BLOCKS
            at = pl.ds(j * BLOCK, BLOCK)
            pieces = []
            for near in range(NY * NX):
                place = (zlo, near // NX, near % NX, far, slice(None), at)
                pieces.append(mine_ref[place].astype(f32) + other_ref[place].astype(f32))
            block = GRAM_DECAY * jnp.concatenate(pieces, axis=0)
            gram[r * BLOCK : (r + 1) * BLOCK, c * BLOCK : (c + 1) * BLOCK] = block
            if 0 < j < BLOCKS // 2:
                gram[c * BLOCK : (c + 1) * BLOCK, r * BLOCK : (r + 1) * BLOCK] = block.T
    grad = grad_ref[...]
    basis = basis_ref[...]
    tile = 256

    def power_tile(t):
        at = pl.ds(t * tile, tile)
        whole = gram[at, :] + (1.0 - GRAM_DECAY) * mm(grad_ref[at, :], grad, 1, 1)
        high, low = split(whole)
        return mm(high, basis, 1, 0) + mm(low, basis, 1, 0)

    refresh(power_tile, gram.shape[0] // tile, tile, first_ref[0], rows, power, start, current, out_ref)


def left_call(first, mine, other, grad, basis, rows):
    deep = basis.shape[0]
    vmem = pl.BlockSpec(memory_space=pltpu.VMEM)
    return pl.pallas_call(
        left_kernel,
        out_shape=jax.ShapeDtypeStruct((rows, deep), f32),
        in_specs=[pl.BlockSpec(memory_space=pltpu.SMEM)] + [vmem] * 4,
        out_specs=vmem,
        scratch_shapes=[
            pltpu.VMEM((deep, deep), f32),
            pltpu.VMEM((deep, deep), f32),
            pltpu.VMEM((deep, deep), bf16),
            pltpu.VMEM((deep, deep), bf16),
        ],
        compiler_params=pltpu.CompilerParams(vmem_limit_bytes=40 << 20),
        cost_estimate=pl.CostEstimate(flops=10 * deep**3, transcendentals=deep, bytes_accessed=8 * deep**2),
        name="left_refresh",
    )(first, mine, other, grad, basis)


def mid_kernel(
    at_ref, mine_ref, other_ref, second_rows_ref, second_ref, left_rows_ref, left_gram_ref,
    basis_ref, grad_ref, update_ref, second_new_ref, left_new_ref, right_term_ref, right_out_ref,
    mom, right, rgram, power, start, current,
):
    core, group, row_first, right_first = (at_ref[i] for i in range(4))
    first = core == 0
    rows, width = second_ref.shape
    deep = basis_ref.shape[0]
    half = deep // 2
    share = second_rows_ref.shape[0] // (deep // rows)
    right_rows = rows // 2
    spot = 0
    for zlo in range(NZ):
        for far in range(NF):
            for y in range(NY):
                for x in range(NX):
                    def lanes(at, n):
                        place = (zlo, y, x, far, slice(None), pl.ds(at, n))
                        return mine_ref[place], other_ref[place]

                    to = pl.ds(spot * rows, rows)
                    a, b = lanes(0, half)
                    basis_ref[to, :half] = a
                    basis_ref[to, half:] = b
                    a, b = lanes(half, width)
                    grad_ref[to, :] = jnp.where(first, a, b)
                    mom[to, :] = jnp.where(first, b, a)
                    to = pl.ds(spot * right_rows, right_rows)
                    n = width // 4
                    a, b = (v.astype(f32) for v in lanes(half + width, n))
                    low, high = jnp.where(first, a, b), jnp.where(first, b, a)
                    for part in range(2):
                        of = slice(part * right_rows, (part + 1) * right_rows)
                        right[to, part * n : (part + 1) * n] = low[of]
                        right[to, (2 + part) * n : (3 + part) * n] = high[of]
                    a, b = lanes(half + width + n, 2 * n)
                    both = GRAM_DECAY * (a.astype(f32) + b.astype(f32))
                    for part in range(2):
                        of = slice(part * right_rows, (part + 1) * right_rows)
                        rgram[to, part * 2 * n : (part + 1) * 2 * n] = both[of]
                    spot += 1
    basis, grad = basis_ref[...], grad_ref[...]
    rbasis = right[...].astype(bf16)

    n = second_rows_ref.shape[0]
    q = lax.broadcasted_iota(jnp.int32, (1, n), 1)
    r, far, near = q % share, (q // share) % NF, q // (share * NF)
    wanted = ((near // (NY * NX) * NF + far) * (NY * NX) + near % (NY * NX)) * rows + group * share + r
    column = (lax.broadcasted_iota(jnp.int32, (deep, n), 0) + core * half) % deep
    pick = jnp.where(column == wanted, 1.0, 0.0).astype(bf16)
    q = lax.broadcasted_iota(jnp.int32, (1, n), 1)
    own = jnp.where((column == row_first + q) & (q < rows), 1.0, 0.0).astype(bf16)
    columns = mm(basis, pick, 1, 0).astype(bf16)
    own_columns = mm(basis, own, 1, 0).astype(bf16)
    rotated_grad = mm(mm(columns, grad, 0, 0).astype(bf16), rbasis, 1, 0)
    rotated_moment = mm(mm(columns, mom[...], 0, 0).astype(bf16), rbasis, 1, 0)
    own_grad = mm(mm(own_columns, grad, 0, 0).astype(bf16), rbasis, 1, 0)[:rows]
    second_part = BETA_TWO * second_rows_ref[...] + (1.0 - BETA_TWO) * rotated_grad * rotated_grad
    second_new_ref[...] = BETA_TWO * second_ref[...] + (1.0 - BETA_TWO) * own_grad * own_grad
    direction = (rotated_moment / (jnp.sqrt(second_part) + ADAM_EPS)).astype(bf16)
    returned = mm(direction, rbasis, 1, 1).astype(bf16)
    own_rows = left_rows_ref[...]
    own_rows = jnp.where(first, own_rows, jnp.concatenate([own_rows[:, half:], own_rows[:, :half]], axis=1))
    update_ref[...] = mm(mm(own_rows, pick, 1, 0).astype(bf16), returned, 1, 0)

    own_grad = grad_ref[pl.ds(pl.multiple_of(row_first, rows), rows), :]
    left_new_ref[...] = GRAM_DECAY * left_gram_ref[...] + (1.0 - GRAM_DECAY) * mm(own_grad, grad, 1, 1)
    q = lax.broadcasted_iota(jnp.int32, (width, BLOCK), 1)
    column = lax.broadcasted_iota(jnp.int32, (width, BLOCK), 0)
    own = jnp.where((column == right_first + q) & (q < rows), 1.0, 0.0).astype(bf16)
    right_term_ref[...] = mm(mm(grad, own, 1, 0).astype(bf16), grad, 0, 0)[:rows]

    tile = 256

    def power_tile(t):
        at = pl.ds(t * tile, tile)
        whole = rgram[at, :] + (1.0 - GRAM_DECAY) * mm(grad_ref[:, t * tile : (t + 1) * tile], grad, 0, 0)
        high, low = split(whole)
        return mm(high, rbasis, 1, 0) + mm(low, rbasis, 1, 0)

    refresh(power_tile, width // tile, tile, right_first, rows, power, start, current, right_out_ref)


def mid_call(at, mine, other, second_rows, second, left_rows, left_gram):
    rows, deep = left_rows.shape
    width = second.shape[1]
    vmem = pl.BlockSpec(memory_space=pltpu.VMEM)
    shapes = [
        ((deep, deep), bf16), ((deep, width), bf16), ((rows, width), f32), ((rows, width), f32),
        ((rows, deep), f32), ((rows, width), f32), ((rows, width), f32),
    ]
    return pl.pallas_call(
        mid_kernel,
        out_shape=[jax.ShapeDtypeStruct(*v) for v in shapes],
        in_specs=[pl.BlockSpec(memory_space=pltpu.SMEM)] + [vmem] * 6,
        out_specs=[vmem] * len(shapes),
        scratch_shapes=[
            pltpu.VMEM((deep, width), bf16),
            pltpu.VMEM((width, width), f32),
            pltpu.VMEM((width, width), f32),
            pltpu.VMEM((width, width), f32),
            pltpu.VMEM((width, width), bf16),
            pltpu.VMEM((width, width), bf16),
        ],
        compiler_params=pltpu.CompilerParams(vmem_limit_bytes=40 << 20),
        cost_estimate=pl.CostEstimate(flops=6 * deep**3, transcendentals=width**2, bytes_accessed=12 * deep**2),
        name="middle",
    )(at, mine, other, second_rows, second, left_rows, left_gram)


def local(gradients, weight, moment, second, left_gram, left_basis, right_gram, right_basis):
    n_grp = CUT[0] * CUT[1]
    rows, width = weight.shape
    right_rows = right_gram.shape[0]
    n_shard = NZ * NF * NY * NX
    deep = n_shard * rows
    core = lax.axis_index("core")
    group = lax.axis_index(GRP)
    shard = lax.axis_index(SHARD)
    row_first = shard * rows
    right_first = shard * right_rows
    first = core == 0

    gradient = jnp.sum(gather(gradients[0], GRP, n_grp), axis=0) / n_grp
    moment_new = BETA_ONE * moment + (1.0 - BETA_ONE) * gradient
    grad_half = gradient.astype(bf16)
    moment_half = moment_new.astype(bf16)
    left_half = left_basis.astype(bf16)
    right_half = right_basis.astype(bf16)

    def fold(value, parts):
        return jnp.concatenate(jnp.split(value, parts, axis=1), axis=0)

    share = rows // n_grp
    own_second = jnp.concatenate([fold(v, 4) for v in pair(lax.dynamic_slice_in_dim(second, group * share, share, 0))], axis=0)
    start = (shard // (n_shard // BLOCKS)) * BLOCK
    round_gram = jnp.concatenate([left_gram, left_gram[:, : (SENT - 1) * BLOCK]], axis=1)
    sent_gram = lax.dynamic_slice_in_dim(round_gram, start, SENT * BLOCK, 1)
    half = deep // 2
    payload = jnp.concatenate(
        [
            jnp.where(first, left_half[:, :half], left_half[:, half:]),
            jnp.where(first, grad_half, moment_half),
            fold(jnp.where(first, right_half[:, : width // 2], right_half[:, width // 2 :]), 2),
            fold(jnp.where(first, *pair(right_gram)), 2),
            own_second,
            jnp.where(first, *pair(sent_gram)),
        ],
        axis=1,
    )
    cut = payload.shape[1] - SENT * BLOCK
    payload = gather(payload, "yhi", NF)
    near = NZ * NY * NX
    parted = lambda v: v.reshape((NZ, NY, NX) + v.shape[1:])
    swap = [(0, 1), (1, 0)]
    early = gather(payload[..., :cut], NEAR, near)
    early_other = lax.ppermute(early, "core", swap)
    late = gather(payload[..., cut:], NEAR, near)

    second_parts = early[..., cut - 128 :].astype(f32)
    second_parts = second_parts[..., : rows // 2, :] + second_parts[..., rows // 2 :, :]
    second_rows = jnp.concatenate(jnp.split(second_parts, 4, axis=-2), axis=-1).reshape(-1, width)

    at = jnp.stack([core, group, row_first, right_first // rows * rows]).astype(jnp.int32)
    results = mid_call(at, parted(early), parted(early_other), second_rows, second, left_half, left_gram)
    results, late = lax.optimization_barrier((results, late))
    basis, grad, update, second_new, left_new, right_term, right_result = results
    late_other = lax.ppermute(late, "core", swap)
    updates = gather(update, GRP, n_grp)
    own = lambda v: lax.dynamic_slice_in_dim(v, right_first % rows, right_rows, 0)
    right_new = GRAM_DECAY * right_gram + (1.0 - GRAM_DECAY) * own(right_term)
    right_result = own(right_result)
    left_result = left_call(row_first[None], parted(late), parted(late_other), grad, basis, rows)
    updates, left_result = lax.optimization_barrier((updates, left_result))
    weight_new = weight - STEP_SIZE * jnp.sum(updates, axis=0)
    swapped = jnp.concatenate([left_result[:, half:], left_result[:, :half]], axis=1)
    left_result = jnp.where(first, left_result, swapped)
    return (weight_new, moment_new, second_new, left_new, left_result, right_new, right_result)


def solution(mesh):
    cut = Mesh(mesh.devices.reshape(CUT), AXES)
    rowwise = P(SHARD, None)
    return jax.shard_map(
        local,
        mesh=cut,
        in_specs=(P(GRP, SHARD, None),) + (rowwise,) * 7,
        out_specs=(rowwise,) * 7,
        check_vma=False,
    )
```

time: 171 us -> 146 us (0.85)
  waiting for transfers between devices: 59.1 us -> 13.5 us
  blocking collectives: 23.4 us -> 56 us
  matrix products: 7.74 us -> 0 us
  local copies, waits for them, and re-layouts: 21.4 us -> 14.4 us
  Pallas kernels: 15.6 us -> 21.2 us
  other arithmetic: 12.3 us -> 8.84 us
    all_to_all x4 -> x3, waiting for transfers between devices: 59.1 us -> 13.5 us  [gather(): return lax.all_to_all(copies, axes, 0, 0)]
    all_to_all x1 -> x2, blocking collectives: 23.4 us -> 56 us  [gather(): return lax.all_to_all(copies, axes, 0, 0)]
    dot_general x7 -> x0, matrix products: 7.74 us -> none  [mm(): lax.dot_general(a, b, (((ca,), (cb,)), ((), ())), preferred_element_type=...]
    slice x10 -> x2, local copies, waits for them, and re-layouts: 5.81 us -> 0.02 us  [the longest x1 0.01 us: local(): early = gather(payload[..., :cut], NEAR, near)]
    pallas_call x1, Pallas kernels: 2.81 us -> 8.49 us  [mid_call(): pl.pallas_call(mid_kernel, out_shape=[jax.ShapeDtypeStruct(*v) for v in s...]
    ppermute x1, starting transfers between devices: 2.8 us -> 6.6 us  [local(): early_other = lax.ppermute(early, 'core', swap)]
    unnamed x23 -> x19, local copies, waits for them, and re-layouts: 3.56 us -> 7.13 us
    all_to_all x4 -> x3, starting transfers between devices: 23 us -> 19.9 us  [gather(): return lax.all_to_all(copies, axes, 0, 0)]
  transfers between devices with their start and end apart: 6 -> 5, of which waited for: 4 -> 2; matrix products, arithmetic and copies ran while one was open for 13% -> 7% of each run, Pallas kernels for 2% -> 15%
where the time goes in v3:
time: 146 us; the launch traced here: 144 us
  blocking collectives  56 us (38%)
  starting transfers between devices  29.5 us (20%)
  Pallas kernels  21.2 us (15%)
  local copies, waits for them, and re-layouts  14.4 us (10%)
  waiting for transfers between devices  13.5 us (9%)
  other arithmetic  8.84 us (6%)
    all_to_all x2, blocking collectives, gather(): return lax.all_to_all(copies, axes, 0, 0)  56 us
    all_to_all x3, starting transfers between devices, gather(): return lax.all_to_all(copies, axes, 0, 0)  19.9 us
    all_to_all x3, waiting for transfers between devices, gather(): return lax.all_to_all(copies, axes, 0, 0)  13.5 us
    pallas_call x1, Pallas kernels, left_call(): pl.pallas_call(left_kernel, out_shape=jax.ShapeDtypeStruct((rows, deep),...  12.7 us
    pallas_call x1, Pallas kernels, mid_call(): pl.pallas_call(mid_kernel, out_shape=[jax.ShapeDtypeStruct(*v) for v in s...  8.49 us
    unnamed x19, local copies, waits for them, and re-layouts  7.13 us
    ppermute x1, starting transfers between devices, local(): early_other = lax.ppermute(early, 'core', swap)  6.6 us
    broadcast_in_dim x5, local copies, waits for them, and re-layouts, gather(): copies = jnp.broadcast_to(value[None], (size,) + value.shape)  3.88 us
  transfers between devices with their start and end apart: 5, of which 2 were waited for; matrix products, arithmetic and copies ran while one was open for 7% of the time, Pallas kernels for 15%

profile of v3, /device:TPU:1, one launch (start us, length us, event | category | flops | bytes accessed | tf_op | source)
XLA Modules:
  0.0 144.3 jit_solution(3712423072567489796)
XLA Ops:
  0.6 1.5 %broadcast_in_dim.13 = f32[8,16,512]{2,1,0:T(8,128)} broadcast(f32[16,512]{1,0:T(8,128)} %bitcast.11), dimensions={1,2} | broadcast | bytes 294912 | tf_op jit(solution)/shard_map/broadcast_in_dim | solution.py:37
  2.1 11.8 %all-to-all-start = ((f32[8,16,512]{2,1,0:T(8,128)}), f32[8,16,512]{2,1,0:T(8,128)S(1)}, u32[]{:S(2)}, u32[]{:S(2)}) async-start(f32[8,16,512]{2,1,0:T(8,128)} %broadcast_in_dim.13), calls=%async_computation | async-start | bytes 524288 | tf_op jit(solution)/shard_map/all_to_all | solution.py:38
  13.9 0.7 convert_element_type.36
  14.6 0.7 fusion.8
  15.4 0.7 fusion.9
  16.1 0.8 convert_element_type.33.left_rows_ref
  17.0 0.8 slice.40
  17.7 0.1 concatenate.23
  17.8 8.3 %all-to-all-done = f32[8,16,512]{2,1,0:T(8,128)S(1)} async-done(((f32[8,16,512]{2,1,0:T(8,128)}), f32[8,16,512]{2,1,0:T(8,128)S(1)}, u32[]{:S(2)}, u32[]{:S(2)}) %all-to-all-start) | async-done | bytes 262176 | tf_op jit(solution)/shard_map/all_to_all | solution.py:38
  26.1 1.4 fusion.6
  27.5 0.8 fusion.3
  28.4 15.9 %all_to_all.25 = bf16[4,16,2176]{2,1,0:T(8,128)(2,1)S(1)} all-to-all(bf16[4,16,2176]{2,1,0:T(8,128)(2,1)S(1)} %broadcast_in_dim.14), channel_id=1, replica_groups=mesh['zhi'=4,'core'=2,'zlo'=2,'yhi'=4,'ylo'=2,'x'=4] {'yhi'}, dimensions={0} | all-to-all | bytes 557056 | tf_op jit(solution)/shard_map/all_to_all | solution.py:38
  44.3 0.4 broadcast_in_dim.15
  44.7 40.1 %all_to_all.26 = bf16[16,4,16,1536]{3,2,1,0:T(8,128)(2,1)S(1)} all-to-all(bf16[16,4,16,1536]{3,2,1,0:T(8,128)(2,1)S(1)} %broadcast_in_dim.15), channel_id=1, replica_groups=mesh['zhi'=4,'core'=2,'zlo'=2,'yhi'=4,'ylo'=2,'x'=4] {'zlo','ylo','x'}, dimensions={0} | all-to-all | bytes 6291456 | tf_op jit(solution)/shard_map/all_to_all | solution.py:38
  84.8 6.6 %collective-permute-start = (bf16[16,4,16,1536]{3,2,1,0:T(8,128)(2,1)S(1)}, bf16[16,4,16,1536]{3,2,1,0:T(8,128)(2,1)}, u32[]{:S(2)}, u32[]{:S(2)}) collective-permute-start(bf16[16,4,16,1536]{3,2,1,0:T(8,128)(2,1)S(1)} %all_to_all.26), channel_id=1, source_target_pairs={{0,64},{64,0},{1,65},{65,1},{2,66},{66,2},{3,67},{67,3},{4,68},{68... | collective-permute-start | bytes 9437192 | tf_op jit(solution)/shard_map/ppermute | solution.py:279
  91.4 1.3 broadcast_in_dim.16
  92.7 0.0 copy-start
  92.7 4.5 %all-to-all-start.3 = ((bf16[16,4,16,640]{3,2,1,0:T(8,128)(2,1)}), bf16[16,4,16,640]{3,2,1,0:T(8,128)(2,1)}, u32[]{:S(2)}, u32[]{:S(2)}) async-start(bf16[16,4,16,640]{3,2,1,0:T(8,128)(2,1)} %broadcast_in_dim.16), calls=%async_computation.3 | async-start | bytes 2621440 | tf_op jit(solution)/shard_map/all_to_all | solution.py:38
  97.2 0.1 pad_add_fusion.at_ref
  97.4 0.1 fusion.10
  97.5 0.8 pad_maximum_fusion
  98.3 1.1 reshape.35.second_rows_ref
  99.4 0.0 collective-permute-done
  99.5 0.0 copy-done
  99.5 0.0 copy-start.3
  99.5 0.7 copy-done.3
  100.2 8.5 %middle.1 = (bf16[1024,1024]{1,0:T(8,128)(2,1)S(1)}, bf16[1024,512]{1,0:T(8,128)(2,1)S(1)}, f32[16,512]{1,0:T(8,128)S(1)}, f32[16,512]{1,0:T(8,128)}, f32[16,102...) custom-call(s32[4]{0:T(128)S(1)} %pad_add_fusion.at_ref, bf16[2,2,4,4,16,1536]{5,4,3,2,1,0:T(8,128)(2,1)S(1)} %bitcast.9, ...), custom_call_target="tpu_custom_call" | custom-call | flops 6442450944 | bytes 12582912 | tf_op jit(solution)/shard_map/middle/pallas_call | solution.py:214
  108.7 0.0 copy-start.1
  108.7 0.6 copy-done.1
  109.3 0.0 copy-start.2
  109.3 0.6 copy-done.2
  110.0 0.0 copy-start.4
  110.0 1.3 copy-done.4
  111.3 1.0 copy-done.6
  112.3 5.1 %all-to-all-done.3 = bf16[16,4,16,640]{3,2,1,0:T(8,128)(2,1)} async-done(((bf16[16,4,16,640]{3,2,1,0:T(8,128)(2,1)}), bf16[16,4,16,640]{3,2,1,0:T(8,128)(2,1)}, u32[]{:S(2)}, u32[]{:S(2)}) %all-to-all-start.3) | async-done | bytes 1310752 | tf_op jit(solution)/shard_map/all_to_all | solution.py:38
  117.4 3.0 %collective-permute-start.1 = (bf16[16,4,16,640]{3,2,1,0:T(8,128)(2,1)}, bf16[16,4,16,640]{3,2,1,0:T(8,128)(2,1)S(1)}, u32[]{:S(2)}, u32[]{:S(2)}) collective-permute-start(bf16[16,4,16,640]{3,2,1,0:T(8,128)(2,1)} %all-to-all-done.3), channel_id=1, source_target_pairs={{0,64},{64,0},{1,65},{65,1},{2,66},{66,2},{3,67},{67,3},{4,68},{68... | collective-permute-start | bytes 3932168 | tf_op jit(solution)/shard_map/ppermute | solution.py:290
  120.4 0.7 broadcast_in_dim.17
  121.2 3.5 %all-to-all-start.4 = ((f32[8,16,512]{2,1,0:T(8,128)}), f32[8,16,512]{2,1,0:T(8,128)S(1)}, u32[]{:S(2)}, u32[]{:S(2)}) async-start(f32[8,16,512]{2,1,0:T(8,128)} %broadcast_in_dim.17), calls=%async_computation.4 | async-start | bytes 524288 | tf_op jit(solution)/shard_map/all_to_all | solution.py:38
  124.7 1.3 constant_dynamic-slice_fusion
  126.0 1.3 multiply_add_fusion.1
  127.4 0.0 collective-permute-done.1
  127.4 1.6 %copy-done.5 = bf16[1024,1024]{1,0:T(8,128)(2,1)S(1)} copy-done((bf16[1024,1024]{1,0:T(8,128)(2,1)S(1)}, bf16[1024,1024]{1,0:T(8,128)(2,1)}, u32[]{:S(2)}) %copy-start.5) | copy-done | bytes 2097176
  129.0 1.2 copy-done.7
  130.2 12.7 %left_refresh.1 = f32[16,1024]{1,0:T(8,128)S(1)} custom-call(s32[1]{0:T(128)} %bitcast.2.first_ref, bf16[2,2,4,4,16,640]{5,4,3,2,1,0:T(8,128)(2,1)} %bitcast.7.mine_ref, bf16[2,2,4,4,16,640]{5,4,3,2,1,0:T(8,128)(2,1)S(1)} %bitcast.10, bf16[1024,512]{1,0:T(8,128)(2,1)S(1)} %copy-done.7, bf16[1024,1024]{1,0:T(8,128)(2,1)S(1)} %copy-done.5), custom_call_target="tpu_custom_call" | custom-call | flops 10737418240 | bytes 8388608 | tf_op jit(solution)/shard_map/left_refresh/pallas_call | solution.py:105
  142.9 0.0 all-to-all-done.4
  143.0 0.6 maximum_select_fusion
  143.6 0.0 copy-done.8
  143.6 0.6 multiply_subtract_fusion
  (20 shorter events, 0.2 us)
Async XLA Ops:
  2.1 24.0 %all-to-all-start = ((f32[8,16,512]{2,1,0:T(8,128)}), f32[8,16,512]{2,1,0:T(8,128)S(1)}, u32[]{:S(2)}, u32[]{:S(2)}) async-start(f32[8,16,512]{2,1,0:T(8,128)} %broadcast_in_dim.13), calls=%async_computation | async-start | bytes 524288 | tf_op jit(solution)/shard_map/all_to_all | solution.py:38
  84.8 14.7 %collective-permute-start = (bf16[16,4,16,1536]{3,2,1,0:T(8,128)(2,1)S(1)}, bf16[16,4,16,1536]{3,2,1,0:T(8,128)(2,1)}, u32[]{:S(2)}, u32[]{:S(2)}) collective-permute-start(bf16[16,4,16,1536]{3,2,1,0:T(8,128)(2,1)S(1)} %all_to_all.26), channel_id=1, source_target_pairs={{0,64},{64,0},{1,65},{65,1},{2,66},{66,2},{3,67},{67,3},{4,68},{68... | collective-permute-start | bytes 9437192 | tf_op jit(solution)/shard_map/ppermute | solution.py:279
  92.7 6.8 %copy-start = (f32[16,1024]{1,0:T(8,128)S(1)}, f32[16,1024]{1,0:T(8,128)}, u32[]{:S(2)}) copy-start(f32[16,1024]{1,0:T(8,128)} %left_gram_ref.1) | copy-start | bytes 196612
  92.7 24.7 %all-to-all-start.3 = ((bf16[16,4,16,640]{3,2,1,0:T(8,128)(2,1)}), bf16[16,4,16,640]{3,2,1,0:T(8,128)(2,1)}, u32[]{:S(2)}, u32[]{:S(2)}) async-start(bf16[16,4,16,640]{3,2,1,0:T(8,128)(2,1)} %broadcast_in_dim.16), calls=%async_computation.3 | async-start | bytes 2621440 | tf_op jit(solution)/shard_map/all_to_all | solution.py:38
  99.5 0.8 copy-start.3
  108.7 0.6 copy-start.1
  109.3 0.6 copy-start.2
  110.0 1.3 copy-start.4
  111.3 1.0 copy-start.6
  117.4 10.0 %collective-permute-start.1 = (bf16[16,4,16,640]{3,2,1,0:T(8,128)(2,1)}, bf16[16,4,16,640]{3,2,1,0:T(8,128)(2,1)S(1)}, u32[]{:S(2)}, u32[]{:S(2)}) collective-permute-start(bf16[16,4,16,640]{3,2,1,0:T(8,128)(2,1)} %all-to-all-done.3), channel_id=1, source_target_pairs={{0,64},{64,0},{1,65},{65,1},{2,66},{66,2},{3,67},{67,3},{4,68},{68... | collective-permute-start | bytes 3932168 | tf_op jit(solution)/shard_map/ppermute | solution.py:290
  121.2 21.8 %all-to-all-start.4 = ((f32[8,16,512]{2,1,0:T(8,128)}), f32[8,16,512]{2,1,0:T(8,128)S(1)}, u32[]{:S(2)}, u32[]{:S(2)}) async-start(f32[8,16,512]{2,1,0:T(8,128)} %broadcast_in_dim.17), calls=%async_computation.4 | async-start | bytes 524288 | tf_op jit(solution)/shard_map/all_to_all | solution.py:38
  127.4 1.6 %copy-start.5 = (bf16[1024,1024]{1,0:T(8,128)(2,1)S(1)}, bf16[1024,1024]{1,0:T(8,128)(2,1)}, u32[]{:S(2)}) copy-start(bf16[1024,1024]{1,0:T(8,128)(2,1)} %copy-done.4) | copy-start | bytes 6291460
  129.0 1.2 copy-start.7
  130.2 13.4 %copy-start.8 = (f32[16,512]{1,0:T(8,128)S(1)}, f32[16,512]{1,0:T(8,128)}, u32[]{:S(2)}) copy-start(f32[16,512]{1,0:T(8,128)} %param.9) | copy-start | bytes 98308

commit v4 on v3

--- a/solution.py
+++ b/solution.py
@@ -1,5 +1,8 @@
+import itertools
+
 import jax
 import jax.numpy as jnp
+import numpy as np
 from jax import lax
 from jax.experimental import pallas as pl
 from jax.experimental.pallas import tpu as pltpu
@@ -15,12 +18,13 @@
 STEP_SIZE = 0.02
 START_SCALE = 0.75
 
-AXES = ("zhi", "core", "zlo", "yhi", "ylo", "x")
-CUT = (4, 2, 2, 4, 2, 4)
+AXES = ("zhi", "core", "zlo", "yhi", "ylo", "xhi", "xlo")
+CUT = (4, 2, 2, 4, 2, 2, 2)
 GRP = ("zhi", "core")
-SHARD = ("zlo", "yhi", "ylo", "x")
-NEAR = ("zlo", "ylo", "x")
-NZ, NF, NY, NX = CUT[2:]
+SHARD = ("zlo", "yhi", "ylo", "xhi", "xlo")
+NZ, NF, NY, NXF, NXN = CUT[2:]
+NX = NXF * NXN
+NEAR = (NZ, NY, NXN)
 bf16 = jnp.bfloat16
 f32 = jnp.float32
 
@@ -33,9 +37,25 @@
     return lax.dot_general(a, b, (((ca,), (cb,)), ((), ())), preferred_element_type=f32)
 
 
-def gather(value, axes, size):
+def cubes():
+    groups = []
+    deep, high, wide = CUT[0] * NZ, NF * NY, NX
+    for core in range(CUT[1]):
+        for corner in itertools.product(range(0, deep, 2), range(0, high, 2), range(0, wide, 2)):
+            group = {}
+            for step in itertools.product(range(2), repeat=3):
+                z, y, x = (
+                    (a + core + b) % n for a, b, n in zip(corner, step, (deep, high, wide))
+                )
+                place = (z // NZ, core, z % NZ, y // NY, y % NY, x // NXN, x % NXN)
+                group[z % NZ, y % NY, x % NXN] = int(np.ravel_multi_index(place, CUT))
+            groups.append([group[k] for k in sorted(group)])
+    return groups
+
+
+def gather(value, axes, size, groups=None):
     copies = jnp.broadcast_to(value[None], (size,) + value.shape)
-    return lax.all_to_all(copies, axes, 0, 0)
+    return lax.all_to_all(copies, axes, 0, 0, axis_index_groups=groups)
 
 
 def pair(value):
@@ -80,7 +100,8 @@
             at = pl.ds(j * BLOCK, BLOCK)
             pieces = []
             for near in range(NY * NX):
-                place = (zlo, near // NX, near % NX, far, slice(None), at)
+                y, x = near // NX, near % NX
+                place = (zlo, y, x % NXN, x // NXN, far, slice(None), at)
                 pieces.append(mine_ref[place].astype(f32) + other_ref[place].astype(f32))
             block = GRAM_DECAY * jnp.concatenate(pieces, axis=0)
             gram[r * BLOCK : (r + 1) * BLOCK, c * BLOCK : (c + 1) * BLOCK] = block
@@ -137,7 +158,7 @@
             for y in range(NY):
                 for x in range(NX):
                     def lanes(at, n):
-                        place = (zlo, y, x, far, slice(None), pl.ds(at, n))
+                        place = (zlo, y, x % NXN, x // NXN, far, slice(None), pl.ds(at, n))
                         return mine_ref[place], other_ref[place]
 
                     to = pl.ds(spot * rows, rows)
@@ -166,8 +187,9 @@
 
     n = second_rows_ref.shape[0]
     q = lax.broadcasted_iota(jnp.int32, (1, n), 1)
-    r, far, near = q % share, (q // share) % NF, q // (share * NF)
-    wanted = ((near // (NY * NX) * NF + far) * (NY * NX) + near % (NY * NX)) * rows + group * share + r
+    r, far, q = q % share, (q // share) % NF, q // (share * NF)
+    xhi, xlo, y, z = q % NXF, (q // NXF) % NXN, (q // NX) % NY, q // (NX * NY)
+    wanted = (((z * NF + far) * NY + y) * NX + xhi * NXN + xlo) * rows + group * share + r
     column = (lax.broadcasted_iota(jnp.int32, (deep, n), 0) + core * half) % deep
     pick = jnp.where(column == wanted, 1.0, 0.0).astype(bf16)
     q = lax.broadcasted_iota(jnp.int32, (1, n), 1)
@@ -237,7 +259,8 @@
     n_shard = NZ * NF * NY * NX
     deep = n_shard * rows
     core = lax.axis_index("core")
-    group = lax.axis_index(GRP)
+    cube = (lax.axis_index("zhi") + CUT[0] - core * (1 - lax.axis_index("zlo"))) % CUT[0]
+    group = cube * CUT[1] + core
     shard = lax.axis_index(SHARD)
     row_first = shard * rows
     right_first = shard * right_rows
@@ -271,13 +294,13 @@
         axis=1,
     )
     cut = payload.shape[1] - SENT * BLOCK
-    payload = gather(payload, "yhi", NF)
-    near = NZ * NY * NX
-    parted = lambda v: v.reshape((NZ, NY, NX) + v.shape[1:])
+    payload = gather(gather(payload, "yhi", NF), "xhi", NXF)
+    near, groups = NZ * NY * NXN, cubes()
+    parted = lambda v: v.reshape(NEAR + v.shape[1:])
     swap = [(0, 1), (1, 0)]
-    early = gather(payload[..., :cut], NEAR, near)
+    early = gather(payload[..., :cut], AXES, near, groups)
     early_other = lax.ppermute(early, "core", swap)
-    late = gather(payload[..., cut:], NEAR, near)
+    late = gather(payload[..., cut:], AXES, near, groups)
 
     second_parts = early[..., cut - 128 :].astype(f32)
     second_parts = second_parts[..., : rows // 2, :] + second_parts[..., rows // 2 :, :]

time: 146 us -> 136 us (0.932)
  waiting for transfers between devices: 13.5 us -> 8.3 us
  starting transfers between devices: 29.5 us -> 25.8 us
  blocking collectives: 56 us -> 54.2 us
    all_to_all x3, waiting for transfers between devices: 13.5 us -> 8.29 us  [gather(): return lax.all_to_all(copies, axes, 0, 0, axis_index_groups=groups)]
    ppermute x1, starting transfers between devices: 6.6 us -> 3.88 us  [local(): early_other = lax.ppermute(early, 'core', swap)]
    all_to_all x2 -> x3, blocking collectives: 56 us -> 54.2 us  [gather(): return lax.all_to_all(copies, axes, 0, 0, axis_index_groups=groups)]
    broadcast_in_dim x5 -> x6, local copies, waits for them, and re-layouts: 3.88 us -> 3.93 us  [gather(): copies = jnp.broadcast_to(value[None], (size,) + value.shape)]
  transfers between devices with their start and end apart: 5 -> 5, of which waited for: 2 -> 1; matrix products, arithmetic and copies ran while one was open for 7% -> 8% of each run, Pallas kernels for 15% -> 16%
where the time goes in v4:
time: 136 us; the launch traced here: 134 us
  blocking collectives  54.2 us (40%)
  starting transfers between devices  25.8 us (19%)
  Pallas kernels  21.3 us (16%)
  local copies, waits for them, and re-layouts  14.5 us (11%)
  other arithmetic  8.84 us (6%)
  waiting for transfers between devices  8.3 us (6%)
    all_to_all x3, blocking collectives, gather(): return lax.all_to_all(copies, axes, 0, 0, axis_index_groups=groups)  54.2 us
    all_to_all x3, starting transfers between devices, gather(): return lax.all_to_all(copies, axes, 0, 0, axis_index_groups=groups)  20 us
    pallas_call x1, Pallas kernels, left_call(): pl.pallas_call(left_kernel, out_shape=jax.ShapeDtypeStruct((rows, deep),...  12.7 us
    pallas_call x1, Pallas kernels, mid_call(): pl.pallas_call(mid_kernel, out_shape=[jax.ShapeDtypeStruct(*v) for v in s...  8.52 us
    all_to_all x3, waiting for transfers between devices, gather(): return lax.all_to_all(copies, axes, 0, 0, axis_index_groups=groups)  8.29 us
    unnamed x19, local copies, waits for them, and re-layouts  7.13 us
    broadcast_in_dim x6, local copies, waits for them, and re-layouts, gather(): copies = jnp.broadcast_to(value[None], (size,) + value.shape)  3.93 us
    ppermute x1, starting transfers between devices, local(): early_other = lax.ppermute(early, 'core', swap)  3.88 us
  transfers between devices with their start and end apart: 5, of which 1 were waited for; matrix products, arithmetic and copies ran while one was open for 8% of the time, Pallas kernels for 16%

profile of v4, /device:TPU:1, one launch (start us, length us, event | category | flops | bytes accessed | tf_op | source)
XLA Modules:
  0.0 133.7 jit_solution(12055934293814754905)
XLA Ops:
  0.6 1.5 %broadcast_in_dim.15 = f32[8,16,512]{2,1,0:T(8,128)} broadcast(f32[16,512]{1,0:T(8,128)} %bitcast.11), dimensions={1,2} | broadcast | bytes 294912 | tf_op jit(solution)/shard_map/broadcast_in_dim | solution.py:57
  2.1 11.8 %all-to-all-start = ((f32[8,16,512]{2,1,0:T(8,128)}), f32[8,16,512]{2,1,0:T(8,128)S(1)}, u32[]{:S(2)}, u32[]{:S(2)}) async-start(f32[8,16,512]{2,1,0:T(8,128)} %broadcast_in_dim.15), calls=%async_computation | async-start | bytes 524288 | tf_op jit(solution)/shard_map/all_to_all | solution.py:58
  13.9 0.7 convert_element_type.36
  14.6 0.7 fusion.8
  15.4 0.7 fusion.9
  16.1 0.8 convert_element_type.33.left_rows_ref
  17.0 0.8 slice.40
  17.7 0.1 concatenate.23
  17.8 8.3 %all-to-all-done = f32[8,16,512]{2,1,0:T(8,128)S(1)} async-done(((f32[8,16,512]{2,1,0:T(8,128)}), f32[8,16,512]{2,1,0:T(8,128)S(1)}, u32[]{:S(2)}, u32[]{:S(2)}) %all-to-all-start) | async-done | bytes 262176 | tf_op jit(solution)/shard_map/all_to_all | solution.py:58
  26.1 1.4 %fusion.6 = (bf16[16,2176]{1,0:T(8,128)(2,1)S(1)}, f32[16,512]{1,0:T(8,128)}) fusion(bf16[16,2176]{1,0:T(8,128)(2,1)S(1)} %fusion.7, f32[16,512]{1,0:T(8,128)S(1)} %reduce_sum.18, pred[]{:T(512)S(6)} %eq.7, f32[16,512]{1,0:T(8,128)} %param.10), kind=kLoop, calls=%fused_computation.19 | loop fusion | flops 57344 | bytes 114689
  27.5 0.8 fusion.3
  28.4 15.9 %all_to_all.30 = bf16[4,16,2176]{2,1,0:T(8,128)(2,1)S(1)} all-to-all(bf16[4,16,2176]{2,1,0:T(8,128)(2,1)S(1)} %broadcast_in_dim.16), channel_id=1, replica_groups=mesh['zhi'=4,'core'=2,'zlo'=2,'yhi'=4,'ylo'=2,'xhi'=2,'xlo'=2] {'yhi'}, dimensions={0} | all-to-all | bytes 557056 | tf_op jit(solution)/shard_map/all_to_all | solution.py:58
  44.3 10.9 %all_to_all.31 = bf16[2,4,16,2176]{3,2,1,0:T(8,128)(2,1)S(1)} all-to-all(bf16[2,4,16,2176]{3,2,1,0:T(8,128)(2,1)S(1)} %broadcast_in_dim.17), channel_id=1, replica_groups=mesh['zhi'=4,'core'=2,'zlo'=2,'yhi'=4,'ylo'=2,'xhi'=2,'xlo'=2] {'xhi'}, dimensions={0} | all-to-all | bytes 1114112 | tf_op jit(solution)/shard_map/all_to_all | solution.py:58
  55.3 0.4 broadcast_in_dim.18
  55.7 27.4 %all_to_all.32 = bf16[8,2,4,16,1536]{4,3,2,1,0:T(8,128)(2,1)S(1)} all-to-all(bf16[8,2,4,16,1536]{4,3,2,1,0:T(8,128)(2,1)S(1)} %broadcast_in_dim.18), channel_id=1, replica_groups={{0,1,4,5,32,33,36,37},{2,3,6,7,34,35,38,39},{8,9,12,13,40,41,44,45},{10..., dimensions={0} | all-to-all | bytes 6291456 | tf_op jit(solution)/shard_map/all_to_all | solution.py:58
  83.0 3.9 %collective-permute-start = (bf16[8,2,4,16,1536]{4,3,2,1,0:T(8,128)(2,1)S(1)}, bf16[8,2,4,16,1536]{4,3,2,1,0:T(8,128)(2,1)}, u32[]{:S(2)}, u32[]{:S(2)}) collective-permute-start(bf16[8,2,4,16,1536]{4,3,2,1,0:T(8,128)(2,1)S(1)} %all_to_all.32), channel_id=1, source_target_pairs={{0,64},{64,0},{1,65},{65,1},{2,66},{66,2},{3,67},{67,3},{4,68},{68... | collective-permute-start | bytes 9437192 | tf_op jit(solution)/shard_map/ppermute | solution.py:302
  86.9 1.3 broadcast_in_dim.19
  88.2 0.0 copy-start
  88.2 4.4 %all-to-all-start.4 = ((bf16[8,2,4,16,640]{4,3,2,1,0:T(8,128)(2,1)}), bf16[8,2,4,16,640]{4,3,2,1,0:T(8,128)(2,1)}, u32[]{:S(2)}, u32[]{:S(2)}) async-start(bf16[8,2,4,16,640]{4,3,2,1,0:T(8,128)(2,1)} %broadcast_in_dim.19), calls=%async_computation.4 | async-start | bytes 2621440 | tf_op jit(solution)/shard_map/all_to_all | solution.py:58
  92.6 0.1 pad_add_fusion.at_ref
  92.8 0.1 fusion.10
  92.9 0.8 pad_maximum_fusion
  93.7 1.1 reshape.36.second_rows_ref
  94.9 0.0 collective-permute-done
  94.9 0.0 copy-done
  94.9 0.0 copy-start.3
  94.9 0.7 copy-done.3
  95.6 8.5 %middle.1 = (bf16[1024,1024]{1,0:T(8,128)(2,1)S(1)}, bf16[1024,512]{1,0:T(8,128)(2,1)S(1)}, f32[16,512]{1,0:T(8,128)S(1)}, f32[16,512]{1,0:T(8,128)}, f32[16,102...) custom-call(s32[4]{0:T(128)S(1)} %pad_add_fusion.at_ref, bf16[2,2,2,2,4,16,1536]{6,5,4,3,2,1,0:T(8,128)(2,1)S(1)} %bitcast.9, ...), custom_call_target="tpu_custom_call" | custom-call | flops 6442450944 | bytes 12582912 | tf_op jit(solution)/shard_map/middle/pallas_call | solution.py:236
  104.2 0.0 copy-start.1
  104.2 0.6 copy-done.1
  104.8 0.0 copy-start.2
  104.8 0.6 copy-done.2
  105.4 1.3 %copy-done.4 = bf16[1024,1024]{1,0:T(8,128)(2,1)} copy-done((bf16[1024,1024]{1,0:T(8,128)(2,1)}, bf16[1024,1024]{1,0:T(8,128)(2,1)S(1)}, u32[]{:S(2)}) %copy-start.4) | copy-done | bytes 2097176
  106.8 1.0 copy-done.6
  107.7 0.0 all-to-all-done.4
  107.7 1.9 %collective-permute-start.1 = (bf16[8,2,4,16,640]{4,3,2,1,0:T(8,128)(2,1)}, bf16[8,2,4,16,640]{4,3,2,1,0:T(8,128)(2,1)S(1)}, u32[]{:S(2)}, u32[]{:S(2)}) collective-permute-start(bf16[8,2,4,16,640]{4,3,2,1,0:T(8,128)(2,1)} %all-to-all-done.4), channel_id=1, source_target_pairs={{0,64},{64,0},{1,65},{65,1},{2,66},{66,2},{3,67},{67,3},{4,68},{68... | collective-permute-start | bytes 3932168 | tf_op jit(solution)/shard_map/ppermute | solution.py:313
  109.7 0.7 broadcast_in_dim.20
  110.4 3.8 %all-to-all-start.5 = ((f32[8,16,512]{2,1,0:T(8,128)}), f32[8,16,512]{2,1,0:T(8,128)S(1)}, u32[]{:S(2)}, u32[]{:S(2)}) async-start(f32[8,16,512]{2,1,0:T(8,128)} %broadcast_in_dim.20), calls=%async_computation.5 | async-start | bytes 524288 | tf_op jit(solution)/shard_map/all_to_all | solution.py:58
  114.2 1.3 constant_dynamic-slice_fusion
  115.5 1.3 %multiply_add_fusion.1 = f32[8,512]{1,0:T(8,128)} fusion(f32[16,512]{1,0:T(8,128)} %copy-done.1, s32[]{:T(128)S(6)} %select_n.91, f32[8,512]{1,0:T(8,128)} %param.14), kind=kLoop, calls=%fused_computation.22 | loop fusion | flops 12288 | bytes 49156 | tf_op jit(solution)/shard_map/add | solution.py:316
  116.9 0.0 collective-permute-done.1
  116.9 1.6 %copy-done.5 = bf16[1024,1024]{1,0:T(8,128)(2,1)S(1)} copy-done((bf16[1024,1024]{1,0:T(8,128)(2,1)S(1)}, bf16[1024,1024]{1,0:T(8,128)(2,1)}, u32[]{:S(2)}) %copy-start.5) | copy-done | bytes 2097176
  118.5 1.2 copy-done.7
  119.7 12.7 %left_refresh.1 = f32[16,1024]{1,0:T(8,128)S(1)} custom-call(s32[1]{0:T(128)} %bitcast.2.first_ref, bf16[2,2,2,2,4,16,640]{6,5,4,3,2,1,0:T(8,128)(2,1)} %bitcast.7.mine_ref, bf16[2,2,2,2,4,16,640]{6,5,4,3,2,1,0:T(8,128)(2,1)S(1)} %bitcast.10, bf16[1024,512]{1,0:T(8,128)(2,1)S(1)} %copy-done.7, bf16[1024,1024]{1,0:T(8,128)(2,1)S(1)} %copy-done.5), custom_call_target="tpu_custom_call" | custom-call | flops 10737418240 | bytes 8388608 | tf_op jit(solution)/shard_map/left_refresh/pallas_call | solution.py:126
  132.4 0.0 all-to-all-done.5
  132.5 0.6 maximum_select_fusion
  133.1 0.0 copy-done.8
  133.1 0.6 multiply_subtract_fusion
  (22 shorter events, 0.3 us)
Async XLA Ops:
  2.1 24.0 %all-to-all-start = ((f32[8,16,512]{2,1,0:T(8,128)}), f32[8,16,512]{2,1,0:T(8,128)S(1)}, u32[]{:S(2)}, u32[]{:S(2)}) async-start(f32[8,16,512]{2,1,0:T(8,128)} %broadcast_in_dim.15), calls=%async_computation | async-start | bytes 524288 | tf_op jit(solution)/shard_map/all_to_all | solution.py:58
  83.0 11.8 %collective-permute-start = (bf16[8,2,4,16,1536]{4,3,2,1,0:T(8,128)(2,1)S(1)}, bf16[8,2,4,16,1536]{4,3,2,1,0:T(8,128)(2,1)}, u32[]{:S(2)}, u32[]{:S(2)}) collective-permute-start(bf16[8,2,4,16,1536]{4,3,2,1,0:T(8,128)(2,1)S(1)} %all_to_all.32), channel_id=1, source_target_pairs={{0,64},{64,0},{1,65},{65,1},{2,66},{66,2},{3,67},{67,3},{4,68},{68... | collective-permute-start | bytes 9437192 | tf_op jit(solution)/shard_map/ppermute | solution.py:302
  88.2 6.6 %copy-start = (f32[16,1024]{1,0:T(8,128)S(1)}, f32[16,1024]{1,0:T(8,128)}, u32[]{:S(2)}) copy-start(f32[16,1024]{1,0:T(8,128)} %left_gram_ref.1) | copy-start | bytes 196612
  88.2 19.5 %all-to-all-start.4 = ((bf16[8,2,4,16,640]{4,3,2,1,0:T(8,128)(2,1)}), bf16[8,2,4,16,640]{4,3,2,1,0:T(8,128)(2,1)}, u32[]{:S(2)}, u32[]{:S(2)}) async-start(bf16[8,2,4,16,640]{4,3,2,1,0:T(8,128)(2,1)} %broadcast_in_dim.19), calls=%async_computation.4 | async-start | bytes 2621440 | tf_op jit(solution)/shard_map/all_to_all | solution.py:58
  94.9 0.8 copy-start.3
  104.2 0.6 copy-start.1
  104.8 0.6 copy-start.2
  105.4 1.3 %copy-start.4 = (bf16[1024,1024]{1,0:T(8,128)(2,1)}, bf16[1024,1024]{1,0:T(8,128)(2,1)S(1)}, u32[]{:S(2)}) copy-start(bf16[1024,1024]{1,0:T(8,128)(2,1)S(1)} %get-tuple-element.34.basis_ref) | copy-start | bytes 6291460
  106.7 1.0 copy-start.6
  107.7 9.1 %collective-permute-start.1 = (bf16[8,2,4,16,640]{4,3,2,1,0:T(8,128)(2,1)}, bf16[8,2,4,16,640]{4,3,2,1,0:T(8,128)(2,1)S(1)}, u32[]{:S(2)}, u32[]{:S(2)}) collective-permute-start(bf16[8,2,4,16,640]{4,3,2,1,0:T(8,128)(2,1)} %all-to-all-done.4), channel_id=1, source_target_pairs={{0,64},{64,0},{1,65},{65,1},{2,66},{66,2},{3,67},{67,3},{4,68},{68... | collective-permute-start | bytes 3932168 | tf_op jit(solution)/shard_map/ppermute | solution.py:313
  110.4 22.0 %all-to-all-start.5 = ((f32[8,16,512]{2,1,0:T(8,128)}), f32[8,16,512]{2,1,0:T(8,128)S(1)}, u32[]{:S(2)}, u32[]{:S(2)}) async-start(f32[8,16,512]{2,1,0:T(8,128)} %broadcast_in_dim.20), calls=%async_computation.5 | async-start | bytes 524288 | tf_op jit(solution)/shard_map/all_to_all | solution.py:58
  116.9 1.6 %copy-start.5 = (bf16[1024,1024]{1,0:T(8,128)(2,1)S(1)}, bf16[1024,1024]{1,0:T(8,128)(2,1)}, u32[]{:S(2)}) copy-start(bf16[1024,1024]{1,0:T(8,128)(2,1)} %copy-done.4) | copy-start | bytes 6291460
  118.5 1.2 copy-start.7
  119.7 13.4 %copy-start.8 = (f32[16,512]{1,0:T(8,128)S(1)}, f32[16,512]{1,0:T(8,128)}, u32[]{:S(2)}) copy-start(f32[16,512]{1,0:T(8,128)} %param.9) | copy-start | bytes 98308

commit v5 on v4

--- a/solution.py
+++ b/solution.py
@@ -118,6 +118,8 @@
         return mm(high, basis, 1, 0) + mm(low, basis, 1, 0)
 
     refresh(power_tile, gram.shape[0] // tile, tile, first_ref[0], rows, power, start, current, out_ref)
+    result, half = out_ref[...], gram.shape[0] // 2
+    out_ref[...] = jnp.where(first_ref[1] == 0, result, jnp.concatenate([result[:, half:], result[:, :half]], axis=1))
 
 
 def left_call(first, mine, other, grad, basis, rows):
@@ -134,23 +136,23 @@
             pltpu.VMEM((deep, deep), bf16),
             pltpu.VMEM((deep, deep), bf16),
         ],
-        compiler_params=pltpu.CompilerParams(vmem_limit_bytes=40 << 20),
+        compiler_params=pltpu.CompilerParams(vmem_limit_bytes=20 << 20),
         cost_estimate=pl.CostEstimate(flops=10 * deep**3, transcendentals=deep, bytes_accessed=8 * deep**2),
         name="left_refresh",
     )(first, mine, other, grad, basis)
 
 
 def mid_kernel(
-    at_ref, mine_ref, other_ref, second_rows_ref, second_ref, left_rows_ref, left_gram_ref,
-    basis_ref, grad_ref, update_ref, second_new_ref, left_new_ref, right_term_ref, right_out_ref,
-    mom, right, rgram, power, start, current,
+    at_ref, mine_ref, other_ref, second_ref, left_rows_ref, left_gram_ref, right_gram_ref,
+    basis_ref, grad_ref, update_ref, second_new_ref, left_new_ref, right_new_ref, right_out_ref,
+    mom, right, rgram, second_rows, term, power, start, current,
 ):
-    core, group, row_first, right_first = (at_ref[i] for i in range(4))
+    right_pair, right_odd, group, row_first, core = (at_ref[i] for i in range(5))
     first = core == 0
     rows, width = second_ref.shape
     deep = basis_ref.shape[0]
     half = deep // 2
-    share = second_rows_ref.shape[0] // (deep // rows)
+    share = second_rows.shape[0] // (deep // rows)
     right_rows = rows // 2
     spot = 0
     for zlo in range(NZ):
@@ -181,15 +183,19 @@
                     for part in range(2):
                         of = slice(part * right_rows, (part + 1) * right_rows)
                         rgram[to, part * 2 * n : (part + 1) * 2 * n] = both[of]
+                    a, _ = lanes(half + width + 3 * n, n)
+                    a = a.astype(f32)
+                    both = a[:right_rows] + a[right_rows:]
+                    for part in range(4):
+                        of = slice(part * share, (part + 1) * share)
+                        second_rows[spot * share : (spot + 1) * share, part * n : (part + 1) * n] = both[of]
                     spot += 1
     basis, grad = basis_ref[...], grad_ref[...]
     rbasis = right[...].astype(bf16)
 
-    n = second_rows_ref.shape[0]
+    n = second_rows.shape[0]
     q = lax.broadcasted_iota(jnp.int32, (1, n), 1)
-    r, far, q = q % share, (q // share) % NF, q // (share * NF)
-    xhi, xlo, y, z = q % NXF, (q // NXF) % NXN, (q // NX) % NY, q // (NX * NY)
-    wanted = (((z * NF + far) * NY + y) * NX + xhi * NXN + xlo) * rows + group * share + r
+    wanted = q // share * rows + group * share + q % share
     column = (lax.broadcasted_iota(jnp.int32, (deep, n), 0) + core * half) % deep
     pick = jnp.where(column == wanted, 1.0, 0.0).astype(bf16)
     q = lax.broadcasted_iota(jnp.int32, (1, n), 1)
@@ -199,7 +205,7 @@
     rotated_grad = mm(mm(columns, grad, 0, 0).astype(bf16), rbasis, 1, 0)
     rotated_moment = mm(mm(columns, mom[...], 0, 0).astype(bf16), rbasis, 1, 0)
     own_grad = mm(mm(own_columns, grad, 0, 0).astype(bf16), rbasis, 1, 0)[:rows]
-    second_part = BETA_TWO * second_rows_ref[...] + (1.0 - BETA_TWO) * rotated_grad * rotated_grad
+    second_part = BETA_TWO * second_rows[...] + (1.0 - BETA_TWO) * rotated_grad * rotated_grad
     second_new_ref[...] = BETA_TWO * second_ref[...] + (1.0 - BETA_TWO) * own_grad * own_grad
     direction = (rotated_moment / (jnp.sqrt(second_part) + ADAM_EPS)).astype(bf16)
     returned = mm(direction, rbasis, 1, 1).astype(bf16)
@@ -211,8 +217,9 @@
     left_new_ref[...] = GRAM_DECAY * left_gram_ref[...] + (1.0 - GRAM_DECAY) * mm(own_grad, grad, 1, 1)
     q = lax.broadcasted_iota(jnp.int32, (width, BLOCK), 1)
     column = lax.broadcasted_iota(jnp.int32, (width, BLOCK), 0)
-    own = jnp.where((column == right_first + q) & (q < rows), 1.0, 0.0).astype(bf16)
-    right_term_ref[...] = mm(mm(grad, own, 1, 0).astype(bf16), grad, 0, 0)[:rows]
+    own = jnp.where((column == right_pair + right_odd + q) & (q < right_rows), 1.0, 0.0).astype(bf16)
+    own = mm(mm(grad, own, 1, 0).astype(bf16), grad, 0, 0)[:right_rows]
+    right_new_ref[...] = GRAM_DECAY * right_gram_ref[...] + (1.0 - GRAM_DECAY) * own
 
     tile = 256
 
@@ -222,16 +229,17 @@
         high, low = split(whole)
         return mm(high, rbasis, 1, 0) + mm(low, rbasis, 1, 0)
 
-    refresh(power_tile, width // tile, tile, right_first, rows, power, start, current, right_out_ref)
-
-
-def mid_call(at, mine, other, second_rows, second, left_rows, left_gram):
+    refresh(power_tile, width // tile, tile, right_pair, rows, power, start, current, term)
+    right_out_ref[...] = term[pl.ds(pl.multiple_of(right_odd, right_rows), right_rows), :]
+
+
+def mid_call(at, mine, other, second, left_rows, left_gram, right_gram):
     rows, deep = left_rows.shape
     width = second.shape[1]
     vmem = pl.BlockSpec(memory_space=pltpu.VMEM)
     shapes = [
         ((deep, deep), bf16), ((deep, width), bf16), ((rows, width), f32), ((rows, width), f32),
-        ((rows, deep), f32), ((rows, width), f32), ((rows, width), f32),
+        ((rows, deep), f32), (right_gram.shape, f32), (right_gram.shape, f32),
     ]
     return pl.pallas_call(
         mid_kernel,
@@ -242,14 +250,16 @@
             pltpu.VMEM((deep, width), bf16),
             pltpu.VMEM((width, width), f32),
             pltpu.VMEM((width, width), f32),
+            pltpu.VMEM((deep // (CUT[0] * CUT[1]), width), f32),
+            pltpu.VMEM((rows, width), f32),
             pltpu.VMEM((width, width), f32),
             pltpu.VMEM((width, width), bf16),
             pltpu.VMEM((width, width), bf16),
         ],
-        compiler_params=pltpu.CompilerParams(vmem_limit_bytes=40 << 20),
+        compiler_params=pltpu.CompilerParams(vmem_limit_bytes=20 << 20),
         cost_estimate=pl.CostEstimate(flops=6 * deep**3, transcendentals=width**2, bytes_accessed=12 * deep**2),
         name="middle",
-    )(at, mine, other, second_rows, second, left_rows, left_gram)
+    )(at, mine, other, second, left_rows, left_gram, right_gram)
 
 
 def local(gradients, weight, moment, second, left_gram, left_basis, right_gram, right_basis):
@@ -294,7 +304,8 @@
         axis=1,
     )
     cut = payload.shape[1] - SENT * BLOCK
-    payload = gather(gather(payload, "yhi", NF), "xhi", NXF)
+    payload = gather(payload, ("xhi", "yhi"), NXF * NF)
+    payload = payload.reshape((NXF, NF) + payload.shape[1:])
     near, groups = NZ * NY * NXN, cubes()
     parted = lambda v: v.reshape(NEAR + v.shape[1:])
     swap = [(0, 1), (1, 0)]
@@ -302,24 +313,16 @@
     early_other = lax.ppermute(early, "core", swap)
     late = gather(payload[..., cut:], AXES, near, groups)
 
-    second_parts = early[..., cut - 128 :].astype(f32)
-    second_parts = second_parts[..., : rows // 2, :] + second_parts[..., rows // 2 :, :]
-    second_rows = jnp.concatenate(jnp.split(second_parts, 4, axis=-2), axis=-1).reshape(-1, width)
-
-    at = jnp.stack([core, group, row_first, right_first // rows * rows]).astype(jnp.int32)
-    results = mid_call(at, parted(early), parted(early_other), second_rows, second, left_half, left_gram)
-    results, late = lax.optimization_barrier((results, late))
-    basis, grad, update, second_new, left_new, right_term, right_result = results
+    right_pair = right_first // rows * rows
+    at = jnp.stack([right_pair, right_first - right_pair, group, row_first, core]).astype(jnp.int32)
+    results = mid_call(at, parted(early), parted(early_other), second, left_half, left_gram, right_gram)
+    basis, grad, update, second_new, left_new, right_new, right_result = results
+    update, late = lax.optimization_barrier((update, late))
     late_other = lax.ppermute(late, "core", swap)
     updates = gather(update, GRP, n_grp)
-    own = lambda v: lax.dynamic_slice_in_dim(v, right_first % rows, right_rows, 0)
-    right_new = GRAM_DECAY * right_gram + (1.0 - GRAM_DECAY) * own(right_term)
-    right_result = own(right_result)
-    left_result = left_call(row_first[None], parted(late), parted(late_other), grad, basis, rows)
+    left_result = left_call(at[3:], parted(late), parted(late_other), grad, basis, rows)
     updates, left_result = lax.optimization_barrier((updates, left_result))
     weight_new = weight - STEP_SIZE * jnp.sum(updates, axis=0)
-    swapped = jnp.concatenate([left_result[:, half:], left_result[:, :half]], axis=1)
-    left_result = jnp.where(first, left_result, swapped)
     return (weight_new, moment_new, second_new, left_new, left_result, right_new, right_result)
 
 

time: 136 us -> 132 us (0.971)
  local copies, waits for them, and re-layouts: 14.5 us -> 9.99 us
  waiting for transfers between devices: 8.3 us -> 11.8 us
  other arithmetic: 8.84 us -> 5.97 us
  starting transfers between devices: 25.8 us -> 23.7 us
  blocking collectives: 54.2 us -> 55.6 us
    all_to_all x3, waiting for transfers between devices: 8.29 us -> 11.8 us  [gather(): return lax.all_to_all(copies, axes, 0, 0, axis_index_groups=groups)]
    unnamed x19 -> x17, local copies, waits for them, and re-layouts: 7.13 us -> 5.14 us
    ppermute x1, starting transfers between devices: 3.88 us -> 1.91 us  [local(): early_other = lax.ppermute(early, 'core', swap)]
    all_to_all x3 -> x2, blocking collectives: 54.2 us -> 55.6 us  [gather(): return lax.all_to_all(copies, axes, 0, 0, axis_index_groups=groups)]
    add x2 -> x0, other arithmetic: 1.37 us -> none  [the longest x1 1.34 us: local(): right_new = GRAM_DECAY * right_gram + (1.0 - GRAM_DECAY) * own(right_term)]
    broadcast_in_dim x6 -> x5, local copies, waits for them, and re-layouts: 3.93 us -> 3.89 us  [gather(): copies = jnp.broadcast_to(value[None], (size,) + value.shape)]
  transfers between devices with their start and end apart: 5 -> 5, of which waited for: 1 -> 3; matrix products, arithmetic and copies ran while one was open for 8% -> 5% of each run, Pallas kernels for 16% -> 17%
where the time goes in v5:
time: 132 us; the launch traced here: 130 us
  blocking collectives  55.6 us (42%)
  starting transfers between devices  23.7 us (18%)
  Pallas kernels  22.5 us (17%)
  waiting for transfers between devices  11.8 us (9%)
  local copies, waits for them, and re-layouts  9.99 us (8%)
  other arithmetic  5.97 us (5%)
    all_to_all x2, blocking collectives, gather(): return lax.all_to_all(copies, axes, 0, 0, axis_index_groups=groups)  55.6 us
    all_to_all x3, starting transfers between devices, gather(): return lax.all_to_all(copies, axes, 0, 0, axis_index_groups=groups)  19.9 us
    pallas_call x1, Pallas kernels, left_call(): pl.pallas_call(left_kernel, out_shape=jax.ShapeDtypeStruct((rows, deep),...  13.4 us
    all_to_all x3, waiting for transfers between devices, gather(): return lax.all_to_all(copies, axes, 0, 0, axis_index_groups=groups)  11.8 us
    pallas_call x1, Pallas kernels, mid_call(): pl.pallas_call(mid_kernel, out_shape=[jax.ShapeDtypeStruct(*v) for v in s...  9.17 us
    unnamed x17, local copies, waits for them, and re-layouts  5.14 us
    broadcast_in_dim x5, local copies, waits for them, and re-layouts, gather(): copies = jnp.broadcast_to(value[None], (size,) + value.shape)  3.89 us
  transfers between devices with their start and end apart: 5, of which 3 were waited for; matrix products, arithmetic and copies ran while one was open for 5% of the time, Pallas kernels for 17%

profile of v5, /device:TPU:1, one launch (start us, length us, event | category | flops | bytes accessed | tf_op | source)
XLA Modules:
  0.0 130.4 jit_solution(3058504644484867252)
XLA Ops:
  0.6 1.5 %broadcast_in_dim.13 = f32[8,16,512]{2,1,0:T(8,128)} broadcast(f32[16,512]{1,0:T(8,128)} %bitcast.15), dimensions={1,2} | broadcast | bytes 294912 | tf_op jit(solution)/shard_map/broadcast_in_dim | solution.py:57
  2.1 11.8 %all-to-all-start = ((f32[8,16,512]{2,1,0:T(8,128)}), f32[8,16,512]{2,1,0:T(8,128)S(1)}, u32[]{:S(2)}, u32[]{:S(2)}) async-start(f32[8,16,512]{2,1,0:T(8,128)} %broadcast_in_dim.13), calls=%async_computation | async-start | bytes 524288 | tf_op jit(solution)/shard_map/all_to_all | solution.py:58
  13.9 0.7 convert_element_type.33
  14.7 0.7 fusion.8
  15.4 0.7 fusion.9
  16.1 0.8 convert_element_type.30.left_rows_ref
  17.0 0.8 slice.27
  17.7 0.1 concatenate.18
  17.8 8.3 %all-to-all-done = f32[8,16,512]{2,1,0:T(8,128)S(1)} async-done(((f32[8,16,512]{2,1,0:T(8,128)}), f32[8,16,512]{2,1,0:T(8,128)S(1)}, u32[]{:S(2)}, u32[]{:S(2)}) %all-to-all-start) | async-done | bytes 262176 | tf_op jit(solution)/shard_map/all_to_all | solution.py:58
  26.1 1.4 %fusion.6 = (bf16[16,2176]{1,0:T(8,128)(2,1)S(1)}, f32[16,512]{1,0:T(8,128)}) fusion(bf16[16,2176]{1,0:T(8,128)(2,1)S(1)} %fusion.7, f32[16,512]{1,0:T(8,128)S(1)} %reduce_sum.18, pred[]{:T(512)S(6)} %eq.5, f32[16,512]{1,0:T(8,128)} %param.10), kind=kLoop, calls=%fused_computation.15 | loop fusion | flops 57344 | bytes 114689
  27.5 0.8 fusion.3
  28.4 28.3 %all_to_all.25 = bf16[8,16,2176]{2,1,0:T(8,128)(2,1)S(1)} all-to-all(bf16[8,16,2176]{2,1,0:T(8,128)(2,1)S(1)} %broadcast_in_dim.14), channel_id=1, replica_groups=mesh['zhi'=4,'core'=2,'zlo'=2,'yhi'=4,'ylo'=2,'xhi'=2,'xlo'=2] {'xhi','y..., dimensions={0} | all-to-all | bytes 1114112 | tf_op jit(solution)/shard_map/all_to_all | solution.py:58
  56.7 0.4 broadcast_in_dim.15
  57.1 27.4 %all_to_all.26 = bf16[8,2,4,16,1536]{4,3,2,1,0:T(8,128)(2,1)S(1)} all-to-all(bf16[8,2,4,16,1536]{4,3,2,1,0:T(8,128)(2,1)S(1)} %broadcast_in_dim.15), channel_id=1, replica_groups={{0,1,4,5,32,33,36,37},{2,3,6,7,34,35,38,39},{8,9,12,13,40,41,44,45},{10..., dimensions={0} | all-to-all | bytes 6291456 | tf_op jit(solution)/shard_map/all_to_all | solution.py:58
  84.4 1.9 %collective-permute-start = (bf16[8,2,4,16,1536]{4,3,2,1,0:T(8,128)(2,1)S(1)}, bf16[8,2,4,16,1536]{4,3,2,1,0:T(8,128)(2,1)}, u32[]{:S(2)}, u32[]{:S(2)}) collective-permute-start(bf16[8,2,4,16,1536]{4,3,2,1,0:T(8,128)(2,1)S(1)} %all_to_all.26), channel_id=1, source_target_pairs={{0,64},{64,0},{1,65},{65,1},{2,66},{66,2},{3,67},{67,3},{4,68},{68... | collective-permute-start | bytes 9437192 | tf_op jit(solution)/shard_map/ppermute | solution.py:313
  86.4 0.0 copy-start
  86.4 0.0 copy-start.1
  86.4 0.0 copy-start.2
  86.4 1.3 broadcast_in_dim.16
  87.7 4.3 %all-to-all-start.3 = ((bf16[8,2,4,16,640]{4,3,2,1,0:T(8,128)(2,1)}), bf16[8,2,4,16,640]{4,3,2,1,0:T(8,128)(2,1)}, u32[]{:S(2)}, u32[]{:S(2)}) async-start(bf16[8,2,4,16,640]{4,3,2,1,0:T(8,128)(2,1)} %broadcast_in_dim.16), calls=%async_computation.3 | async-start | bytes 2621440 | tf_op jit(solution)/shard_map/all_to_all | solution.py:58
  92.0 0.1 stack.25.at_ref
  92.1 0.1 collective-permute-done
  92.1 0.0 copy-done
  92.1 0.0 copy-done.1
  92.1 0.0 copy-done.2
  92.1 9.2 %middle.1 = (bf16[1024,1024]{1,0:T(8,128)(2,1)S(1)}, bf16[1024,512]{1,0:T(8,128)(2,1)S(1)}, f32[16,512]{1,0:T(8,128)S(1)}, f32[16,512]{1,0:T(8,128)}, f32[16,102...) custom-call(s32[5]{0:T(128)S(1)} %stack.25.at_ref, bf16[2,2,2,2,4,16,1536]{6,5,4,3,2,1,0:T(8,128)(2,1)S(1)} %bitcast.11, ...), custom_call_target="tpu_custom_call" | custom-call | flops 6442450944 | bytes 12582912 | tf_op jit(solution)/shard_map/middle/pallas_call | solution.py:244
  101.3 0.0 copy-start.3
  101.3 1.3 %copy-done.3 = bf16[1024,1024]{1,0:T(8,128)(2,1)} copy-done((bf16[1024,1024]{1,0:T(8,128)(2,1)}, bf16[1024,1024]{1,0:T(8,128)(2,1)S(1)}, u32[]{:S(2)}) %copy-start.3) | copy-done | bytes 2097176
  102.6 0.0 copy-start.5
  102.6 1.0 copy-done.5
  103.6 3.5 %all-to-all-done.3 = bf16[8,2,4,16,640]{4,3,2,1,0:T(8,128)(2,1)} async-done(((bf16[8,2,4,16,640]{4,3,2,1,0:T(8,128)(2,1)}), bf16[8,2,4,16,640]{4,3,2,1,0:T(8,128)(2,1)}, u32[]{:S(2)}, u32[]{:S(2)}) %all-to-all-start.3) | async-done | bytes 1310752 | tf_op jit(solution)/shard_map/all_to_all | solution.py:58
  107.0 1.9 %collective-permute-start.1 = (bf16[8,2,4,16,640]{4,3,2,1,0:T(8,128)(2,1)}, bf16[8,2,4,16,640]{4,3,2,1,0:T(8,128)(2,1)S(1)}, u32[]{:S(2)}, u32[]{:S(2)}) collective-permute-start(bf16[8,2,4,16,640]{4,3,2,1,0:T(8,128)(2,1)} %all-to-all-done.3), channel_id=1, source_target_pairs={{0,64},{64,0},{1,65},{65,1},{2,66},{66,2},{3,67},{67,3},{4,68},{68... | collective-permute-start | bytes 3932168 | tf_op jit(solution)/shard_map/ppermute | solution.py:321
  109.0 0.1 pad_add_fusion.first_ref
  109.0 0.7 broadcast_in_dim.17
  109.8 3.8 %all-to-all-start.4 = ((f32[8,16,512]{2,1,0:T(8,128)}), f32[8,16,512]{2,1,0:T(8,128)S(1)}, u32[]{:S(2)}, u32[]{:S(2)}) async-start(f32[8,16,512]{2,1,0:T(8,128)} %broadcast_in_dim.17), calls=%async_computation.4 | async-start | bytes 524288 | tf_op jit(solution)/shard_map/all_to_all | solution.py:58
  113.6 0.0 collective-permute-done.1
  113.6 0.0 copy-start.4
  113.6 1.6 %copy-done.4 = bf16[1024,1024]{1,0:T(8,128)(2,1)S(1)} copy-done((bf16[1024,1024]{1,0:T(8,128)(2,1)S(1)}, bf16[1024,1024]{1,0:T(8,128)(2,1)}, u32[]{:S(2)}) %copy-start.4) | copy-done | bytes 2097176
  115.2 0.0 copy-start.6
  115.2 1.2 copy-done.6
  116.4 0.0 copy-start.7
  116.4 13.4 %left_refresh.1 = f32[16,1024]{1,0:T(8,128)} custom-call(s32[2]{0:T(128)S(1)} %pad_add_fusion.first_ref, bf16[2,2,2,2,4,16,640]{6,5,4,3,2,1,0:T(8,128)(2,1)} %bitcast.9.mine_ref, bf16[2,2,2,2,4,16,640]{6,5,4,3,2,1,0:T(8,128)(2,1)S(1)} %bitcast.12, bf16[1024,512]{1,0:T(8,128)(2,1)S(1)} %copy-done.6, bf16[1024,1024]{1,0:T(8,128)(2,1)S(1)} %copy-done.4), custom_call_target="tpu_custom_call" | custom-call | flops 10737418240 | bytes 8388608 | tf_op jit(solution)/shard_map/left_refresh/pallas_call | solution.py:128
  129.8 0.0 all-to-all-done.4
  129.8 0.0 copy-done.7
  129.8 0.6 multiply_subtract_fusion
  (13 shorter events, 0.2 us)
Async XLA Ops:
  2.1 24.0 %all-to-all-start = ((f32[8,16,512]{2,1,0:T(8,128)}), f32[8,16,512]{2,1,0:T(8,128)S(1)}, u32[]{:S(2)}, u32[]{:S(2)}) async-start(f32[8,16,512]{2,1,0:T(8,128)} %broadcast_in_dim.13), calls=%async_computation | async-start | bytes 524288 | tf_op jit(solution)/shard_map/all_to_all | solution.py:58
  84.4 7.7 %collective-permute-start = (bf16[8,2,4,16,1536]{4,3,2,1,0:T(8,128)(2,1)S(1)}, bf16[8,2,4,16,1536]{4,3,2,1,0:T(8,128)(2,1)}, u32[]{:S(2)}, u32[]{:S(2)}) collective-permute-start(bf16[8,2,4,16,1536]{4,3,2,1,0:T(8,128)(2,1)S(1)} %all_to_all.26), channel_id=1, source_target_pairs={{0,64},{64,0},{1,65},{65,1},{2,66},{66,2},{3,67},{67,3},{4,68},{68... | collective-permute-start | bytes 9437192 | tf_op jit(solution)/shard_map/ppermute | solution.py:313
  86.4 5.7 %copy-start = (f32[16,1024]{1,0:T(8,128)S(1)}, f32[16,1024]{1,0:T(8,128)}, u32[]{:S(2)}) copy-start(f32[16,1024]{1,0:T(8,128)} %left_gram_ref.1) | copy-start | bytes 196612
  86.4 5.7 %copy-start.1 = (f32[8,512]{1,0:T(8,128)S(1)}, f32[8,512]{1,0:T(8,128)}, u32[]{:S(2)}) copy-start(f32[8,512]{1,0:T(8,128)} %right_gram_ref.1) | copy-start | bytes 49156
  86.4 5.7 %copy-start.2 = (f32[16,512]{1,0:T(8,128)S(1)}, f32[16,512]{1,0:T(8,128)}, u32[]{:S(2)}) copy-start(f32[16,512]{1,0:T(8,128)} %second_ref.1) | copy-start | bytes 98308
  87.7 19.4 %all-to-all-start.3 = ((bf16[8,2,4,16,640]{4,3,2,1,0:T(8,128)(2,1)}), bf16[8,2,4,16,640]{4,3,2,1,0:T(8,128)(2,1)}, u32[]{:S(2)}, u32[]{:S(2)}) async-start(bf16[8,2,4,16,640]{4,3,2,1,0:T(8,128)(2,1)} %broadcast_in_dim.16), calls=%async_computation.3 | async-start | bytes 2621440 | tf_op jit(solution)/shard_map/all_to_all | solution.py:58
  101.3 1.3 %copy-start.3 = (bf16[1024,1024]{1,0:T(8,128)(2,1)}, bf16[1024,1024]{1,0:T(8,128)(2,1)S(1)}, u32[]{:S(2)}) copy-start(bf16[1024,1024]{1,0:T(8,128)(2,1)S(1)} %get-tuple-element.22.basis_ref) | copy-start | bytes 6291460
  102.6 1.0 copy-start.5
  107.0 6.5 %collective-permute-start.1 = (bf16[8,2,4,16,640]{4,3,2,1,0:T(8,128)(2,1)}, bf16[8,2,4,16,640]{4,3,2,1,0:T(8,128)(2,1)S(1)}, u32[]{:S(2)}, u32[]{:S(2)}) collective-permute-start(bf16[8,2,4,16,640]{4,3,2,1,0:T(8,128)(2,1)} %all-to-all-done.3), channel_id=1, source_target_pairs={{0,64},{64,0},{1,65},{65,1},{2,66},{66,2},{3,67},{67,3},{4,68},{68... | collective-permute-start | bytes 3932168 | tf_op jit(solution)/shard_map/ppermute | solution.py:321
  109.8 20.0 %all-to-all-start.4 = ((f32[8,16,512]{2,1,0:T(8,128)}), f32[8,16,512]{2,1,0:T(8,128)S(1)}, u32[]{:S(2)}, u32[]{:S(2)}) async-start(f32[8,16,512]{2,1,0:T(8,128)} %broadcast_in_dim.17), calls=%async_computation.4 | async-start | bytes 524288 | tf_op jit(solution)/shard_map/all_to_all | solution.py:58
  113.6 1.6 %copy-start.4 = (bf16[1024,1024]{1,0:T(8,128)(2,1)S(1)}, bf16[1024,1024]{1,0:T(8,128)(2,1)}, u32[]{:S(2)}) copy-start(bf16[1024,1024]{1,0:T(8,128)(2,1)} %copy-done.3) | copy-start | bytes 6291460
  115.2 1.2 copy-start.6
  116.4 13.4 %copy-start.7 = (f32[16,512]{1,0:T(8,128)S(1)}, f32[16,512]{1,0:T(8,128)}, u32[]{:S(2)}) copy-start(f32[16,512]{1,0:T(8,128)} %param.9) | copy-start | bytes 98308

commit v6 on v5

--- a/solution.py
+++ b/solution.py
@@ -91,8 +91,23 @@
     out_ref[...] = 1.5 * rows.astype(f32) - 0.5 * mm(square, x, 1, 0)
 
 
-def left_kernel(first_ref, mine_ref, other_ref, grad_ref, basis_ref, out_ref, gram, power, start, current):
-    rows = mine_ref.shape[-2]
+def left_kernel(
+    first_ref, mine_hbm, other_hbm, grad_hbm, basis_hbm, out_ref,
+    mine_ref, other_ref, grad_ref, basis_ref, gram, power, start, current, sems,
+):
+    pairs = ((grad_hbm, grad_ref), (mine_hbm, mine_ref), (other_hbm, other_ref), (basis_hbm, basis_ref))
+    copies = [pltpu.make_async_copy(a, b, sems.at[i]) for i, (a, b) in enumerate(pairs)]
+    for copy in copies:
+        copy.start()
+    rows, deep = mine_ref.shape[-2], basis_ref.shape[0]
+    tile = 256
+    copies[0].wait()
+    grad = grad_ref[...]
+    for t in range(deep // tile):
+        at = pl.ds(t * tile, tile)
+        power[at, :] = (1.0 - GRAM_DECAY) * mm(grad_ref[at, :], grad, 1, 1)
+    copies[1].wait()
+    copies[2].wait()
     for r in range(BLOCKS):
         zlo, far = r // NF, r % NF
         for j in range(SENT):
@@ -107,36 +122,37 @@
             gram[r * BLOCK : (r + 1) * BLOCK, c * BLOCK : (c + 1) * BLOCK] = block
             if 0 < j < BLOCKS // 2:
                 gram[c * BLOCK : (c + 1) * BLOCK, r * BLOCK : (r + 1) * BLOCK] = block.T
-    grad = grad_ref[...]
+    copies[3].wait()
     basis = basis_ref[...]
-    tile = 256
 
     def power_tile(t):
         at = pl.ds(t * tile, tile)
-        whole = gram[at, :] + (1.0 - GRAM_DECAY) * mm(grad_ref[at, :], grad, 1, 1)
-        high, low = split(whole)
+        high, low = split(gram[at, :] + power[at, :])
         return mm(high, basis, 1, 0) + mm(low, basis, 1, 0)
 
-    refresh(power_tile, gram.shape[0] // tile, tile, first_ref[0], rows, power, start, current, out_ref)
-    result, half = out_ref[...], gram.shape[0] // 2
+    refresh(power_tile, deep // tile, tile, first_ref[0], rows, power, start, current, out_ref)
+    result, half = out_ref[...], deep // 2
     out_ref[...] = jnp.where(first_ref[1] == 0, result, jnp.concatenate([result[:, half:], result[:, :half]], axis=1))
 
 
 def left_call(first, mine, other, grad, basis, rows):
     deep = basis.shape[0]
-    vmem = pl.BlockSpec(memory_space=pltpu.VMEM)
+    hbm = pl.BlockSpec(memory_space=pltpu.HBM)
+    anywhere = pl.BlockSpec(memory_space=pl.ANY)
     return pl.pallas_call(
         left_kernel,
         out_shape=jax.ShapeDtypeStruct((rows, deep), f32),
-        in_specs=[pl.BlockSpec(memory_space=pltpu.SMEM)] + [vmem] * 4,
-        out_specs=vmem,
-        scratch_shapes=[
+        in_specs=[pl.BlockSpec(memory_space=pltpu.SMEM), anywhere, anywhere, hbm, hbm],
+        out_specs=pl.BlockSpec(memory_space=pltpu.VMEM),
+        scratch_shapes=[pltpu.VMEM(v.shape, bf16) for v in (mine, other, grad, basis)]
+        + [
             pltpu.VMEM((deep, deep), f32),
             pltpu.VMEM((deep, deep), f32),
             pltpu.VMEM((deep, deep), bf16),
             pltpu.VMEM((deep, deep), bf16),
+            pltpu.SemaphoreType.DMA((4,)),
         ],
-        compiler_params=pltpu.CompilerParams(vmem_limit_bytes=20 << 20),
+        compiler_params=pltpu.CompilerParams(vmem_limit_bytes=28 << 20),
         cost_estimate=pl.CostEstimate(flops=10 * deep**3, transcendentals=deep, bytes_accessed=8 * deep**2),
         name="left_refresh",
     )(first, mine, other, grad, basis)
@@ -144,8 +160,8 @@
 
 def mid_kernel(
     at_ref, mine_ref, other_ref, second_ref, left_rows_ref, left_gram_ref, right_gram_ref,
-    basis_ref, grad_ref, update_ref, second_new_ref, left_new_ref, right_new_ref, right_out_ref,
-    mom, right, rgram, second_rows, term, power, start, current,
+    basis_hbm, grad_hbm, update_ref, second_new_ref, left_new_ref, right_new_ref, right_out_ref,
+    basis_ref, grad_ref, sems, mom, right, rgram, second_rows, term, power, start, current,
 ):
     right_pair, right_odd, group, row_first, core = (at_ref[i] for i in range(5))
     first = core == 0
@@ -190,6 +206,12 @@
                         of = slice(part * share, (part + 1) * share)
                         second_rows[spot * share : (spot + 1) * share, part * n : (part + 1) * n] = both[of]
                     spot += 1
+    copies = [
+        pltpu.make_async_copy(basis_ref, basis_hbm, sems.at[0]),
+        pltpu.make_async_copy(grad_ref, grad_hbm, sems.at[1]),
+    ]
+    for copy in copies:
+        copy.start()
     basis, grad = basis_ref[...], grad_ref[...]
     rbasis = right[...].astype(bf16)
 
@@ -231,6 +253,8 @@
 
     refresh(power_tile, width // tile, tile, right_pair, rows, power, start, current, term)
     right_out_ref[...] = term[pl.ds(pl.multiple_of(right_odd, right_rows), right_rows), :]
+    for copy in copies:
+        copy.wait()
 
 
 def mid_call(at, mine, other, second, left_rows, left_gram, right_gram):
@@ -243,10 +267,13 @@
     ]
     return pl.pallas_call(
         mid_kernel,
-        out_shape=[jax.ShapeDtypeStruct(*v) for v in shapes],
+        out_shape=[pltpu.HBM(*v) for v in shapes[:2]] + [jax.ShapeDtypeStruct(*v) for v in shapes[2:]],
         in_specs=[pl.BlockSpec(memory_space=pltpu.SMEM)] + [vmem] * 6,
-        out_specs=[vmem] * len(shapes),
+        out_specs=[pl.BlockSpec(memory_space=pltpu.HBM)] * 2 + [vmem] * (len(shapes) - 2),
         scratch_shapes=[
+            pltpu.VMEM((deep, deep), bf16),
+            pltpu.VMEM((deep, width), bf16),
+            pltpu.SemaphoreType.DMA((2,)),
             pltpu.VMEM((deep, width), bf16),
             pltpu.VMEM((width, width), f32),
             pltpu.VMEM((width, width), f32),
@@ -320,6 +347,7 @@
     update, late = lax.optimization_barrier((update, late))
     late_other = lax.ppermute(late, "core", swap)
     updates = gather(update, GRP, n_grp)
+    basis, grad = (pltpu.with_memory_space_constraint(v, pltpu.HBM) for v in (basis, grad))
     left_result = left_call(at[3:], parted(late), parted(late_other), grad, basis, rows)
     updates, left_result = lax.optimization_barrier((updates, left_result))
     weight_new = weight - STEP_SIZE * jnp.sum(updates, axis=0)

time: 132 us -> 130 us (0.985)
  local copies, waits for them, and re-layouts: 9.99 us -> 4.84 us
  waiting for transfers between devices: 11.8 us -> 14 us
    unnamed x17 -> x9, local copies, waits for them, and re-layouts: 5.14 us -> 0.03 us
    all_to_all x3, waiting for transfers between devices: 11.8 us -> 14 us  [gather(): return lax.all_to_all(copies, axes, 0, 0, axis_index_groups=groups)]
  transfers between devices with their start and end apart: 5 -> 5, of which waited for: 3 -> 3; matrix products, arithmetic and copies ran while one was open for 5% -> 5% of each run, Pallas kernels for 17% -> 18%
where the time goes in v6:
time: 130 us; the launch traced here: 129 us
  blocking collectives  55.6 us (43%)
  starting transfers between devices  23.7 us (18%)
  Pallas kernels  23.7 us (18%)
  waiting for transfers between devices  14 us (11%)
  other arithmetic  5.97 us (5%)
  local copies, waits for them, and re-layouts  4.84 us (4%)
    all_to_all x2, blocking collectives, gather(): return lax.all_to_all(copies, axes, 0, 0, axis_index_groups=groups)  55.6 us
    all_to_all x3, starting transfers between devices, gather(): return lax.all_to_all(copies, axes, 0, 0, axis_index_groups=groups)  19.9 us
    pallas_call x1, Pallas kernels, left_call(): pl.pallas_call(left_kernel, out_shape=jax.ShapeDtypeStruct((rows, deep),...  14.5 us
    all_to_all x3, waiting for transfers between devices, gather(): return lax.all_to_all(copies, axes, 0, 0, axis_index_groups=groups)  14 us
    pallas_call x1, Pallas kernels, mid_call(): pl.pallas_call(mid_kernel, out_shape=[pltpu.HBM(*v) for v in shapes[:2]]...  9.22 us
    broadcast_in_dim x5, local copies, waits for them, and re-layouts, gather(): copies = jnp.broadcast_to(value[None], (size,) + value.shape)  3.85 us
  transfers between devices with their start and end apart: 5, of which 3 were waited for; matrix products, arithmetic and copies ran while one was open for 5% of the time, Pallas kernels for 18%

profile of v6, /device:TPU:1, one launch (start us, length us, event | category | flops | bytes accessed | tf_op | source)
XLA Modules:
  0.0 128.7 jit_solution(5520737880563543665)
XLA Ops:
  0.6 1.5 %broadcast_in_dim.13 = f32[8,16,512]{2,1,0:T(8,128)} broadcast(f32[16,512]{1,0:T(8,128)} %bitcast.15), dimensions={1,2} | broadcast | bytes 294912 | tf_op jit(solution)/shard_map/broadcast_in_dim | solution.py:57
  2.1 11.8 %all-to-all-start = ((f32[8,16,512]{2,1,0:T(8,128)}), f32[8,16,512]{2,1,0:T(8,128)S(1)}, u32[]{:S(2)}, u32[]{:S(2)}) async-start(f32[8,16,512]{2,1,0:T(8,128)} %broadcast_in_dim.13), calls=%async_computation | async-start | bytes 524288 | tf_op jit(solution)/shard_map/all_to_all | solution.py:58
  13.9 0.7 convert_element_type.33
  14.7 0.7 fusion.8
  15.4 0.7 fusion.9
  16.1 0.8 convert_element_type.30.left_rows_ref
  17.0 0.8 slice.27
  17.8 0.1 concatenate.18
  17.8 8.3 %all-to-all-done = f32[8,16,512]{2,1,0:T(8,128)S(1)} async-done(((f32[8,16,512]{2,1,0:T(8,128)}), f32[8,16,512]{2,1,0:T(8,128)S(1)}, u32[]{:S(2)}, u32[]{:S(2)}) %all-to-all-start) | async-done | bytes 262176 | tf_op jit(solution)/shard_map/all_to_all | solution.py:58
  26.1 1.4 %fusion.6 = (bf16[16,2176]{1,0:T(8,128)(2,1)S(1)}, f32[16,512]{1,0:T(8,128)}) fusion(bf16[16,2176]{1,0:T(8,128)(2,1)S(1)} %fusion.7, f32[16,512]{1,0:T(8,128)S(1)} %reduce_sum.18, pred[]{:T(512)S(6)} %eq.5, f32[16,512]{1,0:T(8,128)} %param.10), kind=kLoop, calls=%fused_computation.15 | loop fusion | flops 57344 | bytes 114689
  27.5 0.8 fusion.3
  28.4 28.3 %all_to_all.25 = bf16[8,16,2176]{2,1,0:T(8,128)(2,1)S(1)} all-to-all(bf16[8,16,2176]{2,1,0:T(8,128)(2,1)S(1)} %broadcast_in_dim.14), channel_id=1, replica_groups=mesh['zhi'=4,'core'=2,'zlo'=2,'yhi'=4,'ylo'=2,'xhi'=2,'xlo'=2] {'xhi','y..., dimensions={0} | all-to-all | bytes 1114112 | tf_op jit(solution)/shard_map/all_to_all | solution.py:58
  56.7 0.4 broadcast_in_dim.15
  57.1 27.4 %all_to_all.26 = bf16[8,2,4,16,1536]{4,3,2,1,0:T(8,128)(2,1)S(1)} all-to-all(bf16[8,2,4,16,1536]{4,3,2,1,0:T(8,128)(2,1)S(1)} %broadcast_in_dim.15), channel_id=1, replica_groups={{0,1,4,5,32,33,36,37},{2,3,6,7,34,35,38,39},{8,9,12,13,40,41,44,45},{10..., dimensions={0} | all-to-all | bytes 6291456 | tf_op jit(solution)/shard_map/all_to_all | solution.py:58
  84.4 1.9 %collective-permute-start = (bf16[8,2,4,16,1536]{4,3,2,1,0:T(8,128)(2,1)S(1)}, bf16[8,2,4,16,1536]{4,3,2,1,0:T(8,128)(2,1)}, u32[]{:S(2)}, u32[]{:S(2)}) collective-permute-start(bf16[8,2,4,16,1536]{4,3,2,1,0:T(8,128)(2,1)S(1)} %all_to_all.26), channel_id=1, source_target_pairs={{0,64},{64,0},{1,65},{65,1},{2,66},{66,2},{3,67},{67,3},{4,68},{68... | collective-permute-start | bytes 9437192 | tf_op jit(solution)/shard_map/ppermute | solution.py:340
  86.4 0.0 copy-start
  86.4 0.0 copy-start.1
  86.4 0.0 copy-start.2
  86.4 1.2 broadcast_in_dim.16
  87.7 4.3 %all-to-all-start.3 = ((bf16[8,2,4,16,640]{4,3,2,1,0:T(8,128)(2,1)}), bf16[8,2,4,16,640]{4,3,2,1,0:T(8,128)(2,1)}, u32[]{:S(2)}, u32[]{:S(2)}) async-start(bf16[8,2,4,16,640]{4,3,2,1,0:T(8,128)(2,1)} %broadcast_in_dim.16), calls=%async_computation.3 | async-start | bytes 2621440 | tf_op jit(solution)/shard_map/all_to_all | solution.py:58
  92.0 0.1 stack.25.at_ref
  92.0 0.1 collective-permute-done
  92.1 0.0 copy-done
  92.1 0.0 copy-done.1
  92.1 0.0 copy-done.2
  92.1 9.2 %middle.1 = (bf16[1024,1024]{1,0:T(8,128)(2,1)}, bf16[1024,512]{1,0:T(8,128)(2,1)}, f32[16,512]{1,0:T(8,128)S(1)}, f32[16,512]{1,0:T(8,128)}, f32[16,1024]{1,0:T...) custom-call(s32[5]{0:T(128)S(1)} %stack.25.at_ref, bf16[2,2,2,2,4,16,1536]{6,5,4,3,2,1,0:T(8,128)(2,1)S(1)} %bitcast.11, ...), custom_call_target="tpu_custom_call" | custom-call | flops 6442450944 | bytes 12582912 | tf_op jit(solution)/shard_map/middle/pallas_call | solution.py:268
  101.4 5.7 %all-to-all-done.3 = bf16[8,2,4,16,640]{4,3,2,1,0:T(8,128)(2,1)} async-done(((bf16[8,2,4,16,640]{4,3,2,1,0:T(8,128)(2,1)}), bf16[8,2,4,16,640]{4,3,2,1,0:T(8,128)(2,1)}, u32[]{:S(2)}, u32[]{:S(2)}) %all-to-all-start.3) | async-done | bytes 1310752 | tf_op jit(solution)/shard_map/all_to_all | solution.py:58
  107.0 1.9 %collective-permute-start.1 = (bf16[8,2,4,16,640]{4,3,2,1,0:T(8,128)(2,1)}, bf16[8,2,4,16,640]{4,3,2,1,0:T(8,128)(2,1)S(1)}, u32[]{:S(2)}, u32[]{:S(2)}) collective-permute-start(bf16[8,2,4,16,640]{4,3,2,1,0:T(8,128)(2,1)} %all-to-all-done.3), channel_id=1, source_target_pairs={{0,64},{64,0},{1,65},{65,1},{2,66},{66,2},{3,67},{67,3},{4,68},{68... | collective-permute-start | bytes 3932168 | tf_op jit(solution)/shard_map/ppermute | solution.py:348
  108.9 0.1 pad_add_fusion.first_ref
  109.0 0.7 broadcast_in_dim.17
  109.7 3.8 %all-to-all-start.4 = ((f32[8,16,512]{2,1,0:T(8,128)}), f32[8,16,512]{2,1,0:T(8,128)S(1)}, u32[]{:S(2)}, u32[]{:S(2)}) async-start(f32[8,16,512]{2,1,0:T(8,128)} %broadcast_in_dim.17), calls=%async_computation.4 | async-start | bytes 524288 | tf_op jit(solution)/shard_map/all_to_all | solution.py:58
  113.6 0.0 collective-permute-done.1
  113.6 0.0 copy-start.3
  113.6 14.5 %left_refresh.1 = f32[16,1024]{1,0:T(8,128)} custom-call(s32[2]{0:T(128)S(1)} %pad_add_fusion.first_ref, bf16[2,2,2,2,4,16,640]{6,5,4,3,2,1,0:T(8,128)(2,1)} %bitcast.9.mine_hbm, bf16[2,2,2,2,4,16,640]{6,5,4,3,2,1,0:T(8,128)(2,1)S(1)} %bitcast.12, bf16[1024,512]{1,0:T(8,128)(2,1)} %get-tuple-element.21.grad_hbm, bf16[1024,1024]{1,0:T(8,128)(2,1)} %get-tuple-element.22.basis_hbm), custom_call_target="tpu_custom_call" | custom-call | flops 10737418240 | bytes 8388608 | tf_op jit(solution)/shard_map/left_refresh/pallas_call | solution.py:142
  128.1 0.0 all-to-all-done.4
  128.1 0.0 copy-done.3
  128.1 0.6 multiply_subtract_fusion
  (13 shorter events, 0.2 us)
Async XLA Ops:
  2.1 24.0 %all-to-all-start = ((f32[8,16,512]{2,1,0:T(8,128)}), f32[8,16,512]{2,1,0:T(8,128)S(1)}, u32[]{:S(2)}, u32[]{:S(2)}) async-start(f32[8,16,512]{2,1,0:T(8,128)} %broadcast_in_dim.13), calls=%async_computation | async-start | bytes 524288 | tf_op jit(solution)/shard_map/all_to_all | solution.py:58
  84.4 7.7 %collective-permute-start = (bf16[8,2,4,16,1536]{4,3,2,1,0:T(8,128)(2,1)S(1)}, bf16[8,2,4,16,1536]{4,3,2,1,0:T(8,128)(2,1)}, u32[]{:S(2)}, u32[]{:S(2)}) collective-permute-start(bf16[8,2,4,16,1536]{4,3,2,1,0:T(8,128)(2,1)S(1)} %all_to_all.26), channel_id=1, source_target_pairs={{0,64},{64,0},{1,65},{65,1},{2,66},{66,2},{3,67},{67,3},{4,68},{68... | collective-permute-start | bytes 9437192 | tf_op jit(solution)/shard_map/ppermute | solution.py:340
  86.4 5.7 %copy-start = (f32[16,1024]{1,0:T(8,128)S(1)}, f32[16,1024]{1,0:T(8,128)}, u32[]{:S(2)}) copy-start(f32[16,1024]{1,0:T(8,128)} %left_gram_ref.1) | copy-start | bytes 196612
  86.4 5.7 %copy-start.1 = (f32[8,512]{1,0:T(8,128)S(1)}, f32[8,512]{1,0:T(8,128)}, u32[]{:S(2)}) copy-start(f32[8,512]{1,0:T(8,128)} %right_gram_ref.1) | copy-start | bytes 49156
  86.4 5.7 %copy-start.2 = (f32[16,512]{1,0:T(8,128)S(1)}, f32[16,512]{1,0:T(8,128)}, u32[]{:S(2)}) copy-start(f32[16,512]{1,0:T(8,128)} %second_ref.1) | copy-start | bytes 98308
  87.7 19.4 %all-to-all-start.3 = ((bf16[8,2,4,16,640]{4,3,2,1,0:T(8,128)(2,1)}), bf16[8,2,4,16,640]{4,3,2,1,0:T(8,128)(2,1)}, u32[]{:S(2)}, u32[]{:S(2)}) async-start(bf16[8,2,4,16,640]{4,3,2,1,0:T(8,128)(2,1)} %broadcast_in_dim.16), calls=%async_computation.3 | async-start | bytes 2621440 | tf_op jit(solution)/shard_map/all_to_all | solution.py:58
  107.0 6.5 %collective-permute-start.1 = (bf16[8,2,4,16,640]{4,3,2,1,0:T(8,128)(2,1)}, bf16[8,2,4,16,640]{4,3,2,1,0:T(8,128)(2,1)S(1)}, u32[]{:S(2)}, u32[]{:S(2)}) collective-permute-start(bf16[8,2,4,16,640]{4,3,2,1,0:T(8,128)(2,1)} %all-to-all-done.3), channel_id=1, source_target_pairs={{0,64},{64,0},{1,65},{65,1},{2,66},{66,2},{3,67},{67,3},{4,68},{68... | collective-permute-start | bytes 3932168 | tf_op jit(solution)/shard_map/ppermute | solution.py:348
  109.7 18.3 %all-to-all-start.4 = ((f32[8,16,512]{2,1,0:T(8,128)}), f32[8,16,512]{2,1,0:T(8,128)S(1)}, u32[]{:S(2)}, u32[]{:S(2)}) async-start(f32[8,16,512]{2,1,0:T(8,128)} %broadcast_in_dim.17), calls=%async_computation.4 | async-start | bytes 524288 | tf_op jit(solution)/shard_map/all_to_all | solution.py:58
  113.6 14.6 %copy-start.3 = (f32[16,512]{1,0:T(8,128)S(1)}, f32[16,512]{1,0:T(8,128)}, u32[]{:S(2)}) copy-start(f32[16,512]{1,0:T(8,128)} %param.9) | copy-start | bytes 98308

commit v7 on v6

--- a/solution.py
+++ b/solution.py
@@ -92,22 +92,16 @@
 
 
 def left_kernel(
-    first_ref, mine_hbm, other_hbm, grad_hbm, basis_hbm, out_ref,
-    mine_ref, other_ref, grad_ref, basis_ref, gram, power, start, current, sems,
+    first_ref, mine_hbm, other_hbm, outer_hbm, basis_hbm, out_ref,
+    mine_ref, other_ref, basis_ref, gram, power, start, current, sems,
 ):
-    pairs = ((grad_hbm, grad_ref), (mine_hbm, mine_ref), (other_hbm, other_ref), (basis_hbm, basis_ref))
+    pairs = ((mine_hbm, mine_ref), (other_hbm, other_ref), (outer_hbm, power), (basis_hbm, basis_ref))
     copies = [pltpu.make_async_copy(a, b, sems.at[i]) for i, (a, b) in enumerate(pairs)]
     for copy in copies:
         copy.start()
-    rows, deep = mine_ref.shape[-2], basis_ref.shape[0]
-    tile = 256
+    rows, deep, tile = mine_ref.shape[-2], basis_ref.shape[0], 256
     copies[0].wait()
-    grad = grad_ref[...]
-    for t in range(deep // tile):
-        at = pl.ds(t * tile, tile)
-        power[at, :] = (1.0 - GRAM_DECAY) * mm(grad_ref[at, :], grad, 1, 1)
     copies[1].wait()
-    copies[2].wait()
     for r in range(BLOCKS):
         zlo, far = r // NF, r % NF
         for j in range(SENT):
@@ -122,6 +116,7 @@
             gram[r * BLOCK : (r + 1) * BLOCK, c * BLOCK : (c + 1) * BLOCK] = block
             if 0 < j < BLOCKS // 2:
                 gram[c * BLOCK : (c + 1) * BLOCK, r * BLOCK : (r + 1) * BLOCK] = block.T
+    copies[2].wait()
     copies[3].wait()
     basis = basis_ref[...]
 
@@ -135,7 +130,7 @@
     out_ref[...] = jnp.where(first_ref[1] == 0, result, jnp.concatenate([result[:, half:], result[:, :half]], axis=1))
 
 
-def left_call(first, mine, other, grad, basis, rows):
+def left_call(first, mine, other, outer, basis, rows):
     deep = basis.shape[0]
     hbm = pl.BlockSpec(memory_space=pltpu.HBM)
     anywhere = pl.BlockSpec(memory_space=pl.ANY)
@@ -144,7 +139,7 @@
         out_shape=jax.ShapeDtypeStruct((rows, deep), f32),
         in_specs=[pl.BlockSpec(memory_space=pltpu.SMEM), anywhere, anywhere, hbm, hbm],
         out_specs=pl.BlockSpec(memory_space=pltpu.VMEM),
-        scratch_shapes=[pltpu.VMEM(v.shape, bf16) for v in (mine, other, grad, basis)]
+        scratch_shapes=[pltpu.VMEM(v.shape, bf16) for v in (mine, other, basis)]
         + [
             pltpu.VMEM((deep, deep), f32),
             pltpu.VMEM((deep, deep), f32),
@@ -155,13 +150,13 @@
         compiler_params=pltpu.CompilerParams(vmem_limit_bytes=28 << 20),
         cost_estimate=pl.CostEstimate(flops=10 * deep**3, transcendentals=deep, bytes_accessed=8 * deep**2),
         name="left_refresh",
-    )(first, mine, other, grad, basis)
+    )(first, mine, other, outer, basis)
 
 
 def mid_kernel(
     at_ref, mine_ref, other_ref, second_ref, left_rows_ref, left_gram_ref, right_gram_ref,
-    basis_hbm, grad_hbm, update_ref, second_new_ref, left_new_ref, right_new_ref, right_out_ref,
-    basis_ref, grad_ref, sems, mom, right, rgram, second_rows, term, power, start, current,
+    basis_hbm, outer_hbm, update_ref, second_new_ref, left_new_ref, right_new_ref, right_out_ref,
+    basis_ref, grad_ref, outer, sems, mom, right, rgram, second_rows, term, power, start, current,
 ):
     right_pair, right_odd, group, row_first, core = (at_ref[i] for i in range(5))
     first = core == 0
@@ -208,11 +203,15 @@
                     spot += 1
     copies = [
         pltpu.make_async_copy(basis_ref, basis_hbm, sems.at[0]),
-        pltpu.make_async_copy(grad_ref, grad_hbm, sems.at[1]),
+        pltpu.make_async_copy(outer, outer_hbm, sems.at[1]),
     ]
-    for copy in copies:
-        copy.start()
+    copies[0].start()
     basis, grad = basis_ref[...], grad_ref[...]
+    tile = 256
+    for t in range(deep // tile):
+        to = pl.ds(t * tile, tile)
+        outer[to, :] = (1.0 - GRAM_DECAY) * mm(grad_ref[to, :], grad, 1, 1)
+    copies[1].start()
     rbasis = right[...].astype(bf16)
 
     n = second_rows.shape[0]
@@ -235,16 +234,14 @@
     own_rows = jnp.where(first, own_rows, jnp.concatenate([own_rows[:, half:], own_rows[:, :half]], axis=1))
     update_ref[...] = mm(mm(own_rows, pick, 1, 0).astype(bf16), returned, 1, 0)
 
-    own_grad = grad_ref[pl.ds(pl.multiple_of(row_first, rows), rows), :]
-    left_new_ref[...] = GRAM_DECAY * left_gram_ref[...] + (1.0 - GRAM_DECAY) * mm(own_grad, grad, 1, 1)
+    own_at = pl.ds(pl.multiple_of(row_first, rows), rows)
+    left_new_ref[...] = GRAM_DECAY * left_gram_ref[...] + outer[own_at, :]
     q = lax.broadcasted_iota(jnp.int32, (width, BLOCK), 1)
     column = lax.broadcasted_iota(jnp.int32, (width, BLOCK), 0)
     own = jnp.where((column == right_pair + right_odd + q) & (q < right_rows), 1.0, 0.0).astype(bf16)
     own = mm(mm(grad, own, 1, 0).astype(bf16), grad, 0, 0)[:right_rows]
     right_new_ref[...] = GRAM_DECAY * right_gram_ref[...] + (1.0 - GRAM_DECAY) * own
 
-    tile = 256
-
     def power_tile(t):
         at = pl.ds(t * tile, tile)
         whole = rgram[at, :] + (1.0 - GRAM_DECAY) * mm(grad_ref[:, t * tile : (t + 1) * tile], grad, 0, 0)
@@ -262,7 +259,7 @@
     width = second.shape[1]
     vmem = pl.BlockSpec(memory_space=pltpu.VMEM)
     shapes = [
-        ((deep, deep), bf16), ((deep, width), bf16), ((rows, width), f32), ((rows, width), f32),
+        ((deep, deep), bf16), ((deep, deep), f32), ((rows, width), f32), ((rows, width), f32),
         ((rows, deep), f32), (right_gram.shape, f32), (right_gram.shape, f32),
     ]
     return pl.pallas_call(
@@ -273,6 +270,7 @@
         scratch_shapes=[
             pltpu.VMEM((deep, deep), bf16),
             pltpu.VMEM((deep, width), bf16),
+            pltpu.VMEM((deep, deep), f32),
             pltpu.SemaphoreType.DMA((2,)),
             pltpu.VMEM((deep, width), bf16),
             pltpu.VMEM((width, width), f32),
@@ -283,10 +281,40 @@
             pltpu.VMEM((width, width), bf16),
             pltpu.VMEM((width, width), bf16),
         ],
-        compiler_params=pltpu.CompilerParams(vmem_limit_bytes=20 << 20),
+        compiler_params=pltpu.CompilerParams(vmem_limit_bytes=24 << 20),
         cost_estimate=pl.CostEstimate(flops=6 * deep**3, transcendentals=width**2, bytes_accessed=12 * deep**2),
         name="middle",
     )(at, mine, other, second, left_rows, left_gram, right_gram)
+
+
+def pack_kernel(at_ref, grads_ref, kept_ref, early_ref, copies_ref, moment_new_ref):
+    n, width = grads_ref.shape[0], kept_ref.shape[1]
+    gradient = grads_ref[0]
+    for i in range(1, n):
+        gradient = gradient + grads_ref[i]
+    gradient = gradient / n
+    moment_new = kept_ref[...] + (1.0 - BETA_ONE) * gradient
+    moment_new_ref[...] = moment_new
+    mine = jnp.where(at_ref[4] == 0, gradient, moment_new).astype(bf16)
+    early = early_ref[...]
+    for i in range(copies_ref.shape[0]):
+        copies_ref[i, :, :width] = early[:, :width]
+        copies_ref[i, :, width : 2 * width] = mine
+        copies_ref[i, :, 2 * width :] = early[:, width:]
+
+
+def pack_call(at, grads, kept, early, receivers):
+    rows, width = kept.shape
+    vmem = pl.BlockSpec(memory_space=pltpu.VMEM)
+    shapes = [((receivers, rows, early.shape[1] + width), bf16), (kept.shape, f32)]
+    return pl.pallas_call(
+        pack_kernel,
+        out_shape=[jax.ShapeDtypeStruct(*v) for v in shapes],
+        in_specs=[pl.BlockSpec(memory_space=pltpu.SMEM)] + [vmem] * 3,
+        out_specs=[vmem] * 2,
+        compiler_params=pltpu.CompilerParams(vmem_limit_bytes=4 << 20),
+        name="pack",
+    )(at, grads, kept, early)
 
 
 def local(gradients, weight, moment, second, left_gram, left_basis, right_gram, right_basis):
@@ -303,10 +331,9 @@
     right_first = shard * right_rows
     first = core == 0
 
-    gradient = jnp.sum(gather(gradients[0], GRP, n_grp), axis=0) / n_grp
-    moment_new = BETA_ONE * moment + (1.0 - BETA_ONE) * gradient
-    grad_half = gradient.astype(bf16)
-    moment_half = moment_new.astype(bf16)
+    grads = gather(gradients[0], GRP, n_grp)
+    right_pair = right_first // rows * rows
+    at = jnp.stack([right_pair, right_first - right_pair, group, row_first, core]).astype(jnp.int32)
     left_half = left_basis.astype(bf16)
     right_half = right_basis.astype(bf16)
 
@@ -322,7 +349,6 @@
     payload = jnp.concatenate(
         [
             jnp.where(first, left_half[:, :half], left_half[:, half:]),
-            jnp.where(first, grad_half, moment_half),
             fold(jnp.where(first, right_half[:, : width // 2], right_half[:, width // 2 :]), 2),
             fold(jnp.where(first, *pair(right_gram)), 2),
             own_second,
@@ -330,9 +356,11 @@
         ],
         axis=1,
     )
-    cut = payload.shape[1] - SENT * BLOCK
-    payload = gather(payload, ("xhi", "yhi"), NXF * NF)
+    payload, kept = lax.optimization_barrier((payload, BETA_ONE * moment))
+    copies, moment_new = pack_call(at, grads, kept, payload, NXF * NF)
+    payload = lax.all_to_all(copies, ("xhi", "yhi"), 0, 0)
     payload = payload.reshape((NXF, NF) + payload.shape[1:])
+    cut = payload.shape[-1] - SENT * BLOCK
     near, groups = NZ * NY * NXN, cubes()
     parted = lambda v: v.reshape(NEAR + v.shape[1:])
     swap = [(0, 1), (1, 0)]
@@ -340,15 +368,13 @@
     early_other = lax.ppermute(early, "core", swap)
     late = gather(payload[..., cut:], AXES, near, groups)
 
-    right_pair = right_first // rows * rows
-    at = jnp.stack([right_pair, right_first - right_pair, group, row_first, core]).astype(jnp.int32)
     results = mid_call(at, parted(early), parted(early_other), second, left_half, left_gram, right_gram)
-    basis, grad, update, second_new, left_new, right_new, right_result = results
+    basis, outer, update, second_new, left_new, right_new, right_result = results
     update, late = lax.optimization_barrier((update, late))
     late_other = lax.ppermute(late, "core", swap)
     updates = gather(update, GRP, n_grp)
-    basis, grad = (pltpu.with_memory_space_constraint(v, pltpu.HBM) for v in (basis, grad))
-    left_result = left_call(at[3:], parted(late), parted(late_other), grad, basis, rows)
+    basis, outer = (pltpu.with_memory_space_constraint(v, pltpu.HBM) for v in (basis, outer))
+    left_result = left_call(at[3:], parted(late), parted(late_other), outer, basis, rows)
     updates, left_result = lax.optimization_barrier((updates, left_result))
     weight_new = weight - STEP_SIZE * jnp.sum(updates, axis=0)
     return (weight_new, moment_new, second_new, left_new, left_result, right_new, right_result)

time: 130 us -> 129 us (level)
  Pallas kernels: 23.7 us -> 26.1 us
  waiting for transfers between devices: 14 us -> 11.6 us
    all_to_all x2 -> x1, blocking collectives: 55.6 us -> 27.4 us  [gather(): return lax.all_to_all(copies, axes, 0, 0, axis_index_groups=groups)]
    all_to_all x0 -> x1, blocking collectives: none -> 28.2 us  [local(): payload = lax.all_to_all(copies, ('xhi', 'yhi'), 0, 0)]
    all_to_all x3, waiting for transfers between devices: 14 us -> 11.4 us  [gather(): return lax.all_to_all(copies, axes, 0, 0, axis_index_groups=groups)]
    unnamed x4 -> x3, other arithmetic: 1.4 us -> 0.02 us
    broadcast_in_dim x5 -> x4, local copies, waits for them, and re-layouts: 3.85 us -> 3.8 us  [gather(): copies = jnp.broadcast_to(value[None], (size,) + value.shape)]
  transfers between devices with their start and end apart: 5 -> 5, of which waited for: 3 -> 3; matrix products, arithmetic and copies ran while one was open for 5% -> 6% of each run, Pallas kernels for 18% -> 19%
where the time goes in v7:
time: 129 us; the launch traced here: 128 us
  blocking collectives  55.6 us (43%)
  Pallas kernels  26.1 us (20%)
  starting transfers between devices  23.8 us (18%)
  waiting for transfers between devices  11.6 us (9%)
  other arithmetic  5.33 us (4%)
  local copies, waits for them, and re-layouts  4.79 us (4%)
    all_to_all x1, blocking collectives, local(): payload = lax.all_to_all(copies, ('xhi', 'yhi'), 0, 0)  28.2 us
    all_to_all x1, blocking collectives, gather(): return lax.all_to_all(copies, axes, 0, 0, axis_index_groups=groups)  27.4 us
    all_to_all x3, starting transfers between devices, gather(): return lax.all_to_all(copies, axes, 0, 0, axis_index_groups=groups)  19.9 us
    pallas_call x1, Pallas kernels, left_call(): pl.pallas_call(left_kernel, out_shape=jax.ShapeDtypeStruct((rows, deep),...  14.8 us
    all_to_all x3, waiting for transfers between devices, gather(): return lax.all_to_all(copies, axes, 0, 0, axis_index_groups=groups)  11.4 us
    pallas_call x1, Pallas kernels, mid_call(): pl.pallas_call(mid_kernel, out_shape=[pltpu.HBM(*v) for v in shapes[:2]]...  10.1 us
    broadcast_in_dim x4, local copies, waits for them, and re-layouts, gather(): copies = jnp.broadcast_to(value[None], (size,) + value.shape)  3.8 us
  transfers between devices with their start and end apart: 5, of which 3 were waited for; matrix products, arithmetic and copies ran while one was open for 6% of the time, Pallas kernels for 19%

profile of v7, /device:TPU:1, one launch (start us, length us, event | category | flops | bytes accessed | tf_op | source)
XLA Modules:
  0.0 128.0 jit_solution(15879339549339749282)
XLA Ops:
  0.6 1.5 %broadcast_in_dim.11 = f32[8,16,512]{2,1,0:T(8,128)} broadcast(f32[16,512]{1,0:T(8,128)} %bitcast.15), dimensions={1,2} | broadcast | bytes 294912 | tf_op jit(solution)/shard_map/broadcast_in_dim | solution.py:57
  2.1 11.8 %all-to-all-start = ((f32[8,16,512]{2,1,0:T(8,128)}), f32[8,16,512]{2,1,0:T(8,128)S(1)}, u32[]{:S(2)}, u32[]{:S(2)}) async-start(f32[8,16,512]{2,1,0:T(8,128)} %broadcast_in_dim.11), calls=%async_computation | async-start | bytes 524288 | tf_op jit(solution)/shard_map/all_to_all | solution.py:58
  13.9 0.8 convert_element_type.24.left_rows_ref
  14.8 0.7 convert_element_type.25
  15.5 0.7 fusion.6
  16.3 0.7 fusion.7
  17.0 0.8 slice.27
  17.8 0.1 concatenate.18
  17.9 0.8 fusion.3.early_ref
  18.7 0.8 broadcast_multiply_fusion.kept_ref
  19.4 0.1 stack.25.at_ref
  19.5 6.6 %all-to-all-done.grads_ref = f32[8,16,512]{2,1,0:T(8,128)S(1)} async-done(((f32[8,16,512]{2,1,0:T(8,128)}), f32[8,16,512]{2,1,0:T(8,128)S(1)}, u32[]{:S(2)}, u32[]{:S(2)}) %all-to-all-start) | async-done | bytes 262176 | tf_op jit(solution)/shard_map/all_to_all | solution.py:58
  26.1 1.2 pack.1
  27.3 28.2 %all_to_all.25 = bf16[8,16,2176]{2,1,0:T(8,128)(2,1)S(1)} all-to-all(bf16[8,16,2176]{2,1,0:T(8,128)(2,1)S(1)} %get-tuple-element.24), channel_id=1, replica_groups=mesh['zhi'=4,'core'=2,'zlo'=2,'yhi'=4,'ylo'=2,'xhi'=2,'xlo'=2] {'xhi','y..., dimensions={0} | all-to-all | bytes 1114112 | tf_op jit(solution)/shard_map/all_to_all | solution.py:361
  55.6 0.4 broadcast_in_dim.12
  56.0 27.4 %all_to_all.26 = bf16[8,2,4,16,1536]{4,3,2,1,0:T(8,128)(2,1)S(1)} all-to-all(bf16[8,2,4,16,1536]{4,3,2,1,0:T(8,128)(2,1)S(1)} %broadcast_in_dim.12), channel_id=1, replica_groups={{0,1,4,5,32,33,36,37},{2,3,6,7,34,35,38,39},{8,9,12,13,40,41,44,45},{10..., dimensions={0} | all-to-all | bytes 6291456 | tf_op jit(solution)/shard_map/all_to_all | solution.py:58
  83.4 0.0 copy-start
  83.4 0.0 copy-start.1
  83.4 0.0 copy-start.2
  83.4 2.0 %collective-permute-start = (bf16[8,2,4,16,1536]{4,3,2,1,0:T(8,128)(2,1)S(1)}, bf16[8,2,4,16,1536]{4,3,2,1,0:T(8,128)(2,1)}, u32[]{:S(2)}, u32[]{:S(2)}) collective-permute-start(bf16[8,2,4,16,1536]{4,3,2,1,0:T(8,128)(2,1)S(1)} %all_to_all.26), channel_id=1, source_target_pairs={{0,64},{64,0},{1,65},{65,1},{2,66},{66,2},{3,67},{67,3},{4,68},{68... | collective-permute-start | bytes 9437192 | tf_op jit(solution)/shard_map/ppermute | solution.py:368
  85.4 1.2 broadcast_in_dim.13
  86.7 4.3 %all-to-all-start.3 = ((bf16[8,2,4,16,640]{4,3,2,1,0:T(8,128)(2,1)}), bf16[8,2,4,16,640]{4,3,2,1,0:T(8,128)(2,1)}, u32[]{:S(2)}, u32[]{:S(2)}) async-start(bf16[8,2,4,16,640]{4,3,2,1,0:T(8,128)(2,1)} %broadcast_in_dim.13), calls=%async_computation.3 | async-start | bytes 2621440 | tf_op jit(solution)/shard_map/all_to_all | solution.py:58
  90.9 0.2 collective-permute-done
  91.2 0.0 copy-done
  91.2 0.0 copy-done.1
  91.2 0.0 copy-done.2
  91.2 10.1 %middle.1 = (bf16[1024,1024]{1,0:T(8,128)(2,1)}, f32[1024,1024]{1,0:T(8,128)}, f32[16,512]{1,0:T(8,128)S(1)}, f32[16,512]{1,0:T(8,128)}, f32[16,1024]{1,0:T(8,128)}, /*index=5*/f32[8,512]{1,0:T(8,128)}, f32[8,512]{1,0:T(8,128)}) custom-call(s32[5]{0:T(128)S(1)} %stack.25.at_ref, bf16[2,2,2,2,4,16,1536]{6,5,4,3,2,1,0:T(8,128)(2,1)S(1)} %bitcast.11, ...), custom_call_target="tpu_custom_call" | custom-call | flops 6442450944 | bytes 12582912 | tf_op jit(solution)/shard_map/middle/pallas_call | solution.py:265
  101.3 4.8 %all-to-all-done.3 = bf16[8,2,4,16,640]{4,3,2,1,0:T(8,128)(2,1)} async-done(((bf16[8,2,4,16,640]{4,3,2,1,0:T(8,128)(2,1)}), bf16[8,2,4,16,640]{4,3,2,1,0:T(8,128)(2,1)}, u32[]{:S(2)}, u32[]{:S(2)}) %all-to-all-start.3) | async-done | bytes 1310752 | tf_op jit(solution)/shard_map/all_to_all | solution.py:58
  106.0 1.9 %collective-permute-start.1 = (bf16[8,2,4,16,640]{4,3,2,1,0:T(8,128)(2,1)}, bf16[8,2,4,16,640]{4,3,2,1,0:T(8,128)(2,1)S(1)}, u32[]{:S(2)}, u32[]{:S(2)}) collective-permute-start(bf16[8,2,4,16,640]{4,3,2,1,0:T(8,128)(2,1)} %all-to-all-done.3), channel_id=1, source_target_pairs={{0,64},{64,0},{1,65},{65,1},{2,66},{66,2},{3,67},{67,3},{4,68},{68... | collective-permute-start | bytes 3932168 | tf_op jit(solution)/shard_map/ppermute | solution.py:374
  107.9 0.1 pad_add_fusion.first_ref
  108.0 0.7 broadcast_in_dim.14
  108.7 3.8 %all-to-all-start.4 = ((f32[8,16,512]{2,1,0:T(8,128)}), f32[8,16,512]{2,1,0:T(8,128)S(1)}, u32[]{:S(2)}, u32[]{:S(2)}) async-start(f32[8,16,512]{2,1,0:T(8,128)} %broadcast_in_dim.14), calls=%async_computation.4 | async-start | bytes 524288 | tf_op jit(solution)/shard_map/all_to_all | solution.py:58
  112.6 0.0 collective-permute-done.1
  112.6 0.0 copy-start.3
  112.6 14.8 %left_refresh.1 = f32[16,1024]{1,0:T(8,128)} custom-call(s32[2]{0:T(128)S(1)} %pad_add_fusion.first_ref, bf16[2,2,2,2,4,16,640]{6,5,4,3,2,1,0:T(8,128)(2,1)} %bitcast.9.mine_hbm, bf16[2,2,2,2,4,16,640]{6,5,4,3,2,1,0:T(8,128)(2,1)S(1)} %bitcast.12, f32[1024,1024]{1,0:T(8,128)} %get-tuple-element.28.outer_hbm, bf16[1024,1024]{1,0:T(8,128)(2,1)} %get-tuple-element.29.basis_hbm), custom_call_target="tpu_custom_call" | custom-call | flops 10737418240 | bytes 8388608 | tf_op jit(solution)/shard_map/left_refresh/pallas_call | solution.py:137
  127.4 0.0 all-to-all-done.4
  127.4 0.0 copy-done.3
  127.4 0.6 multiply_subtract_fusion
  (11 shorter events, 0.1 us)
Async XLA Ops:
  2.1 24.0 %all-to-all-start = ((f32[8,16,512]{2,1,0:T(8,128)}), f32[8,16,512]{2,1,0:T(8,128)S(1)}, u32[]{:S(2)}, u32[]{:S(2)}) async-start(f32[8,16,512]{2,1,0:T(8,128)} %broadcast_in_dim.11), calls=%async_computation | async-start | bytes 524288 | tf_op jit(solution)/shard_map/all_to_all | solution.py:58
  83.4 7.8 %copy-start = (f32[16,1024]{1,0:T(8,128)S(1)}, f32[16,1024]{1,0:T(8,128)}, u32[]{:S(2)}) copy-start(f32[16,1024]{1,0:T(8,128)} %left_gram_ref.1) | copy-start | bytes 196612
  83.4 7.8 %copy-start.1 = (f32[8,512]{1,0:T(8,128)S(1)}, f32[8,512]{1,0:T(8,128)}, u32[]{:S(2)}) copy-start(f32[8,512]{1,0:T(8,128)} %right_gram_ref.1) | copy-start | bytes 49156
  83.4 7.8 %copy-start.2 = (f32[16,512]{1,0:T(8,128)S(1)}, f32[16,512]{1,0:T(8,128)}, u32[]{:S(2)}) copy-start(f32[16,512]{1,0:T(8,128)} %second_ref.1) | copy-start | bytes 98308
  83.4 7.8 %collective-permute-start = (bf16[8,2,4,16,1536]{4,3,2,1,0:T(8,128)(2,1)S(1)}, bf16[8,2,4,16,1536]{4,3,2,1,0:T(8,128)(2,1)}, u32[]{:S(2)}, u32[]{:S(2)}) collective-permute-start(bf16[8,2,4,16,1536]{4,3,2,1,0:T(8,128)(2,1)S(1)} %all_to_all.26), channel_id=1, source_target_pairs={{0,64},{64,0},{1,65},{65,1},{2,66},{66,2},{3,67},{67,3},{4,68},{68... | collective-permute-start | bytes 9437192 | tf_op jit(solution)/shard_map/ppermute | solution.py:368
  86.7 19.4 %all-to-all-start.3 = ((bf16[8,2,4,16,640]{4,3,2,1,0:T(8,128)(2,1)}), bf16[8,2,4,16,640]{4,3,2,1,0:T(8,128)(2,1)}, u32[]{:S(2)}, u32[]{:S(2)}) async-start(bf16[8,2,4,16,640]{4,3,2,1,0:T(8,128)(2,1)} %broadcast_in_dim.13), calls=%async_computation.3 | async-start | bytes 2621440 | tf_op jit(solution)/shard_map/all_to_all | solution.py:58
  106.0 6.5 %collective-permute-start.1 = (bf16[8,2,4,16,640]{4,3,2,1,0:T(8,128)(2,1)}, bf16[8,2,4,16,640]{4,3,2,1,0:T(8,128)(2,1)S(1)}, u32[]{:S(2)}, u32[]{:S(2)}) collective-permute-start(bf16[8,2,4,16,640]{4,3,2,1,0:T(8,128)(2,1)} %all-to-all-done.3), channel_id=1, source_target_pairs={{0,64},{64,0},{1,65},{65,1},{2,66},{66,2},{3,67},{67,3},{4,68},{68... | collective-permute-start | bytes 3932168 | tf_op jit(solution)/shard_map/ppermute | solution.py:374
  108.7 18.6 %all-to-all-start.4 = ((f32[8,16,512]{2,1,0:T(8,128)}), f32[8,16,512]{2,1,0:T(8,128)S(1)}, u32[]{:S(2)}, u32[]{:S(2)}) async-start(f32[8,16,512]{2,1,0:T(8,128)} %broadcast_in_dim.14), calls=%async_computation.4 | async-start | bytes 524288 | tf_op jit(solution)/shard_map/all_to_all | solution.py:58
  112.6 14.8 %copy-start.3 = (f32[16,512]{1,0:T(8,128)S(1)}, f32[16,512]{1,0:T(8,128)}, u32[]{:S(2)}) copy-start(f32[16,512]{1,0:T(8,128)} %param.9) | copy-start | bytes 98308

commit v8 on v7

--- a/solution.py
+++ b/solution.py
@@ -92,16 +92,18 @@
 
 
 def left_kernel(
-    first_ref, mine_hbm, other_hbm, outer_hbm, basis_hbm, out_ref,
-    mine_ref, other_ref, basis_ref, gram, power, start, current, sems,
+    first_ref, mine_hbm, other_ref, outer_hbm, basis_hbm, out_ref,
+    mine_ref, basis_ref, gram, power, start, current, sems,
 ):
-    pairs = ((mine_hbm, mine_ref), (other_hbm, other_ref), (outer_hbm, power), (basis_hbm, basis_ref))
+    rows, deep, tile = mine_ref.shape[-2], basis_ref.shape[0], 256
+    pairs = [(mine_hbm, mine_ref), (basis_hbm, basis_ref)]
+    for t in range(deep // tile):
+        at = pl.ds(t * tile, tile)
+        pairs.append((outer_hbm.at[at], power.at[at]))
     copies = [pltpu.make_async_copy(a, b, sems.at[i]) for i, (a, b) in enumerate(pairs)]
     for copy in copies:
         copy.start()
-    rows, deep, tile = mine_ref.shape[-2], basis_ref.shape[0], 256
     copies[0].wait()
-    copies[1].wait()
     for r in range(BLOCKS):
         zlo, far = r // NF, r % NF
         for j in range(SENT):
@@ -116,11 +118,11 @@
             gram[r * BLOCK : (r + 1) * BLOCK, c * BLOCK : (c + 1) * BLOCK] = block
             if 0 < j < BLOCKS // 2:
                 gram[c * BLOCK : (c + 1) * BLOCK, r * BLOCK : (r + 1) * BLOCK] = block.T
-    copies[2].wait()
-    copies[3].wait()
+    copies[1].wait()
     basis = basis_ref[...]
 
     def power_tile(t):
+        copies[2 + t].wait()
         at = pl.ds(t * tile, tile)
         high, low = split(gram[at, :] + power[at, :])
         return mm(high, basis, 1, 0) + mm(low, basis, 1, 0)
@@ -134,18 +136,19 @@
     deep = basis.shape[0]
     hbm = pl.BlockSpec(memory_space=pltpu.HBM)
     anywhere = pl.BlockSpec(memory_space=pl.ANY)
+    vmem = pl.BlockSpec(memory_space=pltpu.VMEM)
     return pl.pallas_call(
         left_kernel,
         out_shape=jax.ShapeDtypeStruct((rows, deep), f32),
-        in_specs=[pl.BlockSpec(memory_space=pltpu.SMEM), anywhere, anywhere, hbm, hbm],
-        out_specs=pl.BlockSpec(memory_space=pltpu.VMEM),
-        scratch_shapes=[pltpu.VMEM(v.shape, bf16) for v in (mine, other, basis)]
+        in_specs=[pl.BlockSpec(memory_space=pltpu.SMEM), anywhere, vmem, hbm, hbm],
+        out_specs=vmem,
+        scratch_shapes=[pltpu.VMEM(v.shape, bf16) for v in (mine, basis)]
         + [
             pltpu.VMEM((deep, deep), f32),
             pltpu.VMEM((deep, deep), f32),
             pltpu.VMEM((deep, deep), bf16),
             pltpu.VMEM((deep, deep), bf16),
-            pltpu.SemaphoreType.DMA((4,)),
+            pltpu.SemaphoreType.DMA((2 + deep // 256,)),
         ],
         compiler_params=pltpu.CompilerParams(vmem_limit_bytes=28 << 20),
         cost_estimate=pl.CostEstimate(flops=10 * deep**3, transcendentals=deep, bytes_accessed=8 * deep**2),

time: 129 us -> 128 us (level)
  no operation moved by 1% of the time
where the time goes in v8:
time: 128 us; the launch traced here: 127 us
  blocking collectives  55.6 us (43%)
  Pallas kernels  25.2 us (20%)
  starting transfers between devices  23.8 us (19%)
  waiting for transfers between devices  11.6 us (9%)
  other arithmetic  5.33 us (4%)
  local copies, waits for them, and re-layouts  4.79 us (4%)
    all_to_all x1, blocking collectives, local(): payload = lax.all_to_all(copies, ('xhi', 'yhi'), 0, 0)  28.2 us
    all_to_all x1, blocking collectives, gather(): return lax.all_to_all(copies, axes, 0, 0, axis_index_groups=groups)  27.4 us
    all_to_all x3, starting transfers between devices, gather(): return lax.all_to_all(copies, axes, 0, 0, axis_index_groups=groups)  19.9 us
    pallas_call x1, Pallas kernels, left_call(): pl.pallas_call(left_kernel, out_shape=jax.ShapeDtypeStruct((rows, deep),...  13.9 us
    all_to_all x3, waiting for transfers between devices, gather(): return lax.all_to_all(copies, axes, 0, 0, axis_index_groups=groups)  11.4 us
    pallas_call x1, Pallas kernels, mid_call(): pl.pallas_call(mid_kernel, out_shape=[pltpu.HBM(*v) for v in shapes[:2]]...  10.1 us
    broadcast_in_dim x4, local copies, waits for them, and re-layouts, gather(): copies = jnp.broadcast_to(value[None], (size,) + value.shape)  3.8 us
  transfers between devices with their start and end apart: 5, of which 3 were waited for; matrix products, arithmetic and copies ran while one was open for 6% of the time, Pallas kernels for 19%

profile of v8, /device:TPU:1, one launch (start us, length us, event | category | flops | bytes accessed | tf_op | source)
XLA Modules:
  0.0 127.2 jit_solution(16282773065503745756)
XLA Ops:
  0.6 1.5 %broadcast_in_dim.11 = f32[8,16,512]{2,1,0:T(8,128)} broadcast(f32[16,512]{1,0:T(8,128)} %bitcast.15), dimensions={1,2} | broadcast | bytes 294912 | tf_op jit(solution)/shard_map/broadcast_in_dim | solution.py:57
  2.1 11.8 %all-to-all-start = ((f32[8,16,512]{2,1,0:T(8,128)}), f32[8,16,512]{2,1,0:T(8,128)S(1)}, u32[]{:S(2)}, u32[]{:S(2)}) async-start(f32[8,16,512]{2,1,0:T(8,128)} %broadcast_in_dim.11), calls=%async_computation | async-start | bytes 524288 | tf_op jit(solution)/shard_map/all_to_all | solution.py:58
  13.9 0.8 convert_element_type.24.left_rows_ref
  14.8 0.7 convert_element_type.25
  15.5 0.7 fusion.6
  16.3 0.7 fusion.7
  17.0 0.8 slice.27
  17.8 0.1 concatenate.18
  17.9 0.8 fusion.3.early_ref
  18.7 0.8 broadcast_multiply_fusion.kept_ref
  19.4 0.1 stack.25.at_ref
  19.5 6.6 %all-to-all-done.grads_ref = f32[8,16,512]{2,1,0:T(8,128)S(1)} async-done(((f32[8,16,512]{2,1,0:T(8,128)}), f32[8,16,512]{2,1,0:T(8,128)S(1)}, u32[]{:S(2)}, u32[]{:S(2)}) %all-to-all-start) | async-done | bytes 262176 | tf_op jit(solution)/shard_map/all_to_all | solution.py:58
  26.1 1.2 pack.1
  27.3 28.2 %all_to_all.25 = bf16[8,16,2176]{2,1,0:T(8,128)(2,1)S(1)} all-to-all(bf16[8,16,2176]{2,1,0:T(8,128)(2,1)S(1)} %get-tuple-element.24), channel_id=1, replica_groups=mesh['zhi'=4,'core'=2,'zlo'=2,'yhi'=4,'ylo'=2,'xhi'=2,'xlo'=2] {'xhi','y..., dimensions={0} | all-to-all | bytes 1114112 | tf_op jit(solution)/shard_map/all_to_all | solution.py:364
  55.6 0.4 broadcast_in_dim.12
  56.0 27.4 %all_to_all.26 = bf16[8,2,4,16,1536]{4,3,2,1,0:T(8,128)(2,1)S(1)} all-to-all(bf16[8,2,4,16,1536]{4,3,2,1,0:T(8,128)(2,1)S(1)} %broadcast_in_dim.12), channel_id=1, replica_groups={{0,1,4,5,32,33,36,37},{2,3,6,7,34,35,38,39},{8,9,12,13,40,41,44,45},{10..., dimensions={0} | all-to-all | bytes 6291456 | tf_op jit(solution)/shard_map/all_to_all | solution.py:58
  83.4 0.0 copy-start
  83.4 0.0 copy-start.1
  83.4 0.0 copy-start.2
  83.4 2.0 %collective-permute-start = (bf16[8,2,4,16,1536]{4,3,2,1,0:T(8,128)(2,1)S(1)}, bf16[8,2,4,16,1536]{4,3,2,1,0:T(8,128)(2,1)}, u32[]{:S(2)}, u32[]{:S(2)}) collective-permute-start(bf16[8,2,4,16,1536]{4,3,2,1,0:T(8,128)(2,1)S(1)} %all_to_all.26), channel_id=1, source_target_pairs={{0,64},{64,0},{1,65},{65,1},{2,66},{66,2},{3,67},{67,3},{4,68},{68... | collective-permute-start | bytes 9437192 | tf_op jit(solution)/shard_map/ppermute | solution.py:371
  85.4 1.2 broadcast_in_dim.13
  86.7 4.3 %all-to-all-start.3 = ((bf16[8,2,4,16,640]{4,3,2,1,0:T(8,128)(2,1)}), bf16[8,2,4,16,640]{4,3,2,1,0:T(8,128)(2,1)}, u32[]{:S(2)}, u32[]{:S(2)}) async-start(bf16[8,2,4,16,640]{4,3,2,1,0:T(8,128)(2,1)} %broadcast_in_dim.13), calls=%async_computation.3 | async-start | bytes 2621440 | tf_op jit(solution)/shard_map/all_to_all | solution.py:58
  90.9 0.2 collective-permute-done
  91.2 0.0 copy-done
  91.2 0.0 copy-done.1
  91.2 0.0 copy-done.2
  91.2 10.1 %middle.1 = (bf16[1024,1024]{1,0:T(8,128)(2,1)}, f32[1024,1024]{1,0:T(8,128)}, f32[16,512]{1,0:T(8,128)S(1)}, f32[16,512]{1,0:T(8,128)}, f32[16,1024]{1,0:T(8,128)}, /*index=5*/f32[8,512]{1,0:T(8,128)}, f32[8,512]{1,0:T(8,128)}) custom-call(s32[5]{0:T(128)S(1)} %stack.25.at_ref, bf16[2,2,2,2,4,16,1536]{6,5,4,3,2,1,0:T(8,128)(2,1)S(1)} %bitcast.11, ...), custom_call_target="tpu_custom_call" | custom-call | flops 6442450944 | bytes 12582912 | tf_op jit(solution)/shard_map/middle/pallas_call | solution.py:268
  101.3 4.8 %all-to-all-done.3 = bf16[8,2,4,16,640]{4,3,2,1,0:T(8,128)(2,1)} async-done(((bf16[8,2,4,16,640]{4,3,2,1,0:T(8,128)(2,1)}), bf16[8,2,4,16,640]{4,3,2,1,0:T(8,128)(2,1)}, u32[]{:S(2)}, u32[]{:S(2)}) %all-to-all-start.3) | async-done | bytes 1310752 | tf_op jit(solution)/shard_map/all_to_all | solution.py:58
  106.0 1.9 %collective-permute-start.1 = (bf16[8,2,4,16,640]{4,3,2,1,0:T(8,128)(2,1)}, bf16[8,2,4,16,640]{4,3,2,1,0:T(8,128)(2,1)S(1)}, u32[]{:S(2)}, u32[]{:S(2)}) collective-permute-start(bf16[8,2,4,16,640]{4,3,2,1,0:T(8,128)(2,1)} %all-to-all-done.3), channel_id=1, source_target_pairs={{0,64},{64,0},{1,65},{65,1},{2,66},{66,2},{3,67},{67,3},{4,68},{68... | collective-permute-start | bytes 3932168 | tf_op jit(solution)/shard_map/ppermute | solution.py:377
  107.9 0.1 pad_add_fusion.first_ref
  108.0 0.7 broadcast_in_dim.14
  108.7 3.8 %all-to-all-start.4 = ((f32[8,16,512]{2,1,0:T(8,128)}), f32[8,16,512]{2,1,0:T(8,128)S(1)}, u32[]{:S(2)}, u32[]{:S(2)}) async-start(f32[8,16,512]{2,1,0:T(8,128)} %broadcast_in_dim.14), calls=%async_computation.4 | async-start | bytes 524288 | tf_op jit(solution)/shard_map/all_to_all | solution.py:58
  112.6 0.0 collective-permute-done.1
  112.6 0.0 copy-start.3
  112.6 13.9 %left_refresh.1 = f32[16,1024]{1,0:T(8,128)} custom-call(s32[2]{0:T(128)S(1)} %pad_add_fusion.first_ref, bf16[2,2,2,2,4,16,640]{6,5,4,3,2,1,0:T(8,128)(2,1)} %bitcast.9.mine_hbm, bf16[2,2,2,2,4,16,640]{6,5,4,3,2,1,0:T(8,128)(2,1)S(1)} %bitcast.12, f32[1024,1024]{1,0:T(8,128)} %get-tuple-element.28.outer_hbm, bf16[1024,1024]{1,0:T(8,128)(2,1)} %get-tuple-element.29.basis_hbm), custom_call_target="tpu_custom_call" | custom-call | flops 10737418240 | bytes 8388608 | tf_op jit(solution)/shard_map/left_refresh/pallas_call | solution.py:140
  126.5 0.0 all-to-all-done.4
  126.5 0.0 copy-done.3
  126.5 0.6 multiply_subtract_fusion
  (11 shorter events, 0.1 us)
Async XLA Ops:
  2.1 24.0 %all-to-all-start = ((f32[8,16,512]{2,1,0:T(8,128)}), f32[8,16,512]{2,1,0:T(8,128)S(1)}, u32[]{:S(2)}, u32[]{:S(2)}) async-start(f32[8,16,512]{2,1,0:T(8,128)} %broadcast_in_dim.11), calls=%async_computation | async-start | bytes 524288 | tf_op jit(solution)/shard_map/all_to_all | solution.py:58
  83.4 7.8 %copy-start = (f32[16,1024]{1,0:T(8,128)S(1)}, f32[16,1024]{1,0:T(8,128)}, u32[]{:S(2)}) copy-start(f32[16,1024]{1,0:T(8,128)} %left_gram_ref.1) | copy-start | bytes 196612
  83.4 7.8 %copy-start.1 = (f32[8,512]{1,0:T(8,128)S(1)}, f32[8,512]{1,0:T(8,128)}, u32[]{:S(2)}) copy-start(f32[8,512]{1,0:T(8,128)} %right_gram_ref.1) | copy-start | bytes 49156
  83.4 7.8 %copy-start.2 = (f32[16,512]{1,0:T(8,128)S(1)}, f32[16,512]{1,0:T(8,128)}, u32[]{:S(2)}) copy-start(f32[16,512]{1,0:T(8,128)} %second_ref.1) | copy-start | bytes 98308
  83.4 7.8 %collective-permute-start = (bf16[8,2,4,16,1536]{4,3,2,1,0:T(8,128)(2,1)S(1)}, bf16[8,2,4,16,1536]{4,3,2,1,0:T(8,128)(2,1)}, u32[]{:S(2)}, u32[]{:S(2)}) collective-permute-start(bf16[8,2,4,16,1536]{4,3,2,1,0:T(8,128)(2,1)S(1)} %all_to_all.26), channel_id=1, source_target_pairs={{0,64},{64,0},{1,65},{65,1},{2,66},{66,2},{3,67},{67,3},{4,68},{68... | collective-permute-start | bytes 9437192 | tf_op jit(solution)/shard_map/ppermute | solution.py:371
  86.7 19.4 %all-to-all-start.3 = ((bf16[8,2,4,16,640]{4,3,2,1,0:T(8,128)(2,1)}), bf16[8,2,4,16,640]{4,3,2,1,0:T(8,128)(2,1)}, u32[]{:S(2)}, u32[]{:S(2)}) async-start(bf16[8,2,4,16,640]{4,3,2,1,0:T(8,128)(2,1)} %broadcast_in_dim.13), calls=%async_computation.3 | async-start | bytes 2621440 | tf_op jit(solution)/shard_map/all_to_all | solution.py:58
  106.0 6.5 %collective-permute-start.1 = (bf16[8,2,4,16,640]{4,3,2,1,0:T(8,128)(2,1)}, bf16[8,2,4,16,640]{4,3,2,1,0:T(8,128)(2,1)S(1)}, u32[]{:S(2)}, u32[]{:S(2)}) collective-permute-start(bf16[8,2,4,16,640]{4,3,2,1,0:T(8,128)(2,1)} %all-to-all-done.3), channel_id=1, source_target_pairs={{0,64},{64,0},{1,65},{65,1},{2,66},{66,2},{3,67},{67,3},{4,68},{68... | collective-permute-start | bytes 3932168 | tf_op jit(solution)/shard_map/ppermute | solution.py:377
  108.7 17.7 %all-to-all-start.4 = ((f32[8,16,512]{2,1,0:T(8,128)}), f32[8,16,512]{2,1,0:T(8,128)S(1)}, u32[]{:S(2)}, u32[]{:S(2)}) async-start(f32[8,16,512]{2,1,0:T(8,128)} %broadcast_in_dim.14), calls=%async_computation.4 | async-start | bytes 524288 | tf_op jit(solution)/shard_map/all_to_all | solution.py:58
  112.6 14.0 %copy-start.3 = (f32[16,512]{1,0:T(8,128)S(1)}, f32[16,512]{1,0:T(8,128)}, u32[]{:S(2)}) copy-start(f32[16,512]{1,0:T(8,128)} %param.9) | copy-start | bytes 98308

commit v9 on v8

--- a/solution.py
+++ b/solution.py
@@ -92,11 +92,13 @@
 
 
 def left_kernel(
-    first_ref, mine_hbm, other_ref, outer_hbm, basis_hbm, out_ref,
-    mine_ref, basis_ref, gram, power, start, current, sems,
+    first_ref, mine_hbm, other_hbm, outer_hbm, basis_hbm, out_ref,
+    mine_ref, other_ref, basis_ref, gram, power, start, current, sems,
 ):
     rows, deep, tile = mine_ref.shape[-2], basis_ref.shape[0], 256
-    pairs = [(mine_hbm, mine_ref), (basis_hbm, basis_ref)]
+    part = pl.ds(mine_hbm.shape[-1] - SENT * BLOCK, SENT * BLOCK)
+    lead = (slice(None),) * (len(mine_hbm.shape) - 1)
+    pairs = [(mine_hbm.at[lead + (part,)], mine_ref), (other_hbm.at[lead + (part,)], other_ref), (basis_hbm, basis_ref)]
     for t in range(deep // tile):
         at = pl.ds(t * tile, tile)
         pairs.append((outer_hbm.at[at], power.at[at]))
@@ -104,6 +106,7 @@
     for copy in copies:
         copy.start()
     copies[0].wait()
+    copies[1].wait()
     for r in range(BLOCKS):
         zlo, far = r // NF, r % NF
         for j in range(SENT):
@@ -118,11 +121,11 @@
             gram[r * BLOCK : (r + 1) * BLOCK, c * BLOCK : (c + 1) * BLOCK] = block
             if 0 < j < BLOCKS // 2:
                 gram[c * BLOCK : (c + 1) * BLOCK, r * BLOCK : (r + 1) * BLOCK] = block.T
-    copies[1].wait()
+    copies[2].wait()
     basis = basis_ref[...]
 
     def power_tile(t):
-        copies[2 + t].wait()
+        copies[3 + t].wait()
         at = pl.ds(t * tile, tile)
         high, low = split(gram[at, :] + power[at, :])
         return mm(high, basis, 1, 0) + mm(low, basis, 1, 0)
@@ -135,20 +138,20 @@
 def left_call(first, mine, other, outer, basis, rows):
     deep = basis.shape[0]
     hbm = pl.BlockSpec(memory_space=pltpu.HBM)
-    anywhere = pl.BlockSpec(memory_space=pl.ANY)
     vmem = pl.BlockSpec(memory_space=pltpu.VMEM)
     return pl.pallas_call(
         left_kernel,
         out_shape=jax.ShapeDtypeStruct((rows, deep), f32),
-        in_specs=[pl.BlockSpec(memory_space=pltpu.SMEM), anywhere, vmem, hbm, hbm],
+        in_specs=[pl.BlockSpec(memory_space=pltpu.SMEM)] + [hbm] * 4,
         out_specs=vmem,
-        scratch_shapes=[pltpu.VMEM(v.shape, bf16) for v in (mine, basis)]
+        scratch_shapes=[pltpu.VMEM(mine.shape[:-1] + (SENT * BLOCK,), bf16)] * 2
+        + [pltpu.VMEM(basis.shape, bf16)]
         + [
             pltpu.VMEM((deep, deep), f32),
             pltpu.VMEM((deep, deep), f32),
             pltpu.VMEM((deep, deep), bf16),
             pltpu.VMEM((deep, deep), bf16),
-            pltpu.SemaphoreType.DMA((2 + deep // 256,)),
+            pltpu.SemaphoreType.DMA((3 + deep // 256,)),
         ],
         compiler_params=pltpu.CompilerParams(vmem_limit_bytes=28 << 20),
         cost_estimate=pl.CostEstimate(flops=10 * deep**3, transcendentals=deep, bytes_accessed=8 * deep**2),
@@ -363,21 +366,17 @@
     copies, moment_new = pack_call(at, grads, kept, payload, NXF * NF)
     payload = lax.all_to_all(copies, ("xhi", "yhi"), 0, 0)
     payload = payload.reshape((NXF, NF) + payload.shape[1:])
-    cut = payload.shape[-1] - SENT * BLOCK
     near, groups = NZ * NY * NXN, cubes()
     parted = lambda v: v.reshape(NEAR + v.shape[1:])
     swap = [(0, 1), (1, 0)]
-    early = gather(payload[..., :cut], AXES, near, groups)
-    early_other = lax.ppermute(early, "core", swap)
-    late = gather(payload[..., cut:], AXES, near, groups)
-
-    results = mid_call(at, parted(early), parted(early_other), second, left_half, left_gram, right_gram)
+    whole = parted(gather(payload, AXES, near, groups))
+    other = lax.ppermute(whole, "core", swap)
+
+    results = mid_call(at, whole, other, second, left_half, left_gram, right_gram)
     basis, outer, update, second_new, left_new, right_new, right_result = results
-    update, late = lax.optimization_barrier((update, late))
-    late_other = lax.ppermute(late, "core", swap)
     updates = gather(update, GRP, n_grp)
-    basis, outer = (pltpu.with_memory_space_constraint(v, pltpu.HBM) for v in (basis, outer))
-    left_result = left_call(at[3:], parted(late), parted(late_other), outer, basis, rows)
+    whole, other, basis, outer = (pltpu.with_memory_space_constraint(v, pltpu.HBM) for v in (whole, other, basis, outer))
+    left_result = left_call(at[3:], whole, other, outer, basis, rows)
     updates, left_result = lax.optimization_barrier((updates, left_result))
     weight_new = weight - STEP_SIZE * jnp.sum(updates, axis=0)
     return (weight_new, moment_new, second_new, left_new, left_result, right_new, right_result)

time: 128 us -> 129 us (level)
  blocking collectives: 55.6 us -> 62.8 us
  starting transfers between devices: 23.8 us -> 17.3 us
  waiting for transfers between devices: 11.6 us -> 14 us
    ppermute x2 -> x1, waiting for transfers between devices: 0.24 us -> 7.42 us  [local(): other = lax.ppermute(whole, 'core', swap)]
    all_to_all x1, blocking collectives: 27.4 us -> 34.6 us  [gather(): return lax.all_to_all(copies, axes, 0, 0, axis_index_groups=groups)]
    all_to_all x3 -> x2, waiting for transfers between devices: 11.4 us -> 6.58 us  [gather(): return lax.all_to_all(copies, axes, 0, 0, axis_index_groups=groups)]
    all_to_all x3 -> x2, starting transfers between devices: 19.9 us -> 15.3 us  [gather(): return lax.all_to_all(copies, axes, 0, 0, axis_index_groups=groups)]
    ppermute x2 -> x1, starting transfers between devices: 3.95 us -> 1.91 us  [local(): other = lax.ppermute(whole, 'core', swap)]
    pallas_call x1, Pallas kernels: 10.1 us -> 8.75 us  [mid_call(): pl.pallas_call(mid_kernel, out_shape=[pltpu.HBM(*v) for v in shapes[:2]]...]
    broadcast_in_dim x4 -> x3, local copies, waits for them, and re-layouts: 3.8 us -> 2.67 us  [gather(): copies = jnp.broadcast_to(value[None], (size,) + value.shape)]
  transfers between devices with their start and end apart: 5 -> 3, of which waited for: 3 -> 2; matrix products, arithmetic and copies ran while one was open for 6% -> 4% of each run, Pallas kernels for 19% -> 11%
where the time goes in v9:
time: 129 us; the launch traced here: 128 us
  blocking collectives  62.8 us (49%)
  Pallas kernels  24.3 us (19%)
  starting transfers between devices  17.3 us (13%)
  waiting for transfers between devices  14 us (11%)
  other arithmetic  5.33 us (4%)
  local copies, waits for them, and re-layouts  3.64 us (3%)
    all_to_all x1, blocking collectives, gather(): return lax.all_to_all(copies, axes, 0, 0, axis_index_groups=groups)  34.6 us
    all_to_all x1, blocking collectives, local(): payload = lax.all_to_all(copies, ('xhi', 'yhi'), 0, 0)  28.2 us
    all_to_all x2, starting transfers between devices, gather(): return lax.all_to_all(copies, axes, 0, 0, axis_index_groups=groups)  15.3 us
    pallas_call x1, Pallas kernels, left_call(): pl.pallas_call(left_kernel, out_shape=jax.ShapeDtypeStruct((rows, deep),...  14.4 us
    pallas_call x1, Pallas kernels, mid_call(): pl.pallas_call(mid_kernel, out_shape=[pltpu.HBM(*v) for v in shapes[:2]]...  8.75 us
    ppermute x1, waiting for transfers between devices, local(): other = lax.ppermute(whole, 'core', swap)  7.42 us
    all_to_all x2, waiting for transfers between devices, gather(): return lax.all_to_all(copies, axes, 0, 0, axis_index_groups=groups)  6.58 us
    broadcast_in_dim x3, local copies, waits for them, and re-layouts, gather(): copies = jnp.broadcast_to(value[None], (size,) + value.shape)  2.67 us
  transfers between devices with their start and end apart: 3, of which 2 were waited for; matrix products, arithmetic and copies ran while one was open for 4% of the time, Pallas kernels for 11%

profile of v9, /device:TPU:1, one launch (start us, length us, event | category | flops | bytes accessed | tf_op | source)
XLA Modules:
  0.0 128.2 jit_solution(16577477438188618255)
XLA Ops:
  0.6 1.5 %broadcast_in_dim.21 = f32[8,16,512]{2,1,0:T(8,128)} broadcast(f32[16,512]{1,0:T(8,128)} %bitcast.12), dimensions={1,2} | broadcast | bytes 294912 | tf_op jit(solution)/shard_map/broadcast_in_dim | solution.py:57
  2.1 11.8 %all-to-all-start = ((f32[8,16,512]{2,1,0:T(8,128)}), f32[8,16,512]{2,1,0:T(8,128)S(1)}, u32[]{:S(2)}, u32[]{:S(2)}) async-start(f32[8,16,512]{2,1,0:T(8,128)} %broadcast_in_dim.21), calls=%async_computation | async-start | bytes 524288 | tf_op jit(solution)/shard_map/all_to_all | solution.py:58
  13.9 0.7 convert_element_type.25
  14.7 0.7 fusion.6
  15.4 0.8 convert_element_type.24.left_rows_ref
  16.2 0.7 fusion.7
  17.1 0.8 slice.21
  17.8 0.1 concatenate.18
  17.9 0.8 fusion.3.early_ref
  18.7 0.8 broadcast_multiply_fusion.kept_ref
  19.5 0.1 stack.25.at_ref
  19.5 6.6 %all-to-all-done.grads_ref = f32[8,16,512]{2,1,0:T(8,128)S(1)} async-done(((f32[8,16,512]{2,1,0:T(8,128)}), f32[8,16,512]{2,1,0:T(8,128)S(1)}, u32[]{:S(2)}, u32[]{:S(2)}) %all-to-all-start) | async-done | bytes 262176 | tf_op jit(solution)/shard_map/all_to_all | solution.py:58
  26.1 1.2 pack.1
  27.3 28.2 %all_to_all.20 = bf16[8,16,2176]{2,1,0:T(8,128)(2,1)S(1)} all-to-all(bf16[8,16,2176]{2,1,0:T(8,128)(2,1)S(1)} %get-tuple-element.22), channel_id=1, replica_groups=mesh['zhi'=4,'core'=2,'zlo'=2,'yhi'=4,'ylo'=2,'xhi'=2,'xlo'=2] {'xhi','y..., dimensions={0} | all-to-all | bytes 1114112 | tf_op jit(solution)/shard_map/all_to_all | solution.py:367
  55.6 0.4 broadcast_in_dim.23
  56.0 0.0 copy-start.1
  56.0 0.0 copy-start.2
  56.1 0.0 copy-start.3
  56.1 34.6 %all_to_all.21 = bf16[8,2,4,16,2176]{4,3,2,1,0:T(8,128)(2,1)S(1)} all-to-all(bf16[8,2,4,16,2176]{4,3,2,1,0:T(8,128)(2,1)S(1)} %broadcast_in_dim.23), channel_id=1, replica_groups={{0,1,4,5,32,33,36,37},{2,3,6,7,34,35,38,39},{8,9,12,13,40,41,44,45},{10..., dimensions={0} | all-to-all | bytes 8912896 | tf_op jit(solution)/shard_map/all_to_all | solution.py:58
  90.6 0.0 copy-start
  90.6 1.9 %collective-permute-start = (bf16[2,2,2,2,4,16,2176]{6,5,4,3,2,1,0:T(8,128)(2,1)S(1)}, bf16[2,2,2,2,4,16,2176]{6,5,4,3,2,1,0:T(8,128)(2,1)S(1)}, u32[]{:S(2)}, u32[]{:S(2)}) collective-permute-start(bf16[2,2,2,2,4,16,2176]{6,5,4,3,2,1,0:T(8,128)(2,1)S(1)} %bitcast.8), channel_id=1, source_target_pairs={{0,64},{64,0},{1,65},{65,1},{2,66},{66,2},{3,67},{67,3},{4,68},{68... | collective-permute-start | bytes 13369352 | tf_op jit(solution)/shard_map/ppermute | solution.py:373
  92.5 0.1 pad_add_fusion.first_ref
  92.6 7.4 %collective-permute-done.other_ref.other_hbm = bf16[2,2,2,2,4,16,2176]{6,5,4,3,2,1,0:T(8,128)(2,1)S(1)} collective-permute-done((bf16[2,2,2,2,4,16,2176]{6,5,4,3,2,1,0:T(8,128)(2,1)S(1)}, bf16[2,2,2,2,4,16,2176]{6,5,4,3,2,1,0:T(8,128)(2,1)S(1)}, u32[]{:S(2)}, u32[]{:S(2)}) %collective-permute-start) | collective-permute-done | bytes 4456480 | tf_op jit(solution)/shard_map/ppermute | solution.py:373
  100.0 0.0 copy-done.1
  100.0 0.0 copy-done.2
  100.0 0.0 copy-done.3
  100.0 0.0 copy-start.4
  100.1 8.7 %middle.1 = (bf16[1024,1024]{1,0:T(8,128)(2,1)}, f32[1024,1024]{1,0:T(8,128)}, f32[16,512]{1,0:T(8,128)S(1)}, f32[16,512]{1,0:T(8,128)}, f32[16,1024]{1,0:T(8,128)}, /*index=5*/f32[8,512]{1,0:T(8,128)}, f32[8,512]{1,0:T(8,128)}) custom-call(s32[5]{0:T(128)S(1)} %stack.25.at_ref, bf16[2,2,2,2,4,16,2176]{6,5,4,3,2,1,0:T(8,128)(2,1)S(1)} %bitcast.9, ...), custom_call_target="tpu_custom_call" | custom-call | flops 6442450944 | bytes 12582912 | tf_op jit(solution)/shard_map/middle/pallas_call | solution.py:271
  108.8 0.0 copy-done
  108.8 0.0 copy-done.4
  108.8 0.7 broadcast_in_dim.24
  109.6 3.5 %all-to-all-start.3 = ((f32[8,16,512]{2,1,0:T(8,128)}), f32[8,16,512]{2,1,0:T(8,128)S(1)}, u32[]{:S(2)}, u32[]{:S(2)}) async-start(f32[8,16,512]{2,1,0:T(8,128)} %broadcast_in_dim.24), calls=%async_computation.3 | async-start | bytes 524288 | tf_op jit(solution)/shard_map/all_to_all | solution.py:58
  113.1 0.0 copy-start.5
  113.1 14.4 %left_refresh.1 = f32[16,1024]{1,0:T(8,128)} custom-call(s32[2]{0:T(128)S(1)} %pad_add_fusion.first_ref, bf16[2,2,2,2,4,16,2176]{6,5,4,3,2,1,0:T(8,128)(2,1)} %bitcast.10, bf16[2,2,2,2,4,16,2176]{6,5,4,3,2,1,0:T(8,128)(2,1)} %copy-done.4, f32[1024,1024]{1,0:T(8,128)} %get-tuple-element.24.outer_hbm, bf16[1024,1024]{1,0:T(8,128)(2,1)} %get-tuple-element.25.basis_hbm), custom_call_target="tpu_custom_call" | custom-call | flops 10737418240 | bytes 8388608 | tf_op jit(solution)/shard_map/left_refresh/pallas_call | solution.py:142
  127.5 0.0 all-to-all-done.3
  127.5 0.0 copy-done.5
  127.5 0.6 multiply_subtract_fusion
  (9 shorter events, 0.1 us)
Async XLA Ops:
  2.1 24.0 %all-to-all-start = ((f32[8,16,512]{2,1,0:T(8,128)}), f32[8,16,512]{2,1,0:T(8,128)S(1)}, u32[]{:S(2)}, u32[]{:S(2)}) async-start(f32[8,16,512]{2,1,0:T(8,128)} %broadcast_in_dim.21), calls=%async_computation | async-start | bytes 524288 | tf_op jit(solution)/shard_map/all_to_all | solution.py:58
  56.0 44.0 %copy-start.1 = (f32[16,1024]{1,0:T(8,128)S(1)}, f32[16,1024]{1,0:T(8,128)}, u32[]{:S(2)}) copy-start(f32[16,1024]{1,0:T(8,128)} %left_gram_ref.1) | copy-start | bytes 196612
  56.0 44.0 %copy-start.2 = (f32[8,512]{1,0:T(8,128)S(1)}, f32[8,512]{1,0:T(8,128)}, u32[]{:S(2)}) copy-start(f32[8,512]{1,0:T(8,128)} %right_gram_ref.1) | copy-start | bytes 49156
  56.1 44.0 %copy-start.3 = (f32[16,512]{1,0:T(8,128)S(1)}, f32[16,512]{1,0:T(8,128)}, u32[]{:S(2)}) copy-start(f32[16,512]{1,0:T(8,128)} %second_ref.1) | copy-start | bytes 98308
  90.6 18.2 %copy-start = (bf16[8,2,4,16,2176]{4,3,2,1,0:T(8,128)(2,1)}, bf16[8,2,4,16,2176]{4,3,2,1,0:T(8,128)(2,1)S(1)}, u32[]{:S(2)}) copy-start(bf16[8,2,4,16,2176]{4,3,2,1,0:T(8,128)(2,1)S(1)} %all_to_all.21) | copy-start | bytes 13369348
  90.6 9.4 %collective-permute-start = (bf16[2,2,2,2,4,16,2176]{6,5,4,3,2,1,0:T(8,128)(2,1)S(1)}, bf16[2,2,2,2,4,16,2176]{6,5,4,3,2,1,0:T(8,128)(2,1)S(1)}, u32[]{:S(2)}, u32[]{:S(2)}) collective-permute-start(bf16[2,2,2,2,4,16,2176]{6,5,4,3,2,1,0:T(8,128)(2,1)S(1)} %bitcast.8), channel_id=1, source_target_pairs={{0,64},{64,0},{1,65},{65,1},{2,66},{66,2},{3,67},{67,3},{4,68},{68... | collective-permute-start | bytes 13369352 | tf_op jit(solution)/shard_map/ppermute | solution.py:373
  100.0 8.8 %copy-start.4 = (bf16[2,2,2,2,4,16,2176]{6,5,4,3,2,1,0:T(8,128)(2,1)}, bf16[2,2,2,2,4,16,2176]{6,5,4,3,2,1,0:T(8,128)(2,1)S(1)}, u32[]{:S(2)}) copy-start(bf16[2,2,2,2,4,16,2176]{6,5,4,3,2,1,0:T(8,128)(2,1)S(1)} %collective-permute-done.other_ref.other_hbm) | copy-start | bytes 13369348
  109.6 17.9 %all-to-all-start.3 = ((f32[8,16,512]{2,1,0:T(8,128)}), f32[8,16,512]{2,1,0:T(8,128)S(1)}, u32[]{:S(2)}, u32[]{:S(2)}) async-start(f32[8,16,512]{2,1,0:T(8,128)} %broadcast_in_dim.24), calls=%async_computation.3 | async-start | bytes 524288 | tf_op jit(solution)/shard_map/all_to_all | solution.py:58
  113.1 14.4 %copy-start.5 = (f32[16,512]{1,0:T(8,128)S(1)}, f32[16,512]{1,0:T(8,128)}, u32[]{:S(2)}) copy-start(f32[16,512]{1,0:T(8,128)} %param.9) | copy-start | bytes 98308

commit v10 on v8

--- a/solution.py
+++ b/solution.py
@@ -93,7 +93,7 @@
 
 def left_kernel(
     first_ref, mine_hbm, other_ref, outer_hbm, basis_hbm, out_ref,
-    mine_ref, basis_ref, gram, power, start, current, sems,
+    mine_ref, basis_ref, mine_whole, other_whole, power, start, current, sems,
 ):
     rows, deep, tile = mine_ref.shape[-2], basis_ref.shape[0], 256
     pairs = [(mine_hbm, mine_ref), (basis_hbm, basis_ref)]
@@ -103,29 +103,33 @@
     copies = [pltpu.make_async_copy(a, b, sems.at[i]) for i, (a, b) in enumerate(pairs)]
     for copy in copies:
         copy.start()
+
+    def assemble(ref, whole):
+        for r in range(BLOCKS):
+            zlo, far = r // NF, r % NF
+            for j in range(SENT):
+                c = (r + j) % BLOCKS
+                at = pl.ds(j * BLOCK, BLOCK)
+                pieces = []
+                for near in range(NY * NX):
+                    y, x = near // NX, near % NX
+                    pieces.append(ref[zlo, y, x % NXN, x // NXN, far, :, at])
+                block = jnp.concatenate(pieces, axis=0)
+                whole[r * BLOCK : (r + 1) * BLOCK, c * BLOCK : (c + 1) * BLOCK] = block
+                if 0 < j < BLOCKS // 2:
+                    whole[c * BLOCK : (c + 1) * BLOCK, r * BLOCK : (r + 1) * BLOCK] = block.T
+
+    assemble(other_ref, other_whole)
     copies[0].wait()
-    for r in range(BLOCKS):
-        zlo, far = r // NF, r % NF
-        for j in range(SENT):
-            c = (r + j) % BLOCKS
-            at = pl.ds(j * BLOCK, BLOCK)
-            pieces = []
-            for near in range(NY * NX):
-                y, x = near // NX, near % NX
-                place = (zlo, y, x % NXN, x // NXN, far, slice(None), at)
-                pieces.append(mine_ref[place].astype(f32) + other_ref[place].astype(f32))
-            block = GRAM_DECAY * jnp.concatenate(pieces, axis=0)
-            gram[r * BLOCK : (r + 1) * BLOCK, c * BLOCK : (c + 1) * BLOCK] = block
-            if 0 < j < BLOCKS // 2:
-                gram[c * BLOCK : (c + 1) * BLOCK, r * BLOCK : (r + 1) * BLOCK] = block.T
+    assemble(mine_ref, mine_whole)
     copies[1].wait()
     basis = basis_ref[...]
 
     def power_tile(t):
+        at = pl.ds(t * tile, tile)
+        p = GRAM_DECAY * (mm(other_whole[at, :], basis, 1, 0) + mm(mine_whole[at, :], basis, 1, 0))
         copies[2 + t].wait()
-        at = pl.ds(t * tile, tile)
-        high, low = split(gram[at, :] + power[at, :])
-        return mm(high, basis, 1, 0) + mm(low, basis, 1, 0)
+        return p + power[at, :]
 
     refresh(power_tile, deep // tile, tile, first_ref[0], rows, power, start, current, out_ref)
     result, half = out_ref[...], deep // 2
@@ -144,7 +148,8 @@
         out_specs=vmem,
         scratch_shapes=[pltpu.VMEM(v.shape, bf16) for v in (mine, basis)]
         + [
-            pltpu.VMEM((deep, deep), f32),
+            pltpu.VMEM((deep, deep), bf16),
+            pltpu.VMEM((deep, deep), bf16),
             pltpu.VMEM((deep, deep), f32),
             pltpu.VMEM((deep, deep), bf16),
             pltpu.VMEM((deep, deep), bf16),
@@ -211,9 +216,10 @@
     copies[0].start()
     basis, grad = basis_ref[...], grad_ref[...]
     tile = 256
+    high, low = split((1.0 - GRAM_DECAY) * mm(grad, basis, 0, 0))
     for t in range(deep // tile):
         to = pl.ds(t * tile, tile)
-        outer[to, :] = (1.0 - GRAM_DECAY) * mm(grad_ref[to, :], grad, 1, 1)
+        outer[to, :] = mm(grad_ref[to, :], high, 1, 0) + mm(grad_ref[to, :], low, 1, 0)
     copies[1].start()
     rbasis = right[...].astype(bf16)
 
@@ -238,7 +244,7 @@
     update_ref[...] = mm(mm(own_rows, pick, 1, 0).astype(bf16), returned, 1, 0)
 
     own_at = pl.ds(pl.multiple_of(row_first, rows), rows)
-    left_new_ref[...] = GRAM_DECAY * left_gram_ref[...] + outer[own_at, :]
+    left_new_ref[...] = GRAM_DECAY * left_gram_ref[...] + (1.0 - GRAM_DECAY) * mm(grad_ref[own_at, :], grad, 1, 1)
     q = lax.broadcasted_iota(jnp.int32, (width, BLOCK), 1)
     column = lax.broadcasted_iota(jnp.int32, (width, BLOCK), 0)
     own = jnp.where((column == right_pair + right_odd + q) & (q < right_rows), 1.0, 0.0).astype(bf16)
@@ -379,7 +385,7 @@
     basis, outer = (pltpu.with_memory_space_constraint(v, pltpu.HBM) for v in (basis, outer))
     left_result = left_call(at[3:], parted(late), parted(late_other), outer, basis, rows)
     updates, left_result = lax.optimization_barrier((updates, left_result))
-    weight_new = weight - STEP_SIZE * jnp.sum(updates, axis=0)
+    weight_new = weight - STEP_SIZE * sum(updates[i] for i in range(n_grp))
     return (weight_new, moment_new, second_new, left_new, left_result, right_new, right_result)
 
 

time: 128 us -> 129 us (level)
  Pallas kernels: 25.2 us -> 28.2 us
  waiting for transfers between devices: 11.6 us -> 9.15 us
    all_to_all x3, waiting for transfers between devices: 11.4 us -> 8.91 us  [gather(): return lax.all_to_all(copies, axes, 0, 0, axis_index_groups=groups)]
    pallas_call x1, Pallas kernels: 10.1 us -> 12.5 us  [mid_call(): pl.pallas_call(mid_kernel, out_shape=[pltpu.HBM(*v) for v in shapes[:2]]...]
  transfers between devices with their start and end apart: 5 -> 5, of which waited for: 3 -> 3; matrix products, arithmetic and copies ran while one was open for 6% -> 6% of each run, Pallas kernels for 19% -> 21%
where the time goes in v10:
time: 129 us; the launch traced here: 128 us
  blocking collectives  55.6 us (43%)
  Pallas kernels  28.2 us (22%)
  starting transfers between devices  23.8 us (18%)
  waiting for transfers between devices  9.15 us (7%)
  other arithmetic  5.32 us (4%)
  local copies, waits for them, and re-layouts  4.78 us (4%)
    all_to_all x1, blocking collectives, local(): payload = lax.all_to_all(copies, ('xhi', 'yhi'), 0, 0)  28.2 us
    all_to_all x1, blocking collectives, gather(): return lax.all_to_all(copies, axes, 0, 0, axis_index_groups=groups)  27.4 us
    all_to_all x3, starting transfers between devices, gather(): return lax.all_to_all(copies, axes, 0, 0, axis_index_groups=groups)  19.9 us
    pallas_call x1, Pallas kernels, left_call(): pl.pallas_call(left_kernel, out_shape=jax.ShapeDtypeStruct((rows, deep),...  14.5 us
    pallas_call x1, Pallas kernels, mid_call(): pl.pallas_call(mid_kernel, out_shape=[pltpu.HBM(*v) for v in shapes[:2]]...  12.5 us
    all_to_all x3, waiting for transfers between devices, gather(): return lax.all_to_all(copies, axes, 0, 0, axis_index_groups=groups)  8.91 us
    broadcast_in_dim x4, local copies, waits for them, and re-layouts, gather(): copies = jnp.broadcast_to(value[None], (size,) + value.shape)  3.79 us
  transfers between devices with their start and end apart: 5, of which 3 were waited for; matrix products, arithmetic and copies ran while one was open for 6% of the time, Pallas kernels for 21%

profile of v10, /device:TPU:1, one launch (start us, length us, event | category | flops | bytes accessed | tf_op | source)
XLA Modules:
  0.0 127.7 jit_solution(8207068823564196333)
XLA Ops:
  0.6 1.5 %broadcast_in_dim.11 = f32[8,16,512]{2,1,0:T(8,128)} broadcast(f32[16,512]{1,0:T(8,128)} %bitcast.17), dimensions={1,2} | broadcast | bytes 294912 | tf_op jit(solution)/shard_map/broadcast_in_dim | solution.py:57
  2.1 11.8 %all-to-all-start = ((f32[8,16,512]{2,1,0:T(8,128)}), f32[8,16,512]{2,1,0:T(8,128)S(1)}, u32[]{:S(2)}, u32[]{:S(2)}) async-start(f32[8,16,512]{2,1,0:T(8,128)} %broadcast_in_dim.11), calls=%async_computation | async-start | bytes 524288 | tf_op jit(solution)/shard_map/all_to_all | solution.py:58
  13.9 0.8 convert_element_type.24.left_rows_ref
  14.8 0.7 convert_element_type.25
  15.5 0.7 fusion.6
  16.2 0.7 fusion.7
  17.0 0.8 slice.51
  17.8 0.1 concatenate.18
  17.9 0.8 fusion.3.early_ref
  18.7 0.8 broadcast_multiply_fusion.kept_ref
  19.4 0.1 stack.25.at_ref
  19.5 6.6 %all-to-all-done.grads_ref = f32[8,16,512]{2,1,0:T(8,128)S(1)} async-done(((f32[8,16,512]{2,1,0:T(8,128)}), f32[8,16,512]{2,1,0:T(8,128)S(1)}, u32[]{:S(2)}, u32[]{:S(2)}) %all-to-all-start) | async-done | bytes 262176 | tf_op jit(solution)/shard_map/all_to_all | solution.py:58
  26.1 1.2 pack.1
  27.3 28.2 %all_to_all.25 = bf16[8,16,2176]{2,1,0:T(8,128)(2,1)S(1)} all-to-all(bf16[8,16,2176]{2,1,0:T(8,128)(2,1)S(1)} %get-tuple-element.24), channel_id=1, replica_groups=mesh['zhi'=4,'core'=2,'zlo'=2,'yhi'=4,'ylo'=2,'xhi'=2,'xlo'=2] {'xhi','y..., dimensions={0} | all-to-all | bytes 1114112 | tf_op jit(solution)/shard_map/all_to_all | solution.py:370
  55.6 0.4 broadcast_in_dim.12
  56.0 27.4 %all_to_all.26 = bf16[8,2,4,16,1536]{4,3,2,1,0:T(8,128)(2,1)S(1)} all-to-all(bf16[8,2,4,16,1536]{4,3,2,1,0:T(8,128)(2,1)S(1)} %broadcast_in_dim.12), channel_id=1, replica_groups={{0,1,4,5,32,33,36,37},{2,3,6,7,34,35,38,39},{8,9,12,13,40,41,44,45},{10..., dimensions={0} | all-to-all | bytes 6291456 | tf_op jit(solution)/shard_map/all_to_all | solution.py:58
  83.3 0.0 copy-start
  83.3 0.0 copy-start.1
  83.4 0.0 copy-start.2
  83.4 2.0 %collective-permute-start = (bf16[8,2,4,16,1536]{4,3,2,1,0:T(8,128)(2,1)S(1)}, bf16[8,2,4,16,1536]{4,3,2,1,0:T(8,128)(2,1)}, u32[]{:S(2)}, u32[]{:S(2)}) collective-permute-start(bf16[8,2,4,16,1536]{4,3,2,1,0:T(8,128)(2,1)S(1)} %all_to_all.26), channel_id=1, source_target_pairs={{0,64},{64,0},{1,65},{65,1},{2,66},{66,2},{3,67},{67,3},{4,68},{68... | collective-permute-start | bytes 9437192 | tf_op jit(solution)/shard_map/ppermute | solution.py:377
  85.4 1.2 broadcast_in_dim.13
  86.6 4.3 %all-to-all-start.3 = ((bf16[8,2,4,16,640]{4,3,2,1,0:T(8,128)(2,1)}), bf16[8,2,4,16,640]{4,3,2,1,0:T(8,128)(2,1)}, u32[]{:S(2)}, u32[]{:S(2)}) async-start(bf16[8,2,4,16,640]{4,3,2,1,0:T(8,128)(2,1)} %broadcast_in_dim.13), calls=%async_computation.3 | async-start | bytes 2621440 | tf_op jit(solution)/shard_map/all_to_all | solution.py:58
  90.9 0.2 collective-permute-done
  91.2 0.0 copy-done
  91.2 0.0 copy-done.1
  91.2 0.0 copy-done.2
  91.2 12.5 %middle.1 = (bf16[1024,1024]{1,0:T(8,128)(2,1)}, f32[1024,1024]{1,0:T(8,128)}, f32[16,512]{1,0:T(8,128)S(1)}, f32[16,512]{1,0:T(8,128)}, f32[16,1024]{1,0:T(8,128)}, /*index=5*/f32[8,512]{1,0:T(8,128)}, f32[8,512]{1,0:T(8,128)}) custom-call(s32[5]{0:T(128)S(1)} %stack.25.at_ref, bf16[2,2,2,2,4,16,1536]{6,5,4,3,2,1,0:T(8,128)(2,1)S(1)} %bitcast.13, ...), custom_call_target="tpu_custom_call" | custom-call | flops 6442450944 | bytes 12582912 | tf_op jit(solution)/shard_map/middle/pallas_call | solution.py:274
  103.7 2.3 %all-to-all-done.3 = bf16[8,2,4,16,640]{4,3,2,1,0:T(8,128)(2,1)} async-done(((bf16[8,2,4,16,640]{4,3,2,1,0:T(8,128)(2,1)}), bf16[8,2,4,16,640]{4,3,2,1,0:T(8,128)(2,1)}, u32[]{:S(2)}, u32[]{:S(2)}) %all-to-all-start.3) | async-done | bytes 1310752 | tf_op jit(solution)/shard_map/all_to_all | solution.py:58
  106.0 1.9 %collective-permute-start.1 = (bf16[8,2,4,16,640]{4,3,2,1,0:T(8,128)(2,1)}, bf16[8,2,4,16,640]{4,3,2,1,0:T(8,128)(2,1)S(1)}, u32[]{:S(2)}, u32[]{:S(2)}) collective-permute-start(bf16[8,2,4,16,640]{4,3,2,1,0:T(8,128)(2,1)} %all-to-all-done.3), channel_id=1, source_target_pairs={{0,64},{64,0},{1,65},{65,1},{2,66},{66,2},{3,67},{67,3},{4,68},{68... | collective-permute-start | bytes 3932168 | tf_op jit(solution)/shard_map/ppermute | solution.py:383
  107.9 0.1 pad_add_fusion.first_ref
  108.0 0.7 broadcast_in_dim.14
  108.7 3.8 %all-to-all-start.4 = ((f32[8,16,512]{2,1,0:T(8,128)}), f32[8,16,512]{2,1,0:T(8,128)S(1)}, u32[]{:S(2)}, u32[]{:S(2)}) async-start(f32[8,16,512]{2,1,0:T(8,128)} %broadcast_in_dim.14), calls=%async_computation.4 | async-start | bytes 524288 | tf_op jit(solution)/shard_map/all_to_all | solution.py:58
  112.5 0.0 collective-permute-done.1
  112.6 0.0 copy-start.3
  112.6 14.5 %left_refresh.1 = f32[16,1024]{1,0:T(8,128)} custom-call(s32[2]{0:T(128)S(1)} %pad_add_fusion.first_ref, bf16[2,2,2,2,4,16,640]{6,5,4,3,2,1,0:T(8,128)(2,1)} %bitcast.9.mine_hbm, bf16[2,2,2,2,4,16,640]{6,5,4,3,2,1,0:T(8,128)(2,1)S(1)} %bitcast.14, f32[1024,1024]{1,0:T(8,128)} %get-tuple-element.28.outer_hbm, bf16[1024,1024]{1,0:T(8,128)(2,1)} %get-tuple-element.29.basis_hbm), custom_call_target="tpu_custom_call" | custom-call | flops 10737418240 | bytes 8388608 | tf_op jit(solution)/shard_map/left_refresh/pallas_call | solution.py:144
  127.1 0.0 all-to-all-done.4
  127.1 0.0 copy-done.3
  127.1 0.6 bitcast_subtract_fusion
  (10 shorter events, 0.1 us)
Async XLA Ops:
  2.1 24.0 %all-to-all-start = ((f32[8,16,512]{2,1,0:T(8,128)}), f32[8,16,512]{2,1,0:T(8,128)S(1)}, u32[]{:S(2)}, u32[]{:S(2)}) async-start(f32[8,16,512]{2,1,0:T(8,128)} %broadcast_in_dim.11), calls=%async_computation | async-start | bytes 524288 | tf_op jit(solution)/shard_map/all_to_all | solution.py:58
  83.3 7.8 %copy-start = (f32[16,1024]{1,0:T(8,128)S(1)}, f32[16,1024]{1,0:T(8,128)}, u32[]{:S(2)}) copy-start(f32[16,1024]{1,0:T(8,128)} %left_gram_ref.1) | copy-start | bytes 196612
  83.3 7.8 %copy-start.1 = (f32[8,512]{1,0:T(8,128)S(1)}, f32[8,512]{1,0:T(8,128)}, u32[]{:S(2)}) copy-start(f32[8,512]{1,0:T(8,128)} %right_gram_ref.1) | copy-start | bytes 49156
  83.4 7.8 %copy-start.2 = (f32[16,512]{1,0:T(8,128)S(1)}, f32[16,512]{1,0:T(8,128)}, u32[]{:S(2)}) copy-start(f32[16,512]{1,0:T(8,128)} %second_ref.1) | copy-start | bytes 98308
  83.4 7.8 %collective-permute-start = (bf16[8,2,4,16,1536]{4,3,2,1,0:T(8,128)(2,1)S(1)}, bf16[8,2,4,16,1536]{4,3,2,1,0:T(8,128)(2,1)}, u32[]{:S(2)}, u32[]{:S(2)}) collective-permute-start(bf16[8,2,4,16,1536]{4,3,2,1,0:T(8,128)(2,1)S(1)} %all_to_all.26), channel_id=1, source_target_pairs={{0,64},{64,0},{1,65},{65,1},{2,66},{66,2},{3,67},{67,3},{4,68},{68... | collective-permute-start | bytes 9437192 | tf_op jit(solution)/shard_map/ppermute | solution.py:377
  86.6 19.4 %all-to-all-start.3 = ((bf16[8,2,4,16,640]{4,3,2,1,0:T(8,128)(2,1)}), bf16[8,2,4,16,640]{4,3,2,1,0:T(8,128)(2,1)}, u32[]{:S(2)}, u32[]{:S(2)}) async-start(bf16[8,2,4,16,640]{4,3,2,1,0:T(8,128)(2,1)} %broadcast_in_dim.13), calls=%async_computation.3 | async-start | bytes 2621440 | tf_op jit(solution)/shard_map/all_to_all | solution.py:58
  106.0 6.5 %collective-permute-start.1 = (bf16[8,2,4,16,640]{4,3,2,1,0:T(8,128)(2,1)}, bf16[8,2,4,16,640]{4,3,2,1,0:T(8,128)(2,1)S(1)}, u32[]{:S(2)}, u32[]{:S(2)}) collective-permute-start(bf16[8,2,4,16,640]{4,3,2,1,0:T(8,128)(2,1)} %all-to-all-done.3), channel_id=1, source_target_pairs={{0,64},{64,0},{1,65},{65,1},{2,66},{66,2},{3,67},{67,3},{4,68},{68... | collective-permute-start | bytes 3932168 | tf_op jit(solution)/shard_map/ppermute | solution.py:383
  108.7 18.3 %all-to-all-start.4 = ((f32[8,16,512]{2,1,0:T(8,128)}), f32[8,16,512]{2,1,0:T(8,128)S(1)}, u32[]{:S(2)}, u32[]{:S(2)}) async-start(f32[8,16,512]{2,1,0:T(8,128)} %broadcast_in_dim.14), calls=%async_computation.4 | async-start | bytes 524288 | tf_op jit(solution)/shard_map/all_to_all | solution.py:58
  112.6 14.5 %copy-start.3 = (f32[16,512]{1,0:T(8,128)S(1)}, f32[16,512]{1,0:T(8,128)}, u32[]{:S(2)}) copy-start(f32[16,512]{1,0:T(8,128)} %param.9) | copy-start | bytes 98308

commit v11 on v8

--- a/solution.py
+++ b/solution.py
@@ -96,16 +96,17 @@
     mine_ref, basis_ref, gram, power, start, current, sems,
 ):
     rows, deep, tile = mine_ref.shape[-2], basis_ref.shape[0], 256
-    pairs = [(mine_hbm, mine_ref), (basis_hbm, basis_ref)]
+    pairs = [(mine_hbm.at[z], mine_ref.at[z]) for z in range(NZ)] + [(basis_hbm, basis_ref)]
     for t in range(deep // tile):
         at = pl.ds(t * tile, tile)
         pairs.append((outer_hbm.at[at], power.at[at]))
     copies = [pltpu.make_async_copy(a, b, sems.at[i]) for i, (a, b) in enumerate(pairs)]
     for copy in copies:
         copy.start()
-    copies[0].wait()
     for r in range(BLOCKS):
         zlo, far = r // NF, r % NF
+        if far == 0:
+            copies[zlo].wait()
         for j in range(SENT):
             c = (r + j) % BLOCKS
             at = pl.ds(j * BLOCK, BLOCK)
@@ -118,11 +119,11 @@
             gram[r * BLOCK : (r + 1) * BLOCK, c * BLOCK : (c + 1) * BLOCK] = block
             if 0 < j < BLOCKS // 2:
                 gram[c * BLOCK : (c + 1) * BLOCK, r * BLOCK : (r + 1) * BLOCK] = block.T
-    copies[1].wait()
+    copies[NZ].wait()
     basis = basis_ref[...]
 
     def power_tile(t):
-        copies[2 + t].wait()
+        copies[NZ + 1 + t].wait()
         at = pl.ds(t * tile, tile)
         high, low = split(gram[at, :] + power[at, :])
         return mm(high, basis, 1, 0) + mm(low, basis, 1, 0)
@@ -148,7 +149,7 @@
             pltpu.VMEM((deep, deep), f32),
             pltpu.VMEM((deep, deep), bf16),
             pltpu.VMEM((deep, deep), bf16),
-            pltpu.SemaphoreType.DMA((2 + deep // 256,)),
+            pltpu.SemaphoreType.DMA((NZ + 1 + deep // 256,)),
         ],
         compiler_params=pltpu.CompilerParams(vmem_limit_bytes=28 << 20),
         cost_estimate=pl.CostEstimate(flops=10 * deep**3, transcendentals=deep, bytes_accessed=8 * deep**2),
@@ -379,7 +380,7 @@
     basis, outer = (pltpu.with_memory_space_constraint(v, pltpu.HBM) for v in (basis, outer))
     left_result = left_call(at[3:], parted(late), parted(late_other), outer, basis, rows)
     updates, left_result = lax.optimization_barrier((updates, left_result))
-    weight_new = weight - STEP_SIZE * jnp.sum(updates, axis=0)
+    weight_new = weight - STEP_SIZE * sum(updates[i] for i in range(n_grp))
     return (weight_new, moment_new, second_new, left_new, left_result, right_new, right_result)
 
 

time: 128 us -> 128 us (level)
  no operation moved by 1% of the time
where the time goes in v11:
time: 128 us; the launch traced here: 127 us
  blocking collectives  55.6 us (43%)
  Pallas kernels  25.2 us (20%)
  starting transfers between devices  23.8 us (19%)
  waiting for transfers between devices  11.6 us (9%)
  other arithmetic  5.32 us (4%)
  local copies, waits for them, and re-layouts  4.78 us (4%)
    all_to_all x1, blocking collectives, local(): payload = lax.all_to_all(copies, ('xhi', 'yhi'), 0, 0)  28.2 us
    all_to_all x1, blocking collectives, gather(): return lax.all_to_all(copies, axes, 0, 0, axis_index_groups=groups)  27.4 us
    all_to_all x3, starting transfers between devices, gather(): return lax.all_to_all(copies, axes, 0, 0, axis_index_groups=groups)  19.9 us
    pallas_call x1, Pallas kernels, left_call(): pl.pallas_call(left_kernel, out_shape=jax.ShapeDtypeStruct((rows, deep),...  13.9 us
    all_to_all x3, waiting for transfers between devices, gather(): return lax.all_to_all(copies, axes, 0, 0, axis_index_groups=groups)  11.4 us
    pallas_call x1, Pallas kernels, mid_call(): pl.pallas_call(mid_kernel, out_shape=[pltpu.HBM(*v) for v in shapes[:2]]...  10.1 us
    broadcast_in_dim x4, local copies, waits for them, and re-layouts, gather(): copies = jnp.broadcast_to(value[None], (size,) + value.shape)  3.79 us
  transfers between devices with their start and end apart: 5, of which 3 were waited for; matrix products, arithmetic and copies ran while one was open for 6% of the time, Pallas kernels for 19%

profile of v11, /device:TPU:1, one launch (start us, length us, event | category | flops | bytes accessed | tf_op | source)
XLA Modules:
  0.0 127.1 jit_solution(11203222567050122067)
XLA Ops:
  0.6 1.5 %broadcast_in_dim.11 = f32[8,16,512]{2,1,0:T(8,128)} broadcast(f32[16,512]{1,0:T(8,128)} %bitcast.17), dimensions={1,2} | broadcast | bytes 294912 | tf_op jit(solution)/shard_map/broadcast_in_dim | solution.py:57
  2.1 11.8 %all-to-all-start = ((f32[8,16,512]{2,1,0:T(8,128)}), f32[8,16,512]{2,1,0:T(8,128)S(1)}, u32[]{:S(2)}, u32[]{:S(2)}) async-start(f32[8,16,512]{2,1,0:T(8,128)} %broadcast_in_dim.11), calls=%async_computation | async-start | bytes 524288 | tf_op jit(solution)/shard_map/all_to_all | solution.py:58
  13.9 0.8 convert_element_type.24.left_rows_ref
  14.8 0.7 convert_element_type.25
  15.5 0.7 fusion.6
  16.2 0.7 fusion.7
  17.0 0.8 slice.51
  17.8 0.1 concatenate.18
  17.9 0.8 fusion.3.early_ref
  18.7 0.8 broadcast_multiply_fusion.kept_ref
  19.4 0.1 stack.25.at_ref
  19.5 6.6 %all-to-all-done.grads_ref = f32[8,16,512]{2,1,0:T(8,128)S(1)} async-done(((f32[8,16,512]{2,1,0:T(8,128)}), f32[8,16,512]{2,1,0:T(8,128)S(1)}, u32[]{:S(2)}, u32[]{:S(2)}) %all-to-all-start) | async-done | bytes 262176 | tf_op jit(solution)/shard_map/all_to_all | solution.py:58
  26.1 1.2 pack.1
  27.3 28.2 %all_to_all.25 = bf16[8,16,2176]{2,1,0:T(8,128)(2,1)S(1)} all-to-all(bf16[8,16,2176]{2,1,0:T(8,128)(2,1)S(1)} %get-tuple-element.24), channel_id=1, replica_groups=mesh['zhi'=4,'core'=2,'zlo'=2,'yhi'=4,'ylo'=2,'xhi'=2,'xlo'=2] {'xhi','y..., dimensions={0} | all-to-all | bytes 1114112 | tf_op jit(solution)/shard_map/all_to_all | solution.py:365
  55.6 0.4 broadcast_in_dim.12
  56.0 27.4 %all_to_all.26 = bf16[8,2,4,16,1536]{4,3,2,1,0:T(8,128)(2,1)S(1)} all-to-all(bf16[8,2,4,16,1536]{4,3,2,1,0:T(8,128)(2,1)S(1)} %broadcast_in_dim.12), channel_id=1, replica_groups={{0,1,4,5,32,33,36,37},{2,3,6,7,34,35,38,39},{8,9,12,13,40,41,44,45},{10..., dimensions={0} | all-to-all | bytes 6291456 | tf_op jit(solution)/shard_map/all_to_all | solution.py:58
  83.3 0.0 copy-start
  83.3 0.0 copy-start.1
  83.4 0.0 copy-start.2
  83.4 2.0 %collective-permute-start = (bf16[8,2,4,16,1536]{4,3,2,1,0:T(8,128)(2,1)S(1)}, bf16[8,2,4,16,1536]{4,3,2,1,0:T(8,128)(2,1)}, u32[]{:S(2)}, u32[]{:S(2)}) collective-permute-start(bf16[8,2,4,16,1536]{4,3,2,1,0:T(8,128)(2,1)S(1)} %all_to_all.26), channel_id=1, source_target_pairs={{0,64},{64,0},{1,65},{65,1},{2,66},{66,2},{3,67},{67,3},{4,68},{68... | collective-permute-start | bytes 9437192 | tf_op jit(solution)/shard_map/ppermute | solution.py:372
  85.4 1.2 broadcast_in_dim.13
  86.6 4.3 %all-to-all-start.3 = ((bf16[8,2,4,16,640]{4,3,2,1,0:T(8,128)(2,1)}), bf16[8,2,4,16,640]{4,3,2,1,0:T(8,128)(2,1)}, u32[]{:S(2)}, u32[]{:S(2)}) async-start(bf16[8,2,4,16,640]{4,3,2,1,0:T(8,128)(2,1)} %broadcast_in_dim.13), calls=%async_computation.3 | async-start | bytes 2621440 | tf_op jit(solution)/shard_map/all_to_all | solution.py:58
  90.9 0.2 collective-permute-done
  91.2 0.0 copy-done
  91.2 0.0 copy-done.1
  91.2 0.0 copy-done.2
  91.2 10.1 %middle.1 = (bf16[1024,1024]{1,0:T(8,128)(2,1)}, f32[1024,1024]{1,0:T(8,128)}, f32[16,512]{1,0:T(8,128)S(1)}, f32[16,512]{1,0:T(8,128)}, f32[16,1024]{1,0:T(8,128)}, /*index=5*/f32[8,512]{1,0:T(8,128)}, f32[8,512]{1,0:T(8,128)}) custom-call(s32[5]{0:T(128)S(1)} %stack.25.at_ref, bf16[2,2,2,2,4,16,1536]{6,5,4,3,2,1,0:T(8,128)(2,1)S(1)} %bitcast.13, ...), custom_call_target="tpu_custom_call" | custom-call | flops 6442450944 | bytes 12582912 | tf_op jit(solution)/shard_map/middle/pallas_call | solution.py:269
  101.2 4.8 %all-to-all-done.3 = bf16[8,2,4,16,640]{4,3,2,1,0:T(8,128)(2,1)} async-done(((bf16[8,2,4,16,640]{4,3,2,1,0:T(8,128)(2,1)}), bf16[8,2,4,16,640]{4,3,2,1,0:T(8,128)(2,1)}, u32[]{:S(2)}, u32[]{:S(2)}) %all-to-all-start.3) | async-done | bytes 1310752 | tf_op jit(solution)/shard_map/all_to_all | solution.py:58
  106.0 1.9 %collective-permute-start.1 = (bf16[8,2,4,16,640]{4,3,2,1,0:T(8,128)(2,1)}, bf16[8,2,4,16,640]{4,3,2,1,0:T(8,128)(2,1)S(1)}, u32[]{:S(2)}, u32[]{:S(2)}) collective-permute-start(bf16[8,2,4,16,640]{4,3,2,1,0:T(8,128)(2,1)} %all-to-all-done.3), channel_id=1, source_target_pairs={{0,64},{64,0},{1,65},{65,1},{2,66},{66,2},{3,67},{67,3},{4,68},{68... | collective-permute-start | bytes 3932168 | tf_op jit(solution)/shard_map/ppermute | solution.py:378
  107.9 0.1 pad_add_fusion.first_ref
  108.0 0.7 broadcast_in_dim.14
  108.7 3.8 %all-to-all-start.4 = ((f32[8,16,512]{2,1,0:T(8,128)}), f32[8,16,512]{2,1,0:T(8,128)S(1)}, u32[]{:S(2)}, u32[]{:S(2)}) async-start(f32[8,16,512]{2,1,0:T(8,128)} %broadcast_in_dim.14), calls=%async_computation.4 | async-start | bytes 524288 | tf_op jit(solution)/shard_map/all_to_all | solution.py:58
  112.5 0.0 collective-permute-done.1
  112.6 0.0 copy-start.3
  112.6 13.9 %left_refresh.1 = f32[16,1024]{1,0:T(8,128)} custom-call(s32[2]{0:T(128)S(1)} %pad_add_fusion.first_ref, bf16[2,2,2,2,4,16,640]{6,5,4,3,2,1,0:T(8,128)(2,1)} %bitcast.9.mine_hbm, bf16[2,2,2,2,4,16,640]{6,5,4,3,2,1,0:T(8,128)(2,1)S(1)} %bitcast.14, f32[1024,1024]{1,0:T(8,128)} %get-tuple-element.28.outer_hbm, bf16[1024,1024]{1,0:T(8,128)(2,1)} %get-tuple-element.29.basis_hbm), custom_call_target="tpu_custom_call" | custom-call | flops 10737418240 | bytes 8388608 | tf_op jit(solution)/shard_map/left_refresh/pallas_call | solution.py:141
  126.5 0.0 all-to-all-done.4
  126.5 0.0 copy-done.3
  126.5 0.6 bitcast_subtract_fusion
  (10 shorter events, 0.1 us)
Async XLA Ops:
  2.1 24.0 %all-to-all-start = ((f32[8,16,512]{2,1,0:T(8,128)}), f32[8,16,512]{2,1,0:T(8,128)S(1)}, u32[]{:S(2)}, u32[]{:S(2)}) async-start(f32[8,16,512]{2,1,0:T(8,128)} %broadcast_in_dim.11), calls=%async_computation | async-start | bytes 524288 | tf_op jit(solution)/shard_map/all_to_all | solution.py:58
  83.3 7.8 %copy-start = (f32[16,1024]{1,0:T(8,128)S(1)}, f32[16,1024]{1,0:T(8,128)}, u32[]{:S(2)}) copy-start(f32[16,1024]{1,0:T(8,128)} %left_gram_ref.1) | copy-start | bytes 196612
  83.3 7.8 %copy-start.1 = (f32[8,512]{1,0:T(8,128)S(1)}, f32[8,512]{1,0:T(8,128)}, u32[]{:S(2)}) copy-start(f32[8,512]{1,0:T(8,128)} %right_gram_ref.1) | copy-start | bytes 49156
  83.4 7.8 %copy-start.2 = (f32[16,512]{1,0:T(8,128)S(1)}, f32[16,512]{1,0:T(8,128)}, u32[]{:S(2)}) copy-start(f32[16,512]{1,0:T(8,128)} %second_ref.1) | copy-start | bytes 98308
  83.4 7.8 %collective-permute-start = (bf16[8,2,4,16,1536]{4,3,2,1,0:T(8,128)(2,1)S(1)}, bf16[8,2,4,16,1536]{4,3,2,1,0:T(8,128)(2,1)}, u32[]{:S(2)}, u32[]{:S(2)}) collective-permute-start(bf16[8,2,4,16,1536]{4,3,2,1,0:T(8,128)(2,1)S(1)} %all_to_all.26), channel_id=1, source_target_pairs={{0,64},{64,0},{1,65},{65,1},{2,66},{66,2},{3,67},{67,3},{4,68},{68... | collective-permute-start | bytes 9437192 | tf_op jit(solution)/shard_map/ppermute | solution.py:372
  86.6 19.4 %all-to-all-start.3 = ((bf16[8,2,4,16,640]{4,3,2,1,0:T(8,128)(2,1)}), bf16[8,2,4,16,640]{4,3,2,1,0:T(8,128)(2,1)}, u32[]{:S(2)}, u32[]{:S(2)}) async-start(bf16[8,2,4,16,640]{4,3,2,1,0:T(8,128)(2,1)} %broadcast_in_dim.13), calls=%async_computation.3 | async-start | bytes 2621440 | tf_op jit(solution)/shard_map/all_to_all | solution.py:58
  106.0 6.5 %collective-permute-start.1 = (bf16[8,2,4,16,640]{4,3,2,1,0:T(8,128)(2,1)}, bf16[8,2,4,16,640]{4,3,2,1,0:T(8,128)(2,1)S(1)}, u32[]{:S(2)}, u32[]{:S(2)}) collective-permute-start(bf16[8,2,4,16,640]{4,3,2,1,0:T(8,128)(2,1)} %all-to-all-done.3), channel_id=1, source_target_pairs={{0,64},{64,0},{1,65},{65,1},{2,66},{66,2},{3,67},{67,3},{4,68},{68... | collective-permute-start | bytes 3932168 | tf_op jit(solution)/shard_map/ppermute | solution.py:378
  108.7 17.7 %all-to-all-start.4 = ((f32[8,16,512]{2,1,0:T(8,128)}), f32[8,16,512]{2,1,0:T(8,128)S(1)}, u32[]{:S(2)}, u32[]{:S(2)}) async-start(f32[8,16,512]{2,1,0:T(8,128)} %broadcast_in_dim.14), calls=%async_computation.4 | async-start | bytes 524288 | tf_op jit(solution)/shard_map/all_to_all | solution.py:58
  112.6 13.9 %copy-start.3 = (f32[16,512]{1,0:T(8,128)S(1)}, f32[16,512]{1,0:T(8,128)}, u32[]{:S(2)}) copy-start(f32[16,512]{1,0:T(8,128)} %param.9) | copy-start | bytes 98308
